TPU v7x, 32 devices: a whole 2x2x4 slice. The times are simulated.
32 devices in a mesh: head: 4 (over y, core), blk: 8 (over z, x).
Axes of the slice: x: 2, y: 2, z: 4, core: 2. Of those that a mesh axis runs over, the one named last changes fastest.
Arguments:
- tokens: bfloat16 [4096, 2048], P(('head', 'blk')), may hold values from -50 to 50
- out_grad: bfloat16 [4096, 2048], P(('head', 'blk')), may hold values from -6 to 6
- seq_lengths: int32 [8], replicated, may hold values from 1 to 2048, 4096 in all
- block_deal: int32 [16], replicated, may hold values from 0 to 15, as said below
- norm_gain: bfloat16 [2048], P('blk'), may hold values from 0.5 to 1.5
- q_weight: bfloat16 [2048, 2048], P('blk', 'head'), may hold values from -0.125 to 0.125
- key_projection_weight: bfloat16 [2048, 1024], P('blk', 'head'), may hold values from -0.125 to 0.125
- value_projection_weight: bfloat16 [2048, 1024], P('blk', 'head'), may hold values from -0.125 to 0.125
- q_gain: bfloat16 [128], P('blk'), may hold values from 0.5 to 1.5
- k_gain: bfloat16 [128], P('blk'), may hold values from 0.5 to 1.5
- o_weight: bfloat16 [2048, 2048], P('head', 'blk'), may hold values from -0.75 to 0.75
- mlp_gain: bfloat16 [2048], P('blk'), may hold values from 0.5 to 1.5
- gate_weight: bfloat16 [2048, 6144], P('blk', 'head'), may hold values from -0.125 to 0.125
- up_weight: bfloat16 [2048, 6144], P('blk', 'head'), may hold values from -0.125 to 0.125
- down_weight: bfloat16 [6144, 2048], P('head', 'blk'), may hold values from -0.078125 to 0.078125
Outputs:
- block_out: bfloat16 [4096, 2048], P(('head', 'blk'))
- in_grad: float32 [4096, 2048], P(('head', 'blk'))
- norm_gain_grad: float32 [2048], P(('head', 'blk'))
- q_weight_grad: float32 [2048, 2048], P('blk', 'head')
- k_weight_grad: float32 [2048, 1024], P('blk', 'head')
- v_weight_grad: float32 [2048, 1024], P('blk', 'head')
- q_gain_grad: float32 [128], P(('head', 'blk'))
- k_gain_grad: float32 [128], P(('head', 'blk'))
- o_weight_grad: float32 [2048, 2048], P('head', 'blk')
- mlp_gain_grad: float32 [2048], P(('head', 'blk'))
- gate_weight_grad: float32 [2048, 6144], P('blk', 'head')
- up_weight_grad: float32 [2048, 6144], P('blk', 'head')
- down_weight_grad: float32 [6144, 2048], P('head', 'blk')
Inputs may be any that keep to these rules, and one draw needn't show every extreme that they name: `seq_lengths`: the lengths sum to 4096; the longest has exactly 2048 tokens. `block_deal`: a permutation of 0 to 15 in which entries 2 b and 2 b + 1 sum to 15.
All inputs are finite; a program needn't handle non-finite values.
Results may differ from a plain program's by a relative error of at most 0.035.
Values may be sent and summed in bfloat16 or wider, within the bound.
No kernel may reach another device: no remote copies, remote signals or barrier semaphores. Data moves between devices by JAX's collectives and lax.ppermute only.
A program may use at most 320 MiB of HBM per device.

v0:
```python
import functools
import math

import jax
import jax.numpy as jnp
from jax import lax
from jax.experimental import pallas as pl
from jax.experimental.pallas import tpu as pltpu
from jax.sharding import Mesh
from jax.sharding import PartitionSpec as P

HEAD_SIZE = 128
KEY_VALUE_HEADS = 8
EPSILON = 1e-06
ROPE_BASE = 1000000.0
F32 = jnp.float32
BF16 = jnp.bfloat16
SWAP = [(0, 1), (1, 0)]
PAIRS_OF_ROWS = (((0,), (0,)), ((), ()))
PAIRS_OF_COLS = (((1,), (1,)), ((), ()))
VMEM = pltpu.MemorySpace.VMEM
LIGHT = pl.CostEstimate(flops=1000, bytes_accessed=1000, transcendentals=0)
SMEM = pltpu.MemorySpace.SMEM


def matmul(left, right):
    return jnp.dot(left, right, preferred_element_type=F32)


def contract_rows(left, right):
    return lax.dot_general(left, right, PAIRS_OF_ROWS, preferred_element_type=F32)


def contract_cols(left, right):
    return lax.dot_general(left, right, PAIRS_OF_COLS, preferred_element_type=F32)


def swap(value, axis):
    return lax.ppermute(value, axis, SWAP)


def attend_kernel(off_ref, tile_ref, low_ref, q_ref, start_ref, *refs, parts, first, last):
    half = 128
    kv_refs, refs = refs[:parts], refs[parts:]
    if not first:
        before_ref, refs = refs[0], refs[1:]
    if last:
        out_ref, inv_ref, kv_ref, acc_ref = refs
    else:
        after_ref, kv_ref, acc_ref = refs
    share = kv_refs[0].shape[0]
    for part, ref in enumerate(kv_refs):
        kv_ref[part * share : (part + 1) * share, :] = ref[...]
    lane = lax.broadcasted_iota(jnp.int32, (256, 256), 1)
    row = lax.broadcasted_iota(jnp.int32, (256, 256), 0) % half
    ones = jnp.ones((256, HEAD_SIZE), BF16)

    def tile(index, unused):
        rows = pl.ds(pl.multiple_of(index * half, half), half)
        queries = jnp.concatenate([q_ref[rows, :HEAD_SIZE], q_ref[rows, HEAD_SIZE:]], axis=0)
        start = start_ref[rows, :]
        start = jnp.concatenate([start, start], axis=1)
        start = jnp.concatenate([start, start], axis=0)
        places = tile_ref[index] * half + row
        acc_ref[...] = jnp.zeros_like(acc_ref) if first else before_ref[index]

        def step(block, unused_step):
            at = off_ref[2 * block]

            @pl.when(at >= 0)
            def _():
                low = pl.ds(pl.multiple_of(at, half), half)
                high = pl.ds(pl.multiple_of(off_ref[2 * block + 1], half), half)
                keys = jnp.concatenate([kv_ref[low, :HEAD_SIZE], kv_ref[high, :HEAD_SIZE]], axis=0)
                values = jnp.concatenate([kv_ref[low, HEAD_SIZE:], kv_ref[high, HEAD_SIZE:]], axis=0)
                scores = contract_cols(queries, keys)
                natural = block * 256 + lane
                allowed = (natural <= places) & (natural >= start)
                weights = jnp.where(allowed, jnp.exp(scores), 0.0).astype(BF16)
                acc_ref[...] += matmul(weights, jnp.concatenate([values, ones], axis=1))

            return unused_step

        lax.fori_loop(low_ref[index], tile_ref[index] // 2 + 1, step, 0)
        if last:
            inverse = 1.0 / acc_ref[:, HEAD_SIZE:]
            attended = (acc_ref[:, :HEAD_SIZE] * inverse).astype(BF16)
            out_ref[rows, :HEAD_SIZE] = attended[:half]
            out_ref[rows, HEAD_SIZE:] = attended[half:]
            inv_ref[index, 0:1, :] = jnp.transpose(inverse[:half])[0:1, :]
            inv_ref[index, 1:2, :] = jnp.transpose(inverse[half:])[0:1, :]
        else:
            after_ref[index] = acc_ref[...]
        return unused

    lax.fori_loop(0, q_ref.shape[0] // half, tile, 0)


def attend_back_kernel(
    off_ref, tile_ref, low_ref, q_ref, start_ref, inv_ref, out_ref, grad_ref, *refs, parts, first, last
):
    half = 128
    kv_refs, refs = refs[:parts], refs[parts:]
    if not first:
        before_ref, refs = refs[0], refs[1:]
    dq_ref, *dkv_refs = refs[: 1 + parts]
    kv_ref, dk_ref, dv_ref, acc_ref = refs[1 + parts :]
    share = kv_refs[0].shape[0]
    for part, ref in enumerate(kv_refs):
        kv_ref[part * share : (part + 1) * share, :] = ref[...]
    key_row = lax.broadcasted_iota(jnp.int32, (256, 256), 0)
    query_lane = lax.broadcasted_iota(jnp.int32, (1, 256), 1) % half

    def clear(index, unused):
        rows = pl.ds(pl.multiple_of(index * 256, 256), 256)
        dk_ref[rows, :] = jnp.zeros((256, HEAD_SIZE), F32)
        dv_ref[rows, :] = jnp.zeros((256, HEAD_SIZE), F32)
        return unused

    lax.fori_loop(0, dk_ref.shape[0] // 256, clear, 0)

    def tile(index, unused):
        rows = pl.ds(pl.multiple_of(index * half, half), half)

        def both(ref):
            return jnp.concatenate([ref[rows, :HEAD_SIZE], ref[rows, HEAD_SIZE:]], axis=0)

        def along(ref):
            return jnp.concatenate([ref[index, 0:1, :], ref[index, 1:2, :]], axis=1)

        queries = both(q_ref)
        grads = both(grad_ref)
        products = both(out_ref).astype(F32) * grads.astype(F32)
        deltas = jnp.sum(jnp.transpose(products), axis=0, keepdims=True)
        inverse = along(inv_ref)
        start = along(start_ref)
        places = tile_ref[index] * half + query_lane
        acc_ref[...] = jnp.zeros_like(acc_ref) if first else both(before_ref)

        def step(block, unused_step):
            at = off_ref[2 * block]

            @pl.when(at >= 0)
            def _():
                low = pl.ds(pl.multiple_of(at, half), half)
                high = pl.ds(pl.multiple_of(off_ref[2 * block + 1], half), half)
                keys = jnp.concatenate([kv_ref[low, :HEAD_SIZE], kv_ref[high, :HEAD_SIZE]], axis=0)
                values = jnp.concatenate([kv_ref[low, HEAD_SIZE:], kv_ref[high, HEAD_SIZE:]], axis=0)
                scores = contract_cols(keys, queries)
                natural = block * 256 + key_row
                allowed = (natural <= places) & (natural >= start)
                probs = jnp.where(allowed, jnp.exp(scores) * inverse, 0.0)
                prob_grad = contract_cols(values, grads)
                score_grad = (probs * (prob_grad - deltas)).astype(BF16)
                value_part = matmul(probs.astype(BF16), grads)
                key_part = matmul(score_grad, queries)
                dv_ref[low, :] += value_part[:half]
                dv_ref[high, :] += value_part[half:]
                dk_ref[low, :] += key_part[:half]
                dk_ref[high, :] += key_part[half:]
                acc_ref[...] += contract_rows(score_grad, keys)

            return unused_step

        lax.fori_loop(low_ref[index], tile_ref[index] // 2 + 1, step, 0)
        dq_ref[rows, :HEAD_SIZE] = acc_ref[:half, :].astype(dq_ref.dtype)
        dq_ref[rows, HEAD_SIZE:] = acc_ref[half:, :].astype(dq_ref.dtype)
        return unused

    lax.fori_loop(0, q_ref.shape[0] // half, tile, 0)

    for part, ref in enumerate(dkv_refs):

        def store(index, unused):
            target = pl.ds(pl.multiple_of(index * 256, 256), 256)
            source = pl.ds(pl.multiple_of(part * share + index * 256, 256), 256)
            ref[target, :HEAD_SIZE] = dk_ref[source, :].astype(BF16)
            ref[target, HEAD_SIZE:] = dv_ref[source, :].astype(BF16)
            return unused

        lax.fori_loop(0, share // 256, store, 0)


def attend(offsets, tiles, queries, start_cols, kv_parts, before=None, last=True):
    rows, width = queries.shape
    parts, share = len(kv_parts), kv_parts[0].shape[0]
    keys = parts * share
    first = before is None
    extra = () if first else (before,)
    whole = (
        (jax.ShapeDtypeStruct((rows, width), BF16), jax.ShapeDtypeStruct((rows // 128, 2, 128), F32))
        if last
        else (jax.ShapeDtypeStruct((rows // 128, 256, 256), F32),)
    )
    return pl.pallas_call(
        functools.partial(attend_kernel, parts=parts, first=first, last=last),
        name="attend",
        out_shape=whole,
        in_specs=[pl.BlockSpec(memory_space=SMEM)] * 3 + [pl.BlockSpec(memory_space=VMEM)] * (2 + parts + len(extra)),
        out_specs=[pl.BlockSpec(memory_space=VMEM)] * len(whole),
        scratch_shapes=[pltpu.VMEM((keys, width), BF16), pltpu.VMEM((256, 256), F32)],
        compiler_params=pltpu.CompilerParams(vmem_limit_bytes=12 * 2**20 + keys * 1536),
        cost_estimate=LIGHT,
    )(offsets, *tiles, queries, start_cols, *kv_parts, *extra)


def attend_back(offsets, tiles, queries, start_rows, inverse, attended, grads, kv_parts, before=None, last=True):
    rows, width = queries.shape
    parts, share = len(kv_parts), kv_parts[0].shape[0]
    keys = parts * share
    first = before is None
    extra = () if first else (before,)
    return pl.pallas_call(
        functools.partial(attend_back_kernel, parts=parts, first=first, last=last),
        name="attend_back",
        out_shape=(jax.ShapeDtypeStruct((rows, width), BF16 if last else F32),)
        + tuple(jax.ShapeDtypeStruct((share, width), BF16) for unused in kv_parts),
        in_specs=[pl.BlockSpec(memory_space=SMEM)] * 3 + [pl.BlockSpec(memory_space=VMEM)] * (5 + parts + len(extra)),
        out_specs=[pl.BlockSpec(memory_space=VMEM)] * (1 + parts),
        scratch_shapes=[
            pltpu.VMEM((keys, width), BF16),
            pltpu.VMEM((keys, HEAD_SIZE), F32),
            pltpu.VMEM((keys, HEAD_SIZE), F32),
            pltpu.VMEM((256, HEAD_SIZE), F32),
        ],
        compiler_params=pltpu.CompilerParams(vmem_limit_bytes=12 * 2**20 + keys * 2816),
        cost_estimate=LIGHT,
    )(offsets, *tiles, queries, start_rows, inverse, attended, grads, *kv_parts, *extra)


def shape_kernel(raw_ref, cos_ref, sin_ref, gain_ref, q_ref, kv_ref):
    cosine = cos_ref[...]
    sine = sin_ref[...]

    def shaped(first, gain):
        value = raw_ref[:, first : first + HEAD_SIZE]
        mean_square = jnp.mean(value * value, axis=-1, keepdims=True)
        value = value * lax.rsqrt(mean_square + EPSILON) * gain
        return value * cosine + pltpu.roll(value, HEAD_SIZE // 2, 1) * sine

    for head in range(2):
        columns = slice(head * HEAD_SIZE, (head + 1) * HEAD_SIZE)
        q_ref[:, columns] = (shaped(head * HEAD_SIZE, gain_ref[0:1, :]) * HEAD_SIZE**-0.5).astype(BF16)
    kv_ref[:, :HEAD_SIZE] = shaped(2 * HEAD_SIZE, gain_ref[1:2, :]).astype(BF16)
    kv_ref[:, HEAD_SIZE:] = raw_ref[:, 3 * HEAD_SIZE :].astype(BF16)


def shape_back_kernel(raw_ref, grad_ref, cos_ref, sin_ref, gain_ref, low_ref, gain_grad_ref, *, heads, gain_row, factor):
    @pl.when(pl.program_id(0) == 0)
    def _():
        gain_grad_ref[...] = jnp.zeros_like(gain_grad_ref)

    cosine = cos_ref[...]
    sine = sin_ref[...]
    gain = gain_ref[gain_row : gain_row + 1, :]
    total = jnp.zeros((8, HEAD_SIZE), F32)
    for head in range(heads):
        columns = slice(head * HEAD_SIZE, (head + 1) * HEAD_SIZE)
        value = raw_ref[:, columns]
        grad = grad_ref[:, columns].astype(F32) * factor
        grad = grad * cosine - pltpu.roll(grad, HEAD_SIZE // 2, 1) * sine
        rho = lax.rsqrt(jnp.mean(value * value, axis=-1, keepdims=True) + EPSILON)
        unit = value * rho
        total = total + jnp.sum((grad * unit).reshape(-1, 8, HEAD_SIZE), axis=0)
        scaled = grad * gain
        inner = jnp.mean(scaled * unit, axis=-1, keepdims=True)
        low_ref[:, columns] = (rho * (scaled - unit * inner)).astype(BF16)
    if heads == 1:
        low_ref[:, HEAD_SIZE:] = grad_ref[:, HEAD_SIZE:].astype(BF16)
    gain_grad_ref[...] += total


ROW_TILE = 256


def shape_heads(raw, cosine, sine, gains):
    rows = raw.shape[0]
    block = lambda width: pl.BlockSpec((ROW_TILE, width), lambda i: (i, 0))
    return pl.pallas_call(
        shape_kernel,
        name="shape_heads",
        grid=(rows // ROW_TILE,),
        out_shape=(jax.ShapeDtypeStruct((rows, 256), BF16), jax.ShapeDtypeStruct((rows, 256), BF16)),
        in_specs=[block(512), block(128), block(128), pl.BlockSpec((2, 128), lambda i: (0, 0))],
        out_specs=[block(256), block(256)],
        compiler_params=pltpu.CompilerParams(vmem_limit_bytes=8 * 2**20),
        cost_estimate=LIGHT,
    )(raw, cosine, sine, gains)


def shape_back(raw, grads, cosine, sine, gains, heads, column, gain_row, factor):
    rows = raw.shape[0]
    block = lambda width, at=0: pl.BlockSpec((ROW_TILE, width), lambda i: (i, at))
    return pl.pallas_call(
        functools.partial(shape_back_kernel, heads=heads, gain_row=gain_row, factor=factor),
        name="shape_back",
        grid=(rows // ROW_TILE,),
        out_shape=(jax.ShapeDtypeStruct((rows, 256), BF16), jax.ShapeDtypeStruct((8, 128), F32)),
        in_specs=[
            block(heads * 128, column),
            block(256),
            block(128),
            block(128),
            pl.BlockSpec((2, 128), lambda i: (0, 0)),
        ],
        out_specs=[block(256), pl.BlockSpec((8, 128), lambda i: (0, 0))],
        compiler_params=pltpu.CompilerParams(vmem_limit_bytes=8 * 2**20),
        cost_estimate=LIGHT,
    )(raw, grads, cosine, sine, gains)


def reorder_kernel(order_ref, *refs):
    half = len(refs) // 2
    for source, target in zip(refs[:half], refs[half:]):
        target[...] = source[...].astype(target.dtype)


def reorder(order, values, types):
    rows, width = values[0].shape
    blocks = order.shape[0]
    size = width // blocks
    taken = pl.BlockSpec((rows, size), lambda i, order_ref: (0, order_ref[i]))
    put = pl.BlockSpec((rows, size), lambda i, order_ref: (0, i))
    return pl.pallas_call(
        reorder_kernel,
        name="reorder",
        grid_spec=pltpu.PrefetchScalarGridSpec(
            num_scalar_prefetch=1,
            grid=(blocks,),
            in_specs=[taken] * len(values),
            out_specs=[put] * len(values),
        ),
        out_shape=[jax.ShapeDtypeStruct(value.shape, kind) for value, kind in zip(values, types)],
        compiler_params=pltpu.CompilerParams(vmem_limit_bytes=8 * 2**20),
        cost_estimate=LIGHT,
    )(order, *values)


def assemble_kernel(at_ref, *refs, entries, axis):
    out_ref = refs[-1]
    for source, (place, kind) in zip(refs[:-1], entries):
        size = source.shape[axis]
        if kind == 0:
            span = slice(place, place + size)
        else:
            at = at_ref[0] if kind > 0 else 1 - at_ref[0]
            span = pl.ds(pl.multiple_of(place + at * 256, 16 if axis == 0 else 128), size)
        if axis == 0:
            out_ref[span, :] = source[...]
        else:
            out_ref[:, span] = source[...]


def assemble(at, parts, axis):
    values = [value for value, unused, kind in parts]
    total = sum(value.shape[axis] for value in values)
    other = values[0].shape[1 - axis]
    shape = (total, other) if axis == 0 else (other, total)
    return pl.pallas_call(
        functools.partial(assemble_kernel, entries=tuple((place, kind) for unused, place, kind in parts), axis=axis),
        name="assemble",
        out_shape=jax.ShapeDtypeStruct(shape, BF16),
        in_specs=[pl.BlockSpec(memory_space=SMEM)] + [pl.BlockSpec(memory_space=VMEM)] * len(values),
        out_specs=pl.BlockSpec(memory_space=VMEM),
        compiler_params=pltpu.CompilerParams(vmem_limit_bytes=12 * 2**20),
        cost_estimate=LIGHT,
    )(at, *values)


def terms_kernel(left_ref, right_ref, left_cols_ref, right_cols_ref, kept_ref, given_ref):
    total = contract_cols(left_ref[...], left_cols_ref[...]) + contract_cols(right_ref[...], right_cols_ref[...])
    middle = kept_ref.shape[0]
    kept_ref[...] = total[:middle]
    given_ref[...] = total[middle:].astype(BF16)


def two_terms(left, right, left_cols, right_cols):
    rows, depth = left.shape
    width = left_cols.shape[0]
    tile = 512
    value = pl.BlockSpec((rows, depth), lambda i: (0, 0))
    cols = pl.BlockSpec((tile, depth), lambda i: (i, 0))
    half = pl.BlockSpec((rows // 2, tile), lambda i: (0, i))
    return pl.pallas_call(
        terms_kernel,
        name="two_terms",
        grid=(width // tile,),
        out_shape=(jax.ShapeDtypeStruct((rows // 2, width), F32), jax.ShapeDtypeStruct((rows // 2, width), BF16)),
        in_specs=[value, value, cols, cols],
        out_specs=(half, half),
        cost_estimate=LIGHT,
    )(left, right, left_cols, right_cols)


def hidden_kernel(mine_ref, theirs_ref, gate_ref, up_ref, hidden_ref, gate_slope_ref, up_slope_ref):
    middle = mine_ref.shape[0]
    for part, source in ((slice(0, middle), mine_ref), (slice(middle, 2 * middle), theirs_ref)):
        rows = source[...]
        gate = matmul(rows, gate_ref[...])
        up = matmul(rows, up_ref[...])
        sig = 1.0 / (1.0 + jnp.exp(-gate))
        silu = gate * sig
        hidden_ref[part, :] = (silu * up).astype(BF16)
        gate_slope_ref[part, :] = (up * (sig * (1.0 + gate * (1.0 - sig)))).astype(BF16)
        up_slope_ref[part, :] = silu.astype(BF16)


def hidden_units(mine, theirs, gate_cols, up_cols):
    middle, width = mine.shape
    units = gate_cols.shape[1]
    tile = 256
    whole = pl.BlockSpec((middle, width), lambda i: (0, 0))
    cols = pl.BlockSpec((width, tile), lambda i: (0, i))
    out = pl.BlockSpec((2 * middle, tile), lambda i: (0, i))
    return pl.pallas_call(
        hidden_kernel,
        name="hidden_units",
        grid=(units // tile,),
        out_shape=(jax.ShapeDtypeStruct((2 * middle, units), BF16),) * 3,
        in_specs=[whole, whole, cols, cols],
        out_specs=(out,) * 3,
        cost_estimate=LIGHT,
    )(mine, theirs, gate_cols, up_cols)


def prologue_kernel(
    order_ref, at_ref, tokens_ref, grad_ref, q_ref, k_ref, v_ref, norm_ref, mlp_ref, q_gain_ref, k_gain_ref,
    tokens_out, grad_out, keep_ref, give_ref
):
    size = tokens_ref.shape[1] // 8
    for block in range(8):
        source = pl.ds(pl.multiple_of(order_ref[block] * size, 128), size)
        tokens_out[:, block * size : (block + 1) * size] = tokens_ref[:, source]
        grad_out[:, block * size : (block + 1) * size] = grad_ref[:, source]

    rows, q_width = q_ref.shape[0], q_ref.shape[1] // 2
    k_width = k_ref.shape[1] // 2
    total = q_width + 2 * k_width
    small = q_gain_ref.shape[1]
    place = lax.broadcasted_iota(jnp.int32, (small, HEAD_SIZE), 1) - lax.broadcasted_iota(
        jnp.int32, (small, HEAD_SIZE), 0
    )
    put = (place == at_ref[1] * small).astype(BF16)
    extra = jnp.concatenate(
        [
            jnp.concatenate([norm_ref[...], mlp_ref[...]], axis=1),
            jnp.concatenate(
                [
                    matmul(q_gain_ref[...], put).astype(BF16),
                    matmul(k_gain_ref[...], put).astype(BF16),
                    jnp.zeros((1, total - 2 * HEAD_SIZE), BF16),
                ],
                axis=1,
            ),
            jnp.zeros((14, total), BF16),
        ],
        axis=0,
    )
    for target, at in ((keep_ref, at_ref[0]), (give_ref, 1 - at_ref[0])):
        target[:rows, :q_width] = q_ref[:, pl.ds(pl.multiple_of(at * q_width, 128), q_width)]
        target[:rows, q_width : q_width + k_width] = k_ref[:, pl.ds(pl.multiple_of(at * k_width, 128), k_width)]
        target[:rows, q_width + k_width :] = v_ref[:, pl.ds(pl.multiple_of(at * k_width, 128), k_width)]
        target[rows:, :] = extra


def prologue(order, at, tokens, out_grad, q_weight, k_weight, v_weight, gains):
    shape = jax.ShapeDtypeStruct((q_weight.shape[0] + 16, (q_weight.shape[1] + 2 * k_weight.shape[1]) // 2), BF16)
    whole = lambda value: pl.BlockSpec(value.shape, lambda i, order_ref, at_ref: (0, 0))
    fixed = (q_weight, k_weight, v_weight) + gains
    return pl.pallas_call(
        prologue_kernel,
        name="prologue",
        grid_spec=pltpu.PrefetchScalarGridSpec(
            num_scalar_prefetch=2,
            grid=(1,),
            in_specs=[whole(tokens), whole(out_grad)] + [whole(value) for value in fixed],
            out_specs=[whole(tokens), whole(tokens), whole(shape), whole(shape)],
        ),
        out_shape=(jax.ShapeDtypeStruct(tokens.shape, BF16),) * 2 + (shape, shape),
        cost_estimate=LIGHT,
    )(order, at, tokens, out_grad, *fixed)


def after(token, values):
    return lax.optimization_barrier((token, values))[1]


def meet(token, values):
    return lax.optimization_barrier((token, values))


def trade(token, sends):
    held = after(token, [value for value, unused in sends])
    return [swap(value, axis) for value, (unused, axis) in zip(held, sends)]


def places_of(query_tile, key_tile, seq_lengths, tok_dev):
    rows = query_tile.shape[0] * tok_dev
    tile_ids = jnp.arange(key_tile.shape[0], dtype=jnp.int32)
    shares = (tile_ids // 16) * 8 + tile_ids % 8
    found = key_tile[None, :] == tile_ids[:, None]

    def offsets_of(parity):
        mine = found & (tile_ids // 8 % 2 == parity)[None, :]
        return jnp.sum(jnp.where(mine, shares * tok_dev + 1, 0), axis=1, dtype=jnp.int32) - 1

    offsets = (offsets_of(0), offsets_of(1))
    natural = query_tile[:, None] * tok_dev + jnp.arange(tok_dev, dtype=jnp.int32)[None, :]
    seq_ids = jnp.arange(seq_lengths.shape[0], dtype=jnp.int32)
    seq_ends = jnp.sum(jnp.where(seq_ids[None, :] <= seq_ids[:, None], seq_lengths[None, :], 0), axis=1, dtype=jnp.int32)
    starts = jnp.max(jnp.where(seq_ends <= natural[..., None], seq_ends, 0), axis=-1)
    tiles = (query_tile, jnp.max(jnp.where(seq_ends <= (query_tile * tok_dev)[:, None], seq_ends, 0), axis=-1) // (2 * tok_dev))
    start_rows = jnp.stack([starts, starts], axis=1)
    start_cols = jnp.broadcast_to(starts.reshape(rows, 1), (rows, 128))
    places = (natural - starts).reshape(rows)
    half_width = HEAD_SIZE // 2
    frequency = jnp.power(ROPE_BASE, -jnp.arange(half_width, dtype=F32) * (2.0 / HEAD_SIZE))
    angles = places.astype(F32)[:, None] * frequency[None, :]
    cosine = jnp.cos(angles)
    sine = jnp.sin(angles)
    cosine = jnp.concatenate([cosine, cosine], axis=1)
    sine = jnp.concatenate([-sine, sine], axis=1)
    return offsets, tiles, start_rows, start_cols, cosine, sine


FAR = 96
KEEP_ROWS = 128
UP_ROWS = 96


def paired_layer(
    tokens,
    out_grad,
    seq_lengths,
    block_deal,
    norm_gain,
    q_weight,
    k_weight,
    v_weight,
    q_gain,
    k_gain,
    o_weight,
    mlp_gain,
    gate_weight,
    up_weight,
    down_weight,
):
    y_at, core_at, zb_at, za_at, x_at = (lax.axis_index(name) for name in ("y", "core", "zb", "za", "x"))
    tok_dev, width = tokens.shape
    blk_rows = q_weight.shape[0]
    rows = 8 * tok_dev
    middle = rows // 2
    half, quarter = width // 2, width // 4
    token = seq_lengths


    place_ids = jnp.arange(8, dtype=jnp.int32)
    to_order = ((zb_at ^ (place_ids // 2 % 2)) * 2 + place_ids % 2) * 2 + (x_at ^ (place_ids // 4))
    from_order = ((x_at ^ (place_ids % 2)) * 2 + (zb_at ^ (place_ids // 4))) * 2 + place_ids // 2 % 2

    def in_order(mine, other, axis):
        first = jnp.where(za_at == 0, mine, other)
        second = jnp.where(za_at == 0, other, mine)
        return jnp.concatenate([first, second], axis=axis)

    def half_of(weight, at, axis):
        size = weight.shape[axis] // 2
        return lax.dynamic_slice_in_dim(weight, at * size, size, axis=axis)


    def near(value):
        return [(value, "y"), (value, "za")]

    def far(from_y, from_z, rows_y):
        sends = [(from_z[:rows_y], "y")]
        return sends + ([(from_y[rows_y:], "za")] if rows_y < tok_dev else [])

    def mine_of(value, from_y, from_z, fars):
        return jnp.concatenate([value, from_y, from_z] + fars, axis=0)

    def far_sums(kept):
        return [(kept[3 * tok_dev :].astype(BF16), "y")]

    def near_sums(kept, from_y):
        to_y, to_z = kept[tok_dev : 2 * tok_dev], kept[2 * tok_dev : 3 * tok_dev] + from_y.astype(F32)
        return [(to_y.astype(BF16), "y"), (to_z.astype(BF16), "za")]

    def own_sum(kept, nears):
        return kept[:tok_dev] + nears[0].astype(F32) + nears[1].astype(F32)


    def za_parts(part, axis):
        first = lax.slice_in_dim(part, 0, blk_rows, axis=axis)
        second = lax.slice_in_dim(part, blk_rows, 2 * blk_rows, axis=axis)
        return jnp.where(za_at == 0, first, second), jnp.where(za_at == 0, second, first).astype(BF16)

    def za_join(mine, other):
        other = other.astype(F32)
        return [jnp.where(za_at == 0, mine, other), jnp.where(za_at == 0, other, mine)]


    member = jnp.arange(8, dtype=jnp.int32)
    member_y, member_za, member_core = y_at ^ (member % 2), za_at ^ (member // 2 % 2), core_at ^ (member // 4)
    group = jnp.arange(4, dtype=jnp.int32)
    span_table = jnp.arange(block_deal.shape[0], dtype=jnp.int32)

    def natural_tile(zb_of, x_of):
        entry = 2 * ((zb_of * 2 + member_za) * 2 + x_of) + member_y
        span = jnp.sum(jnp.where(entry[..., None] == span_table, block_deal, 0), axis=-1, dtype=jnp.int32)
        return span * 2 + member_core

    query_tile = natural_tile(zb_at, x_at)
    key_tile = natural_tile(zb_at ^ (group % 2)[:, None], x_at ^ (group // 2)[:, None]).reshape(-1)
    offsets, tiles, start_rows, start_cols, cosine, sine = places_of(query_tile, key_tile, seq_lengths, tok_dev)


    q_width, k_width = q_weight.shape[1] // 2, k_weight.shape[1] // 2
    qkv_width = q_width + 2 * k_width
    local_low, grad_local, qkv_keep, qkv_give = prologue(
        to_order,
        jnp.stack([za_at, (zb_at * 2 + za_at) * 2 + x_at]),
        tokens,
        out_grad,
        q_weight,
        k_weight,
        v_weight,
        (norm_gain[None], mlp_gain[None], q_gain[None], k_gain[None]),
    )
    local_rows = local_low.astype(F32)
    o_give = half_of(o_weight, 1 - za_at, 0)
    za_place = za_at[None].astype(jnp.int32)
    z_keep, qkv_far, x_keep = swap(qkv_keep, "zb"), swap(qkv_give, "za"), swap(qkv_keep, "x")
    tokens_y = swap(local_low, "y")
    (o_far,) = trade(qkv_keep, [(o_give, "za")])
    token, (qkv_far, z_keep, x_keep, tokens_y, o_far) = meet(token, (qkv_far, z_keep, x_keep, tokens_y, o_far))
    down_keep = half_of(down_weight, za_at, 0)
    tokens_z, z_far, xz_keep, x_far, down_xk = trade(
        token, [(local_low, "za"), (qkv_far, "zb"), (z_keep, "x"), (qkv_far, "x"), (down_keep, "x")]
    )
    o_pair = in_order(half_of(o_weight, za_at, 0), o_far, 1)
    token, (z_far, tokens_z, xz_keep, x_far, o_pair, down_xk) = meet(
        token, (z_far, tokens_z, xz_keep, x_far, o_pair, down_xk)
    )
    *fars, xz_far, o_x, o_z = trade(
        token, far(tokens_y, tokens_z, FAR) + [(z_far, "x"), (o_pair, "x"), (o_pair, "zb")]
    )
    gate_weight, up_weight, down_weight = after(token, (gate_weight, up_weight, down_weight))
    gate_keep, up_keep = half_of(gate_weight, za_at, 1), half_of(up_weight, za_at, 1)
    gate_give, up_give = half_of(gate_weight, 1 - za_at, 1), half_of(up_weight, 1 - za_at, 1)
    down_give = half_of(down_weight, 1 - za_at, 0)
    token, (xz_far, fars, o_x, o_z) = meet(token, (xz_far, fars, o_x, o_z))
    mine = mine_of(local_low, tokens_y, tokens_z, fars)
    theirs, gate_zk0, gate_far, gate_xk = trade(
        token, [(mine, "core"), (gate_keep[:KEEP_ROWS], "zb"), (gate_give, "za"), (gate_keep, "x")]
    )
    qkv_all = jnp.concatenate(
        [
            in_order(qkv_keep, qkv_far, 0),
            in_order(z_keep, z_far, 0),
            in_order(x_keep, x_far, 0),
            in_order(xz_keep, xz_far, 0),
        ],
        axis=0,
    ).reshape(8, blk_rows + 16, qkv_width)
    qkv_cols = qkv_all[:, :blk_rows].reshape(width, qkv_width)
    gains = qkv_all[:, blk_rows, : 2 * blk_rows].astype(F32)
    gain_one = gains[:, :blk_rows].reshape(1, width)
    gain_two = gains[:, blk_rows:].reshape(1, width)
    head_sum = jnp.sum(qkv_all[:, blk_rows + 1, : 2 * HEAD_SIZE].astype(F32), axis=0, keepdims=True)
    qk_gains = jnp.concatenate([head_sum[:, :HEAD_SIZE], head_sum[:, HEAD_SIZE:]], axis=0)


    input_rows = jnp.concatenate([mine, theirs], axis=0).astype(F32)
    input_rho = lax.rsqrt(jnp.mean(input_rows * input_rows, axis=-1, keepdims=True) + EPSILON)
    normed = (input_rows * input_rho * gain_one).astype(BF16)
    raw = matmul(normed, qkv_cols)
    queries, kv_own = shape_heads(raw, cosine, sine, qk_gains)
    token, (queries, kv_own, gate_zk0, gate_far, gate_xk) = meet(
        token, (queries, kv_own, gate_zk0, gate_far, gate_xk)
    )
    kv_z, kv_x, up_far, grads_y = trade(
        token, [(kv_own, "zb"), (kv_own, "x"), (up_give, "za"), (grad_local, "y")]
    )
    token, (kv_x,) = meet(token, (kv_x,))
    (o_xz,) = trade(token, [(o_z, "x")])
    (attn_part,) = attend(offsets[0], tiles, queries, start_cols, [kv_own, kv_x], last=False)
    gate_pair = in_order(gate_keep, gate_far, 0)
    token, (kv_z, attn_part, grads_y, o_xz, up_far, gate_pair) = meet(
        token, (kv_z, attn_part, grads_y, o_xz, up_far, gate_pair)
    )
    gate_rest = jnp.concatenate([gate_keep[KEEP_ROWS:], gate_far], axis=0)
    token, (gate_rest,) = meet(token, (gate_rest,))
    kv_xz, gate_zr, grads_z = trade(token, [(kv_z, "x"), (gate_rest, "zb"), (grad_local, "za")])
    o_cols = jnp.concatenate([o_pair, o_z, o_x, o_xz], axis=1)
    token, (kv_xz, o_cols) = meet(token, (kv_xz, o_cols))
    (gate_xf,) = trade(token, [(gate_far, "x")])
    attn_low, inverse = attend(offsets[1], tiles, queries, start_cols, [kv_z, kv_xz], before=attn_part)
    given = matmul(attn_low[middle:], o_cols).astype(BF16)
    token, (given, attn_low, gate_xf, gate_zr, grads_z) = meet(token, (given, attn_low, gate_xf, gate_zr, grads_z))
    up_pair = in_order(up_keep, up_far, 0)
    given, up_z0, up_x0, grads_far, down_far = trade(
        token,
        [(given, "core"), (up_pair[:UP_ROWS], "zb"), (up_pair[:blk_rows], "x"), (grads_z, "y"), (down_give, "za")],
    )
    kept = matmul(attn_low[:middle], o_cols)
    token, (given, kept, up_z0, up_x0, up_pair, grads_far, down_far) = meet(
        token, (given, kept, up_z0, up_x0, up_pair, grads_far, down_far)
    )
    grad_mine = mine_of(grad_local, grads_y, grads_z, [grads_far])
    kept = kept + given.astype(F32)
    from_y, up_z1, up_x1 = trade(
        token,
        far_sums(kept) + [(up_pair[UP_ROWS:blk_rows], "zb"), (up_pair[blk_rows:], "x")],
    )
    gate_z = assemble(
        za_place,
        [
            (gate_zk0, 0, 1),
            (gate_zr[: blk_rows - KEEP_ROWS], KEEP_ROWS, 1),
            (gate_zr[blk_rows - KEEP_ROWS :], 0, -1),
        ],
        0,
    )
    token, (from_y, kept, up_x1, gate_z, up_z1, grad_mine) = meet(
        token, (from_y, kept, up_x1, gate_z, up_z1, grad_mine)
    )
    *nears, gate_xz, up_z2, grad_theirs = trade(
        token, near_sums(kept, from_y) + [(gate_z, "x"), (up_pair[blk_rows:], "zb"), (grad_mine, "core")]
    )
    token, (nears, kept, gate_xz, up_z2, grad_theirs) = meet(token, (nears, kept, gate_xz, up_z2, grad_theirs))
    up_z01 = jnp.concatenate([up_z0, up_z1], axis=0)
    residual = local_rows + own_sum(kept, nears)


    rho_two = lax.rsqrt(jnp.mean(residual * residual, axis=-1, keepdims=True) + EPSILON)
    unit_two = residual * rho_two
    mlp_low = (unit_two * gain_two).astype(BF16)
    token, (mlp_low,) = meet(token, (mlp_low,))
    mlp_y, mlp_z, down_zk, down_xf, up_xz0 = trade(
        token, near(mlp_low) + [(down_keep, "zb"), (down_far, "x"), (up_z01, "x")]
    )
    gate_cols = assemble(
        za_place,
        [(gate_pair, 0, 0), (gate_z, quarter, 0), (gate_xk, half, 1), (gate_xf, half, -1)]
        + [(gate_xz, half + quarter, 0)],
        0,
    )
    grad_mine, grad_theirs = after(token, (grad_mine, grad_theirs))
    grad_rows = assemble(za_place, [(grad_mine, 0, 0), (grad_theirs, middle, 0)], 0)
    token, (mlp_y, mlp_z, down_xf, up_xz0, gate_cols, down_zk, grad_rows) = meet(
        token, (mlp_y, mlp_z, down_xf, up_xz0, gate_cols, down_zk, grad_rows)
    )
    *fars, up_xz1, down_zf0 = trade(token, far(mlp_y, mlp_z, FAR) + [(up_z2, "x"), (down_far[:400], "zb")])
    token, (fars, down_zf0, up_xz1) = meet(token, (fars, down_zf0, up_xz1))
    mlp_mine = mine_of(mlp_low, mlp_y, mlp_z, fars)
    mlp_theirs, down_zf1, down_xzk, down_xzf0 = trade(
        token, [(mlp_mine, "core"), (down_far[400:], "zb"), (down_zk, "x"), (down_zf0, "x")]
    )
    up_cols = assemble(
        za_place,
        [
            (up_pair, 0, 0),
            (up_z01, quarter, 0),
            (up_z2, quarter + blk_rows, 0),
            (up_x0, half, 0),
            (up_x1, half + blk_rows, 0),
            (up_xz0, half + quarter, 0),
            (up_xz1, half + quarter + blk_rows, 0),
        ],
        0,
    )
    token, (mlp_theirs, up_cols, down_zf1, down_xzk, down_xzf0) = meet(
        token, (mlp_theirs, up_cols, down_zf1, down_xzk, down_xzf0)
    )
    (down_xzf1,) = trade(token, [(down_zf1, "x")])
    mlp_rows = jnp.concatenate([mlp_mine, mlp_theirs], axis=0)
    gate_act = matmul(mlp_rows, gate_cols)
    token, (gate_act, up_cols, mlp_rows) = meet(token, (gate_act, up_cols, mlp_rows))
    sig = jax.nn.sigmoid(gate_act)
    silu = gate_act * sig
    slope = sig * (1.0 + gate_act * (1.0 - sig))
    up_slope = silu.astype(BF16)
    token, (silu, slope, up_slope, up_cols, mlp_rows) = meet(token, (silu, slope, up_slope, up_cols, mlp_rows))
    up_act = matmul(mlp_rows, up_cols)
    hidden = (silu * up_act).astype(BF16)
    gate_slope = (up_act * slope).astype(BF16)
    down_zf = jnp.concatenate([down_zf0, down_zf1], axis=0)
    token, (hidden, gate_slope, up_slope, grad_rows, down_xzf1, down_zf) = meet(
        token, (hidden, gate_slope, up_slope, grad_rows, down_xzf1, down_zf)
    )
    down_xzf = jnp.concatenate([down_xzf0, down_xzf1], axis=0)

    def columns_of(value, piece):
        return value[:, piece * quarter : (piece + 1) * quarter]

    down_cols = assemble(
        za_place,
        [
            (down_keep, 0, 1),
            (down_far, 0, -1),
            (down_zk, quarter, 1),
            (down_zf, quarter, -1),
            (down_xk, half, 1),
            (down_xf, half, -1),
            (down_xzk, half + quarter, 1),
            (down_xzf, half + quarter, -1),
        ],
        1,
    )
    down_3 = contract_rows(hidden, columns_of(grad_rows, 3)).astype(BF16)
    token, (down_3, down_cols) = meet(token, (down_3, down_cols))
    (down_3,) = trade(token, [(down_3, "x")])
    hidden_grad = contract_cols(grad_rows, down_cols)
    gate_low = (hidden_grad * gate_slope.astype(F32)).astype(BF16)
    up_low = (hidden_grad * up_slope.astype(F32)).astype(BF16)

    kept, given = two_terms(gate_low, up_low, gate_cols, up_cols)
    token, (kept, given, gate_low, up_low, down_3) = meet(token, (kept, given, gate_low, up_low, down_3))
    hidden, grad_rows = after(token, (hidden, grad_rows))
    down_1 = (contract_rows(hidden, columns_of(grad_rows, 1)) + down_3.astype(F32)).astype(BF16)
    given, down_1a = trade(token, [(given, "core"), (down_1[:144], "zb")])
    gate_3 = contract_rows(columns_of(mlp_rows, 3), gate_low).astype(BF16)
    token, (given, kept, down_1, down_1a, gate_3) = meet(token, (given, kept, down_1, down_1a, gate_3))
    kept = kept + given.astype(F32)
    token, (kept,) = meet(token, (kept,))
    from_y, down_1b, gate_3 = trade(token, far_sums(kept) + [(down_1[144:416], "zb"), (gate_3, "x")])
    down_2 = contract_rows(hidden, columns_of(grad_rows, 2)).astype(BF16)
    up_3 = contract_rows(columns_of(mlp_rows, 3), up_low).astype(BF16)
    gate_1 = contract_rows(columns_of(mlp_rows, 1), gate_low)
    token, (from_y, kept, down_1b, gate_3, down_2, up_3, gate_1) = meet(
        token, (from_y, kept, down_1b, gate_3, down_2, up_3, gate_1)
    )
    *nears, down_1c, up_3 = trade(token, near_sums(kept, from_y) + [(down_1[416:], "zb"), (up_3, "x")])
    gate_1 = (gate_1 + gate_3.astype(F32)).astype(BF16)
    gate_2 = contract_rows(columns_of(mlp_rows, 2), gate_low).astype(BF16)
    up_1 = contract_rows(columns_of(mlp_rows, 1), up_low)
    up_2 = contract_rows(columns_of(mlp_rows, 2), up_low).astype(BF16)
    token, (nears, kept, down_1c, up_3, gate_2, up_1, up_2, gate_1) = meet(
        token, (nears, kept, down_1c, up_3, gate_2, up_1, up_2, gate_1)
    )
    mlp_in_grad = own_sum(kept, nears)
    gain_two_part = jnp.sum(mlp_in_grad * unit_two, axis=0, keepdims=True)
    scaled = mlp_in_grad * gain_two
    inner = jnp.mean(scaled * unit_two, axis=-1, keepdims=True)
    residual_grad = grad_local.astype(F32) + rho_two * (scaled - unit_two * inner)


    branch_low = residual_grad.astype(BF16)
    token, (branch_low, residual_grad, gain_two_part, gate_1) = meet(
        token, (branch_low, residual_grad, gain_two_part, gate_1)
    )
    branch_y, branch_z, gate_1a, gate_2 = trade(
        token, near(branch_low) + [(gate_1[:blk_rows], "zb"), (gate_2, "x")]
    )
    hidden, down_cols = after(token, (hidden, down_cols))
    out_given = matmul(hidden[middle:], down_cols).astype(BF16)
    up_1 = (up_1 + up_3.astype(F32)).astype(BF16)
    down_0 = contract_rows(hidden, columns_of(grad_rows, 0)) + jnp.concatenate(
        [down_1a, down_1b, down_1c], axis=0
    ).astype(F32)
    token, (branch_y, branch_z, gate_1a, gate_2, out_given, up_1, down_0, gate_low, up_low) = meet(
        token, (branch_y, branch_z, gate_1a, gate_2, out_given, up_1, down_0, gate_low, up_low)
    )
    gate_0 = contract_rows(columns_of(mlp_rows, 0), gate_low) + gate_2.astype(F32)
    *fars, gate_1b, down_2a = trade(
        token, far(branch_y, branch_z, FAR) + [(gate_1[blk_rows:384], "zb"), (down_2[:384], "x")]
    )
    hidden, down_cols = after(token, (hidden, down_cols))
    out_kept = matmul(hidden[:middle], down_cols)
    token, (fars, out_kept, gate_1b, down_2a, gate_0) = meet(token, (fars, out_kept, gate_1b, down_2a, gate_0))
    branch_mine = mine_of(branch_low, branch_y, branch_z, fars)
    branch_theirs, gate_1c, down_2b, out_given = trade(
        token,
        [(branch_mine, "core"), (gate_1[384:464], "zb"), (down_2[384:512], "x"), (out_given, "core")],
    )
    grad_own = contract_cols(branch_mine, o_cols).astype(BF16)
    attn_grad = jnp.concatenate([grad_own, contract_cols(branch_theirs, o_cols).astype(BF16)], axis=0)
    mixed = jnp.concatenate([gate_1[464:], up_1[:144]], axis=0)
    token, (attn_grad, gate_1c, down_2b, mixed) = meet(token, (attn_grad, gate_1c, down_2b, mixed))
    mixed, up_2a, down_2c = trade(token, [(mixed, "zb"), (up_2[:blk_rows], "x"), (down_2[512:], "x")])
    query_part, kv_1, kv_3 = attend_back(
        offsets[1], tiles, queries, start_rows, inverse, attn_low, attn_grad, [kv_z, kv_xz], last=False
    )
    out_kept = out_kept + out_given.astype(F32)
    token, (query_part, kv_1, kv_3, mixed, up_2a, down_2c, out_kept) = meet(
        token, (query_part, kv_1, kv_3, mixed, up_2a, down_2c, out_kept)
    )
    gate_1d, up_1a = mixed[:48], mixed[48:]
    kv_3, up_1b, out_from = trade(token, [(kv_3, "x"), (up_1[144:336], "zb")] + far_sums(out_kept))
    query_grad, kv_0, kv_2 = attend_back(
        offsets[0],
        tiles,
        queries,
        start_rows,
        inverse,
        attn_low,
        attn_grad,
        [kv_own, kv_x],
        before=query_part,
    )
    token, (query_grad, kv_0, kv_2, kv_3, up_1b, out_from) = meet(
        token, (query_grad, kv_0, kv_2, kv_3, up_1b, out_from)
    )
    kv_1 = (kv_1.astype(F32) + kv_3.astype(F32)).astype(BF16)
    kv_1, kv_2, *out_nears = trade(token, [(kv_1, "zb"), (kv_2, "x")] + near_sums(out_kept, out_from))
    token, (kv_2, branch_mine, branch_theirs, up_low, query_grad, gate_0, down_0) = meet(
        token, (kv_2, branch_mine, branch_theirs, up_low, query_grad, gate_0, down_0)
    )
    q_low, q_gain_part = shape_back(raw, query_grad, cosine, sine, qk_gains, 2, 0, 0, HEAD_SIZE**-0.5)
    q_3 = swap(contract_rows(columns_of(normed, 3), q_low).astype(BF16), "x")
    branch_rows = jnp.concatenate([branch_mine, branch_theirs], axis=0)
    o_3 = contract_rows(attn_low, columns_of(branch_rows, 3)).astype(BF16)
    q_1 = contract_rows(columns_of(normed, 1), q_low)
    gate_part = gate_0 + jnp.concatenate([gate_1a, gate_1b, gate_1c, gate_1d], axis=0).astype(F32)
    gate_mine, gate_give = za_parts(gate_part, 0)
    down_part = down_0 + jnp.concatenate([down_2a, down_2b, down_2c], axis=0).astype(F32)
    down_mine, down_give = za_parts(down_part, 1)
    token, (kv_1, out_nears, q_low, q_gain_part, o_3, gate_mine, gate_give, down_mine, down_give, q_1) = meet(
        token, (kv_1, out_nears, q_low, q_gain_part, o_3, gate_mine, gate_give, down_mine, down_give, q_1)
    )
    gate_give, up_1c, down_give, up_2b = trade(
        token, [(gate_give, "za"), (up_1[336:], "zb"), (down_give, "za"), (up_2[blk_rows:], "x")]
    )
    kv_grad = (kv_0.astype(F32) + kv_1.astype(F32) + kv_2.astype(F32)).astype(BF16)
    kv_low, k_gain_part = shape_back(raw, kv_grad, cosine, sine, qk_gains, 1, 2, 1, 1.0)
    low = jnp.concatenate([q_low, kv_low], axis=1)
    given = contract_cols(low[middle:], qkv_cols).astype(BF16)
    w_3 = contract_rows(columns_of(normed, 3), kv_low).astype(BF16)
    q_1 = (q_1 + q_3.astype(F32)).astype(BF16)
    token, (given, low, kv_low, k_gain_part, w_3, q_1, gate_give, up_1c, up_2b) = meet(
        token, (given, low, kv_low, k_gain_part, w_3, q_1, gate_give, up_1c, up_2b)
    )
    given_low = given
    kv_late, normed, low = after(token, (kv_low, normed, low))
    given, q_1, w_3, o_3 = trade(token, [(given, "core"), (q_1, "zb"), (w_3, "x"), (o_3, "x")])
    terms = contract_cols(low[:middle], qkv_cols)
    w_1 = contract_rows(columns_of(normed, 1), kv_late)
    token, (given, terms, q_1, w_3, o_3, w_1, down_give, up_low, attn_low, branch_rows) = meet(
        token, (given, terms, q_1, w_3, o_3, w_1, down_give, up_low, attn_low, branch_rows)
    )
    kept = terms + given.astype(F32)
    w_1 = (w_1 + w_3.astype(F32)).astype(BF16)
    token, (kept, w_1) = meet(token, (kept, w_1))
    from_y, w_1 = trade(token, far_sums(kept) + [(w_1, "zb")])
    o_1 = (contract_rows(attn_low, columns_of(branch_rows, 1)) + o_3.astype(F32)).astype(BF16)
    o_2 = contract_rows(attn_low, columns_of(branch_rows, 2)).astype(BF16)
    terms_low, given_low, normed_low = after(token, (terms, given_low, normed))
    gain_one_part = (
        jnp.sum(
            terms_low * normed_low[:middle].astype(F32) + given_low.astype(F32) * normed_low[middle:].astype(F32),
            axis=0,
            keepdims=True,
        )
        / gain_one
    )
    gain_sum = jnp.concatenate(
        [
            *reorder(from_order, [gain_one_part, gain_two_part], [F32, F32]),
            jnp.sum(q_gain_part, axis=0, keepdims=True),
            jnp.sum(k_gain_part, axis=0, keepdims=True),
        ],
        axis=1,
    )
    qw_2 = contract_rows(columns_of(normed, 2), low).astype(BF16)
    token, (from_y, kept, w_1, o_1, qw_2, o_2, gain_sum, up_low, attn_low, branch_rows, low) = meet(
        token, (from_y, kept, w_1, o_1, qw_2, o_2, gain_sum, up_low, attn_low, branch_rows, low)
    )
    *nears, o_1, qw_2, gain_x = trade(
        token, near_sums(kept, from_y) + [(o_1, "zb"), (qw_2, "x"), (gain_sum, "core")]
    )
    gain_sum = gain_sum + gain_x
    gain_sum = gain_sum + swap(gain_sum, "zb")
    gate_mine, gate_give, down_mine, down_give = after(token, (gate_mine, gate_give, down_mine, down_give))
    up_part = (
        contract_rows(columns_of(mlp_rows, 0), up_low)
        + jnp.concatenate([up_2a, up_2b], axis=0).astype(F32)
        + jnp.concatenate([up_1a, up_1b, up_1c], axis=0).astype(F32)
    )
    up_mine, up_give = za_parts(up_part, 0)
    qw_0 = contract_rows(columns_of(normed, 0), low)
    o_0 = contract_rows(attn_low, columns_of(branch_rows, 0))
    block_out = residual + own_sum(out_kept, out_nears)
    token, (nears, kept, qw_2, qw_0, o_0, block_out, gain_sum, o_1, up_mine, up_give) = meet(
        token, (nears, kept, qw_2, qw_0, o_0, block_out, gain_sum, o_1, up_mine, up_give)
    )
    qkv_mine, qkv_give = za_parts(qw_0 + qw_2.astype(F32) + jnp.concatenate([q_1, w_1], axis=1).astype(F32), 0)
    token, (qkv_mine, qkv_give) = meet(token, (qkv_mine, qkv_give))
    gain_x, qkv_give, up_give, o_2 = trade(
        token, [(gain_sum, "za"), (qkv_give, "za"), (up_give, "za"), (o_2, "x")]
    )
    gain_sum = gain_sum + gain_x
    gain_x = swap(gain_sum, "y")
    o_mine, o_give = za_parts(o_0 + o_2.astype(F32) + o_1.astype(F32), 1)
    token, (gain_sum, o_mine, o_give) = meet(token, (gain_sum + gain_x, o_mine, o_give))
    gain_x, o_give = trade(token, [(gain_sum, "x"), (o_give, "za")])
    gain_sum = gain_sum + gain_x
    input_grad = own_sum(kept, nears)
    unit_one = local_rows * (rho_one := lax.rsqrt(jnp.mean(local_rows * local_rows, axis=-1, keepdims=True) + EPSILON))
    scaled = input_grad * gain_one
    inner = jnp.mean(scaled * unit_one, axis=-1, keepdims=True)
    in_grad = residual_grad + rho_one * (scaled - unit_one * inner)
    block_out, in_grad = reorder(from_order, [block_out, in_grad], [BF16, F32])
    device = (((y_at * 2 + core_at) * 2 + zb_at) * 2 + za_at) * 2 + x_at

    def own_slice(first, length):
        share = length // 32
        return lax.dynamic_slice_in_dim(gain_sum[0], first + device * share, share, axis=0)

    qkv_parts = za_join(qkv_mine, qkv_give)

    def columns(lo, hi):
        return jnp.concatenate([part[:, lo:hi] for part in qkv_parts], axis=1)

    return (
        block_out,
        in_grad,
        own_slice(0, width),
        columns(0, q_width),
        columns(q_width, q_width + k_width),
        columns(q_width + k_width, qkv_width),
        own_slice(2 * width, HEAD_SIZE),
        own_slice(2 * width + HEAD_SIZE, HEAD_SIZE),
        jnp.concatenate(za_join(o_mine, o_give), axis=0),
        own_slice(width, width),
        jnp.concatenate(za_join(gate_mine, gate_give), axis=1),
        jnp.concatenate(za_join(up_mine, up_give), axis=1),
        jnp.concatenate(za_join(down_mine, down_give), axis=0),
    )


def layer(
    sizes,
    tokens,
    out_grad,
    seq_lengths,
    block_deal,
    norm_gain,
    q_weight,
    k_weight,
    v_weight,
    q_gain,
    k_gain,
    o_weight,
    mlp_gain,
    gate_weight,
    up_weight,
    down_weight,
):
    y_count, core_count, zb_count, za_count, x_count = sizes
    pairwise = sizes == (2, 2, 2, 2, 2)
    all_axes = ("y", "core", "zb", "za", "x")
    y_at, core_at, zb_at, za_at, x_at = (lax.axis_index(name) for name in all_axes)
    tok_dev, width = tokens.shape
    blk_rows = q_weight.shape[0]
    group_count = zb_count * x_count
    member_count = y_count * core_count * za_count
    head_count = y_count * core_count
    rows = member_count * tok_dev
    piece = za_count * blk_rows


    def gather_rows(value):
        if not pairwise:
            return lax.all_gather(value, ("y", "core", "za"), axis=0, tiled=True)
        half = tok_dev // 2
        along_y = swap(value, "y")
        along_z = swap(value, "za")
        parts = [value, along_y, along_z, swap(along_z[:half], "y"), swap(along_y[half:], "za")]
        mine = jnp.concatenate(parts, axis=0)
        return jnp.concatenate([mine, swap(mine, "core")], axis=0)

    def scatter_rows(part_of):
        if not pairwise:
            full = part_of(slice(0, rows)).astype(BF16)
            return lax.psum_scatter(full, ("y", "core", "za"), scatter_dimension=0, tiled=True).astype(F32)
        middle = rows // 2
        half = tok_dev // 2
        given = swap(part_of(slice(middle, rows)).astype(BF16), "core")
        kept = part_of(slice(0, middle)) + given.astype(F32)
        own, to_y, to_z, far = (kept[i * tok_dev : (i + 1) * tok_dev] for i in range(4))
        far = far.astype(BF16)
        from_y = swap(far[:half], "y").astype(F32)
        from_z = swap(far[half:], "za").astype(F32)
        z_sum = jnp.concatenate([to_z[:half] + from_y, to_z[half:]], axis=0).astype(BF16)
        y_sum = jnp.concatenate([to_y[:half], to_y[half:] + from_z], axis=0).astype(BF16)
        return own + swap(y_sum, "y").astype(F32) + swap(z_sum, "za").astype(F32)


    def gather_pieces(own, axis):
        if not pairwise:
            return lax.all_gather(own, ("zb", "x"), axis=axis, tiled=True)
        along_z = swap(own, "zb")
        return jnp.concatenate([own, along_z, swap(own, "x"), swap(along_z, "x")], axis=axis)

    def scatter_pieces(part_of, length, axis):
        if not pairwise:
            full = part_of(0, length).astype(BF16)
            return lax.psum_scatter(full, ("zb", "x"), scatter_dimension=axis, tiled=True).astype(F32)
        half, quarter = length // 2, length // 4
        given = swap(part_of(half, length).astype(BF16), "x")
        kept = part_of(0, half) + given.astype(F32)
        given = swap(lax.slice_in_dim(kept, quarter, half, axis=axis).astype(BF16), "zb")
        return lax.slice_in_dim(kept, 0, quarter, axis=axis) + given.astype(F32)

    def in_order(mine, other, axis):
        first = jnp.where(za_at == 0, mine, other)
        second = jnp.where(za_at == 0, other, mine)
        return jnp.concatenate([first, second], axis=axis)

    def gather_weight(part_of, axis):
        mine = part_of(za_at)
        if za_count > 1:
            mine = in_order(mine, swap(part_of(1 - za_at), "za"), axis)
        return gather_pieces(mine, axis)

    def scatter_weight(part_of, axis):
        part = scatter_pieces(part_of, width, axis)
        if za_count == 1:
            return [part]
        first = lax.slice_in_dim(part, 0, blk_rows, axis=axis)
        second = lax.slice_in_dim(part, blk_rows, 2 * blk_rows, axis=axis)
        mine = jnp.where(za_at == 0, first, second)
        other = swap(jnp.where(za_at == 0, second, first).astype(BF16), "za").astype(F32)
        return [jnp.where(za_at == 0, mine, other), jnp.where(za_at == 0, other, mine)]

    def half_of(weight, at, axis):
        size = weight.shape[axis] // za_count
        return lax.dynamic_slice_in_dim(weight, at * size, size, axis=axis)


    def piece_group(index):
        if pairwise:
            return zb_at ^ (index % 2), x_at ^ (index // 2)
        return index // x_count, index % x_count

    def to_pieces(value):
        blocks = []
        for index in range(group_count):
            zb_of, x_of = piece_group(index)
            for za_of in range(za_count):
                block = (zb_of * za_count + za_of) * x_count + x_of
                blocks.append(lax.dynamic_slice_in_dim(value, block * blk_rows, blk_rows, axis=1))
        return jnp.concatenate(blocks, axis=1) if pairwise else value

    def from_pieces(value):
        if not pairwise:
            return value
        blocks = []
        for block in range(group_count * za_count):
            zb_of, za_of, x_of = block // 4, block // 2 % 2, block % 2
            index = (x_at ^ x_of) * 2 + (zb_at ^ zb_of)
            blocks.append(lax.dynamic_slice_in_dim(value, (index * 2 + za_of) * blk_rows, blk_rows, axis=1))
        return jnp.concatenate(blocks, axis=1)


    per_span = head_count // 2
    member = jnp.arange(member_count, dtype=jnp.int32)
    if pairwise:
        member_y, member_za, member_core = y_at ^ (member % 2), za_at ^ (member // 2 % 2), core_at ^ (member // 4)
    else:
        member_za = member % za_count
        member_core = member // za_count % core_count
        member_y = member // (za_count * core_count)
    group = jnp.arange(group_count, dtype=jnp.int32)
    group_zb, group_x = piece_group(group)
    member_head = member_y * core_count + member_core
    span_table = jnp.arange(block_deal.shape[0], dtype=jnp.int32)

    def natural_tile(zb_of, x_of):
        blk = (zb_of * za_count + member_za) * x_count + x_of
        entry = 2 * blk + member_head // per_span
        span = jnp.sum(
            jnp.where(entry[..., None] == span_table, block_deal, 0), axis=-1, dtype=jnp.int32
        )
        return span * per_span + member_head % per_span

    query_tile = natural_tile(zb_at, x_at)
    key_tile = natural_tile(group_zb[:, None], group_x[:, None]).reshape(-1)
    tile_ids = jnp.arange(key_tile.shape[0], dtype=jnp.int32)
    offsets = jnp.sum(
        jnp.where(key_tile[None, :] == tile_ids[:, None], tile_ids[None, :] * tok_dev, 0), axis=1, dtype=jnp.int32
    )
    natural = query_tile[:, None] * tok_dev + jnp.arange(tok_dev, dtype=jnp.int32)[None, :]
    seq_ids = jnp.arange(seq_lengths.shape[0], dtype=jnp.int32)
    seq_ends = jnp.sum(jnp.where(seq_ids[None, :] <= seq_ids[:, None], seq_lengths[None, :], 0), axis=1, dtype=jnp.int32)
    starts = jnp.max(jnp.where(seq_ends <= natural[..., None], seq_ends, 0), axis=-1)
    tiles = (query_tile, starts[:, 0] // (2 * tok_dev))
    start_rows = jnp.stack([starts, starts], axis=1)
    start_cols = jnp.broadcast_to(starts.reshape(rows, 1), (rows, 128))
    places = (natural - starts).reshape(rows)
    half_width = HEAD_SIZE // 2
    frequency = jnp.power(ROPE_BASE, -jnp.arange(half_width, dtype=F32) * (2.0 / HEAD_SIZE))
    angles = places.astype(F32)[:, None] * frequency[None, :]
    cosine = jnp.cos(angles)
    sine = jnp.sin(angles)
    cosine = jnp.concatenate([cosine, cosine], axis=1)
    sine = jnp.concatenate([-sine, sine], axis=1)


    q_width = q_weight.shape[1] // za_count
    k_width = k_weight.shape[1] // za_count
    qkv_width = q_width + 2 * k_width
    gain_pad = 16

    gain_row = jnp.concatenate([norm_gain, mlp_gain])
    head_gains = jnp.concatenate([q_gain, k_gain])

    def gain_rows():
        top = jnp.pad(gain_row, (0, qkv_width - gain_row.shape[0]))[None]
        bottom = jnp.pad(head_gains, (0, qkv_width - head_gains.shape[0]))[None]
        return jnp.concatenate([top, bottom, jnp.zeros((gain_pad - 2, qkv_width), BF16)], axis=0)

    def qkv_part(at):
        return jnp.concatenate(
            [half_of(q_weight, at, 1), half_of(k_weight, at, 1), half_of(v_weight, at, 1), ], axis=1
        )

    padded = blk_rows + gain_pad
    own_gain_rows = gain_rows()
    qkv_all = gather_weight(lambda at: jnp.concatenate([qkv_part(at), own_gain_rows], axis=0), 0)
    qkv_all = qkv_all.reshape(group_count * za_count, padded, qkv_width)
    qkv_cols = qkv_all[:, :blk_rows].reshape(width, qkv_width)
    gains = qkv_all[:, blk_rows, : 2 * blk_rows].astype(F32)
    gain_one = gains[:, :blk_rows].reshape(1, width)
    gain_two = gains[:, blk_rows:].reshape(1, width)
    small = q_gain.shape[0]
    head_parts = qkv_all[:, blk_rows + 1, : 2 * small].astype(F32).reshape(group_count * za_count, 2, small)

    def head_gain(which):
        return from_small(head_parts[:, which])

    def from_small(parts):
        if not pairwise:
            return parts.reshape(1, -1)
        rows_of = []
        for block in range(8):
            zb_of, za_of, x_of = block // 4, block // 2 % 2, block % 2
            index = ((x_at ^ x_of) * 2 + (zb_at ^ zb_of)) * 2 + za_of
            rows_of.append(lax.dynamic_slice_in_dim(parts, index, 1, axis=0))
        return jnp.concatenate(rows_of, axis=1)

    qk_gains = jnp.concatenate([head_gain(0), head_gain(1)], axis=0)


    local_low = to_pieces(tokens)
    local_rows = local_low.astype(F32)
    input_rows = gather_rows(local_low).astype(F32)
    o_cols = gather_weight(lambda at: half_of(o_weight, at, 0), 1)
    gu_cols = gather_weight(
        lambda at: jnp.concatenate([half_of(gate_weight, at, 1), half_of(up_weight, at, 1)], axis=1), 0
    )
    down_cols = gather_weight(lambda at: half_of(down_weight, at, 0), 1)
    grad_local = to_pieces(out_grad)
    grad_rows = gather_rows(grad_local)

    def unit_rows(value):
        return value * lax.rsqrt(jnp.mean(value * value, axis=-1, keepdims=True) + EPSILON)

    input_unit = unit_rows(input_rows)
    normed = (input_unit * gain_one).astype(BF16)
    raw = matmul(normed, qkv_cols)
    queries, kv_own = shape_heads(raw, cosine, sine, qk_gains)
    key_values = gather_pieces(kv_own, 0)
    attn_low, inverse = attend(offsets, tiles, queries, start_cols, [key_values])
    residual = local_rows + scatter_rows(lambda at: matmul(attn_low[at], o_cols))


    rho_two = lax.rsqrt(jnp.mean(residual * residual, axis=-1, keepdims=True) + EPSILON)
    unit_two = residual * rho_two
    mlp_rows = gather_rows((unit_two * gain_two).astype(BF16))
    ff = gu_cols.shape[1] // 2
    gate_up = matmul(mlp_rows, gu_cols)
    gate_act, up_act = gate_up[:, :ff], gate_up[:, ff:]
    sig = jax.nn.sigmoid(gate_act)
    silu = gate_act * sig
    hidden = (silu * up_act).astype(BF16)
    hidden_grad = contract_cols(grad_rows, down_cols)
    gate_low = (hidden_grad * up_act * (sig * (1.0 + gate_act * (1.0 - sig)))).astype(BF16)
    up_low = (hidden_grad * silu).astype(BF16)
    gu_low = jnp.concatenate([gate_low, up_low], axis=1)
    mlp_in_grad = scatter_rows(lambda at: contract_cols(gu_low[at], gu_cols))

    down_parts = scatter_weight(lambda lo, hi: contract_rows(hidden, grad_rows[:, lo:hi]), 1)
    gate_parts = scatter_weight(lambda lo, hi: contract_rows(mlp_rows[:, lo:hi], gate_low), 0)
    up_parts = scatter_weight(lambda lo, hi: contract_rows(mlp_rows[:, lo:hi], up_low), 0)
    block_out = residual + scatter_rows(lambda at: matmul(hidden[at], down_cols))

    gain_two_part = jnp.sum(mlp_in_grad * unit_two, axis=0, keepdims=True)
    scaled = mlp_in_grad * gain_two
    inner = jnp.mean(scaled * unit_two, axis=-1, keepdims=True)
    residual_grad = grad_local.astype(F32) + rho_two * (scaled - unit_two * inner)


    branch_rows = gather_rows(residual_grad.astype(BF16))
    attn_grad = contract_cols(branch_rows, o_cols).astype(BF16)
    query_grad, kv_grads = attend_back(
        offsets, tiles, queries, start_rows, inverse, attn_low, attn_grad, [key_values]
    )
    o_parts = scatter_weight(lambda lo, hi: contract_rows(attn_low, branch_rows[:, lo:hi]), 1)
    kv_grad = scatter_pieces(lambda lo, hi: kv_grads[lo:hi].astype(F32), kv_grads.shape[0], 0).astype(BF16)
    q_low, q_gain_part = shape_back(raw, query_grad, cosine, sine, qk_gains, 2, 0, 0, HEAD_SIZE**-0.5)
    kv_low, k_gain_part = shape_back(raw, kv_grad, cosine, sine, qk_gains, 1, 2, 1, 1.0)
    low = jnp.concatenate([q_low, kv_low], axis=1)

    gain_one_parts = []

    def input_terms(at):
        terms = contract_cols(low[at], qkv_cols)
        gain_one_parts.append(jnp.sum(terms * input_unit[at], axis=0, keepdims=True))
        return terms

    input_grad = scatter_rows(input_terms)
    qkv_parts = scatter_weight(lambda lo, hi: contract_rows(normed[:, lo:hi], low), 0)

    gain_sum = jnp.concatenate(
        [
            from_pieces(sum(gain_one_parts)),
            from_pieces(gain_two_part),
            jnp.sum(q_gain_part, axis=0, keepdims=True),
            jnp.sum(k_gain_part, axis=0, keepdims=True),
        ],
        axis=1,
    )
    if pairwise:
        for name in ("core", "y", "za", "x", "zb"):
            gain_sum = gain_sum + swap(gain_sum, name)
    else:
        gain_sum = lax.psum(gain_sum, all_axes)

    unit_one = local_rows * (rho_one := lax.rsqrt(jnp.mean(local_rows * local_rows, axis=-1, keepdims=True) + EPSILON))
    scaled = input_grad * gain_one
    inner = jnp.mean(scaled * unit_one, axis=-1, keepdims=True)
    in_grad = residual_grad + rho_one * (scaled - unit_one * inner)

    device = (((y_at * core_count + core_at) * zb_count + zb_at) * za_count + za_at) * x_count + x_at
    device_count = head_count * zb_count * za_count * x_count

    def own_slice(first, length):
        share = length // device_count
        return lax.dynamic_slice_in_dim(gain_sum[0], first + device * share, share, axis=0)

    def join(parts, lo, hi, axis):
        cut = [lax.slice_in_dim(part, lo, hi, axis=axis) for part in parts]
        return jnp.concatenate(cut, axis=axis)

    return (
        from_pieces(block_out).astype(BF16),
        from_pieces(in_grad),
        own_slice(0, width),
        join(qkv_parts, 0, q_width, 1),
        join(qkv_parts, q_width, q_width + k_width, 1),
        join(qkv_parts, q_width + k_width, qkv_width, 1),
        own_slice(2 * width, HEAD_SIZE),
        own_slice(2 * width + HEAD_SIZE, HEAD_SIZE),
        jnp.concatenate(o_parts, axis=0),
        own_slice(width, width),
        jnp.concatenate(gate_parts, axis=1),
        jnp.concatenate(up_parts, axis=1),
        jnp.concatenate(down_parts, axis=0),
    )


def solution(mesh):
    heads, blks = mesh.shape["head"], mesh.shape["blk"]
    za_count = KEY_VALUE_HEADS // heads
    side = math.isqrt(blks // za_count)
    sizes = (heads // 2, 2, side, za_count, side)
    names = ("y", "core", "zb", "za", "x")
    devices = mesh.devices.reshape(sizes)
    inner = Mesh(devices, names)
    head, blk = ("y", "core"), ("zb", "za", "x")
    rows, in_weight, out_weight, gain = P(names, None), P(blk, head), P(head, blk), P(blk)
    return jax.shard_map(
        paired_layer if sizes == (2, 2, 2, 2, 2) else functools.partial(layer, sizes),
        mesh=inner,
        in_specs=(
            rows,
            rows,
            P(),
            P(),
            gain,
            in_weight,
            in_weight,
            in_weight,
            gain,
            gain,
            out_weight,
            gain,
            in_weight,
            in_weight,
            out_weight,
        ),
        out_specs=(
            rows,
            rows,
            P(names),
            in_weight,
            in_weight,
            in_weight,
            P(names),
            P(names),
            out_weight,
            P(names),
            in_weight,
            in_weight,
            out_weight,
        ),
        check_vma=False,
    )
```

profile of v0, /device:TPU:0, one launch (start us, length us, event | category | flops | bytes accessed | tf_op | source)
XLA Modules:
  0.0 554.6 jit_solution(14497287223242215182)
XLA Ops:
  4.2 3.3 prologue.1
  7.5 4.0 collective-permute-start.1
  23.8 5.0 collective-permute-done.4
  39.6 3.3 collective-permute-done.5
  43.0 4.5 collective-permute-done.8
  47.5 5.6 %collective-permute-done.9.refs_4_ = bf16[768,256]{1,0:T(8,128)(2,1)S(1)} collective-permute-done((bf16[768,256]{1,0:T(8,128)(2,1)S(1)}, bf16[768,256]{1,0:T(8,128)(2,1)S(1)}, u32[]{:S(2)}, u32[]{:S(2)}) %collective-permute-start.9) | collective-permute-done | bytes 393248 | tf_op jit(solution)/shard_map/ppermute | solution.py:39
  59.8 3.0 collective-permute-done.12
  64.3 3.2 collective-permute-done.14
  80.5 4.4 collective-permute-done.17
  89.2 9.3 %collective-permute-done.19.refs_1_ = bf16[1024,256]{1,0:T(8,128)(2,1)S(1)} collective-permute-done((bf16[1024,256]{1,0:T(8,128)(2,1)S(1)}, bf16[1024,256]{1,0:T(8,128)(2,1)S(1)}, u32[]{:S(2)}, u32[]{:S(2)}) %collective-permute-start.19) | collective-permute-done | bytes 524320 | tf_op jit(solution)/shard_map/ppermute | solution.py:39
  100.1 5.2 attend.2.refs_2_
  106.1 4.9 collective-permute-done.20.refs_0_
  114.8 10.1 %collective-permute-done.24.refs_1_ = bf16[1024,256]{1,0:T(8,128)(2,1)S(1)} collective-permute-done((bf16[1024,256]{1,0:T(8,128)(2,1)S(1)}, bf16[1024,256]{1,0:T(8,128)(2,1)S(1)}, u32[]{:S(2)}, u32[]{:S(2)}) %collective-permute-start.24) | collective-permute-done | bytes 524320 | tf_op jit(solution)/shard_map/ppermute | solution.py:39
  129.0 7.1 %collective-permute-done.27 = bf16[128,2048]{1,0:T(8,128)(2,1)S(1)} collective-permute-done((bf16[128,2048]{1,0:T(8,128)(2,1)S(1)}, bf16[128,2048]{1,0:T(8,128)(2,1)S(1)}, u32[]{:S(2)}, u32[]{:S(2)}) %collective-permute-start.27) | collective-permute-done | bytes 524320 | tf_op jit(solution)/shard_map/ppermute | solution.py:39
  136.0 4.0 collective-permute-done.26
  144.9 8.8 %collective-permute-done.29 = bf16[96,768]{1,0:T(8,128)(2,1)S(1)} collective-permute-done((bf16[96,768]{1,0:T(8,128)(2,1)S(1)}, bf16[96,768]{1,0:T(8,128)(2,1)S(1)}, u32[]{:S(2)}, u32[]{:S(2)}) %collective-permute-start.29) | collective-permute-done | bytes 147488 | tf_op jit(solution)/shard_map/ppermute | solution.py:39
  160.9 11.1 %collective-permute-done.35 = bf16[160,768]{1,0:T(8,128)(2,1)S(1)} collective-permute-done((bf16[160,768]{1,0:T(8,128)(2,1)S(1)}, bf16[160,768]{1,0:T(8,128)(2,1)S(1)}, u32[]{:S(2)}, u32[]{:S(2)}) %collective-permute-start.35) | collective-permute-done | bytes 245792 | tf_op jit(solution)/shard_map/ppermute | solution.py:39
  176.4 17.6 %collective-permute-done.39.refs_2_ = bf16[256,768]{1,0:T(8,128)(2,1)S(1)} collective-permute-done((bf16[256,768]{1,0:T(8,128)(2,1)S(1)}, bf16[256,768]{1,0:T(8,128)(2,1)S(1)}, u32[]{:S(2)}, u32[]{:S(2)}) %collective-permute-start.39) | collective-permute-done | bytes 393248 | tf_op jit(solution)/shard_map/ppermute | solution.py:39
  203.4 7.7 %collective-permute-done.43.refs_5_ = bf16[768,256]{1,0:T(8,128)(2,1)S(1)} collective-permute-done((bf16[768,256]{1,0:T(8,128)(2,1)S(1)}, bf16[768,256]{1,0:T(8,128)(2,1)S(1)}, u32[]{:S(2)}, u32[]{:S(2)}) %collective-permute-start.43) | collective-permute-done | bytes 393248 | tf_op jit(solution)/shard_map/ppermute | solution.py:39
  211.0 6.2 %collective-permute-done.44.refs_5_ = bf16[256,768]{1,0:T(8,128)(2,1)S(1)} collective-permute-done((bf16[256,768]{1,0:T(8,128)(2,1)S(1)}, bf16[256,768]{1,0:T(8,128)(2,1)S(1)}, u32[]{:S(2)}, u32[]{:S(2)}) %collective-permute-start.44) | collective-permute-done | bytes 393248 | tf_op jit(solution)/shard_map/ppermute | solution.py:39
  225.2 6.2 %collective-permute-done.48 = bf16[400,256]{1,0:T(8,128)(2,1)S(1)} collective-permute-done((bf16[400,256]{1,0:T(8,128)(2,1)S(1)}, bf16[400,256]{1,0:T(8,128)(2,1)S(1)}, u32[]{:S(2)}, u32[]{:S(2)}) %collective-permute-start.48) | collective-permute-done | bytes 204832 | tf_op jit(solution)/shard_map/ppermute | solution.py:39
  235.3 9.8 %collective-permute-done.51 = bf16[368,256]{1,0:T(8,128)(2,1)S(1)} collective-permute-done((bf16[368,256]{1,0:T(8,128)(2,1)S(1)}, bf16[368,256]{1,0:T(8,128)(2,1)S(1)}, u32[]{:S(2)}, u32[]{:S(2)}) %collective-permute-start.51) | collective-permute-done | bytes 188448 | tf_op jit(solution)/shard_map/ppermute | solution.py:39
  247.8 3.4 fusion.81
  253.3 3.9 multiply_convert_fusion.2
  262.0 5.0 multiply_convert_fusion
  267.0 10.8 %two_terms.1 = (f32[512,2048]{1,0:T(8,128)}, bf16[512,2048]{1,0:T(8,128)(2,1)}) custom-call(bf16[1024,768]{1,0:T(8,128)(2,1)} %get-tuple-element.652.left_ref, bf16[1024,768]{1,0:T(8,128)(2,1)} %get-tuple-element.780.right_ref, bf16[2048,768]{1,0:T(8,128)(2,1)} %copy-done.2, bf16[2048,768]{1,0:T(8,128)(2,1)} %copy-done.3), custom_call_target="tpu_custom_call" | custom-call | flops 1000 | bytes 1000 | tf_op jit(solution)/shard_map/two_terms/pallas_call | solution.py:384
  279.8 2.8 fusion.27
  287.9 6.7 %collective-permute-done.57 = bf16[144,512]{1,0:T(8,128)(2,1)S(1)} collective-permute-done((bf16[144,512]{1,0:T(8,128)(2,1)S(1)}, bf16[144,512]{1,0:T(8,128)(2,1)S(1)}, u32[]{:S(2)}, u32[]{:S(2)}) %collective-permute-start.57) | collective-permute-done | bytes 147488 | tf_op jit(solution)/shard_map/ppermute | solution.py:39
  301.4 12.4 %collective-permute-done.59 = bf16[272,512]{1,0:T(8,128)(2,1)S(1)} collective-permute-done((bf16[272,512]{1,0:T(8,128)(2,1)S(1)}, bf16[272,512]{1,0:T(8,128)(2,1)S(1)}, u32[]{:S(2)}, u32[]{:S(2)}) %collective-permute-start.59) | collective-permute-done | bytes 278560 | tf_op jit(solution)/shard_map/ppermute | solution.py:39
  322.1 14.4 %collective-permute-done.63 = bf16[352,512]{1,0:T(8,128)(2,1)S(1)} collective-permute-done((bf16[352,512]{1,0:T(8,128)(2,1)S(1)}, bf16[352,512]{1,0:T(8,128)(2,1)S(1)}, u32[]{:S(2)}, u32[]{:S(2)}) %collective-permute-start.63) | collective-permute-done | bytes 360480 | tf_op jit(solution)/shard_map/ppermute | solution.py:39
  348.6 12.5 %collective-permute-done.67 = bf16[256,768]{1,0:T(8,128)(2,1)S(1)} collective-permute-done((bf16[256,768]{1,0:T(8,128)(2,1)S(1)}, bf16[256,768]{1,0:T(8,128)(2,1)S(1)}, u32[]{:S(2)}, u32[]{:S(2)}) %collective-permute-start.67) | collective-permute-done | bytes 393248 | tf_op jit(solution)/shard_map/ppermute | solution.py:39
  370.6 4.2 collective-permute-done.71
  380.9 5.0 collective-permute-done.74
  388.9 3.0 attend_back.2
  392.0 10.7 %collective-permute-done.78 = bf16[256,512]{1,0:T(8,128)(2,1)S(1)} collective-permute-done((bf16[256,512]{1,0:T(8,128)(2,1)S(1)}, bf16[256,512]{1,0:T(8,128)(2,1)S(1)}, u32[]{:S(2)}, u32[]{:S(2)}) %collective-permute-start.78) | collective-permute-done | bytes 262176 | tf_op jit(solution)/shard_map/ppermute | solution.py:39
  408.3 8.0 %attend_back.3 = (bf16[1024,256]{1,0:T(8,128)(2,1)S(1)}, bf16[1024,256]{1,0:T(8,128)(2,1)S(1)}, bf16[1024,256]{1,0:T(8,128)(2,1)S(1)}) custom-call(s32[32]{0:T(128)S(1)} %broadcast_add_fusion.1.off_ref, s32[8]{0:T(128)S(1)} %get-tuple-element.834.tile_ref, s32[8]{0:T(128)S(1)} %and_select_fusion.low_ref, bf16[1024,256]{1,0:T(8,128)(2,1)S(1)} %get-tuple-element.462.q_ref, ...), custom_call_target="tpu_custom_call" | custom-call | flops 1000 | bytes 1000 | tf_op jit(solution)/shard_map/attend_back/pallas_call | solution.py:213
  416.3 4.2 collective-permute-done.81
  422.1 3.3 collective-permute-start.84
  428.7 5.1 collective-permute-done.83
  443.8 3.5 collective-permute-done.84
  461.3 7.3 %collective-permute-done.89 = bf16[176,768]{1,0:T(8,128)(2,1)S(1)} collective-permute-done((bf16[176,768]{1,0:T(8,128)(2,1)S(1)}, bf16[176,768]{1,0:T(8,128)(2,1)S(1)}, u32[]{:S(2)}, u32[]{:S(2)}) %collective-permute-start.89) | collective-permute-done | bytes 270368 | tf_op jit(solution)/shard_map/ppermute | solution.py:39
  471.1 3.1 collective-permute-start.95
  480.1 3.2 fusion.47
  492.2 3.6 convert_add_fusion
  503.9 6.9 %collective-permute-done.97 = bf16[512,256]{1,0:T(8,128)(2,1)S(1)} collective-permute-done((bf16[512,256]{1,0:T(8,128)(2,1)S(1)}, bf16[512,256]{1,0:T(8,128)(2,1)S(1)}, u32[]{:S(2)}, u32[]{:S(2)}) %collective-permute-start.97) | collective-permute-done | bytes 262176 | tf_op jit(solution)/shard_map/ppermute | solution.py:39
  523.8 7.0 %collective-permute-done.102 = f32[1,4352]{1,0:T(1,128)S(1)} collective-permute-done((f32[1,4352]{1,0:T(1,128)S(1)}, f32[1,4352]{1,0:T(1,128)S(1)}, u32[]{:S(2)}, u32[]{:S(2)}) %collective-permute-start.102) | collective-permute-done | bytes 17440 | tf_op jit(solution)/shard_map/ppermute | solution.py:39
  537.5 3.5 reorder.3
  549.3 2.8 collective-permute-done.109
  (585 shorter events, 250.8 us)
Async XLA Ops:
  7.5 21.3 %collective-permute-start.1 = (bf16[272,512]{1,0:T(8,128)(2,1)}, bf16[272,512]{1,0:T(8,128)(2,1)S(1)}, u32[]{:S(2)}, u32[]{:S(2)}) collective-permute-start(bf16[272,512]{1,0:T(8,128)(2,1)} %get-tuple-element.419), channel_id=1, source_target_pairs={{0,4},{4,0},{1,5},{5,1},{2,6},{6,2},{3,7},{7,3},{8,12},{12,8},{9,1... | collective-permute-start | bytes 835592 | tf_op jit(solution)/shard_map/ppermute | solution.py:39
  11.5 17.3 %collective-permute-start.2 = (bf16[272,512]{1,0:T(8,128)(2,1)}, bf16[272,512]{1,0:T(8,128)(2,1)S(1)}, u32[]{:S(2)}, u32[]{:S(2)}) collective-permute-start(bf16[272,512]{1,0:T(8,128)(2,1)} %get-tuple-element.419), channel_id=1, source_target_pairs={{0,1},{1,0},{2,3},{3,2},{4,5},{5,4},{6,7},{7,6},{8,9},{9,8},{10,11... | collective-permute-start | bytes 835592 | tf_op jit(solution)/shard_map/ppermute | solution.py:39
  13.0 15.8 %collective-permute-start = (bf16[272,512]{1,0:T(8,128)(2,1)}, bf16[272,512]{1,0:T(8,128)(2,1)}, u32[]{:S(2)}, u32[]{:S(2)}) collective-permute-start(bf16[272,512]{1,0:T(8,128)(2,1)} %get-tuple-element.418), channel_id=1, source_target_pairs={{0,2},{2,0},{1,3},{3,1},{4,6},{6,4},{5,7},{7,5},{8,10},{10,8},{9,1... | collective-permute-start | bytes 835592 | tf_op jit(solution)/shard_map/ppermute | solution.py:39
  29.5 23.6 %collective-permute-start.6 = (bf16[128,2048]{1,0:T(8,128)(2,1)S(1)}, bf16[128,2048]{1,0:T(8,128)(2,1)S(1)}, u32[]{:S(2)}, u32[]{:S(2)}) collective-permute-start(bf16[128,2048]{1,0:T(8,128)(2,1)S(1)} %copy-done.34), channel_id=1, source_target_pairs={{0,2},{2,0},{1,3},{3,1},{4,6},{6,4},{5,7},{7,5},{8,10},{10,8},{9,1... | collective-permute-start | bytes 1572872 | tf_op jit(solution)/shard_map/ppermute | solution.py:39
  34.0 19.1 %collective-permute-start.9 = (bf16[768,256]{1,0:T(8,128)(2,1)S(1)}, bf16[768,256]{1,0:T(8,128)(2,1)S(1)}, u32[]{:S(2)}, u32[]{:S(2)}) collective-permute-start(bf16[768,256]{1,0:T(8,128)(2,1)S(1)} %constant_dynamic-slice_fusion.9.refs_0_), channel_id=1, source_target_pairs={{0,1},{1,0},{2,3},{3,2},{4,5},{5,4},{6,7},{7,6},{8,9},{9,8},{10,11... | collective-permute-start | bytes 1179656 | tf_op jit(solution)/shard_map/ppermute | solution.py:39
  68.5 16.4 %collective-permute-start.17 = (bf16[256,768]{1,0:T(8,128)(2,1)S(1)}, bf16[256,768]{1,0:T(8,128)(2,1)S(1)}, u32[]{:S(2)}, u32[]{:S(2)}) collective-permute-start(bf16[256,768]{1,0:T(8,128)(2,1)S(1)} %get-tuple-element.453), channel_id=1, source_target_pairs={{0,2},{2,0},{1,3},{3,1},{4,6},{6,4},{5,7},{7,5},{8,10},{10,8},{9,1... | collective-permute-start | bytes 1179656 | tf_op jit(solution)/shard_map/ppermute | solution.py:39
  86.2 24.8 %collective-permute-start.20 = (bf16[1024,256]{1,0:T(8,128)(2,1)S(1)}, bf16[1024,256]{1,0:T(8,128)(2,1)S(1)}, u32[]{:S(2)}, u32[]{:S(2)}) collective-permute-start(bf16[1024,256]{1,0:T(8,128)(2,1)S(1)} %get-tuple-element.461.refs_0_), channel_id=1, source_target_pairs={{0,4},{4,0},{1,5},{5,1},{2,6},{6,2},{3,7},{7,3},{8,12},{12,8},{9,1... | collective-permute-start | bytes 1572872 | tf_op jit(solution)/shard_map/ppermute | solution.py:39
  86.6 24.4 %collective-permute-start.21 = (bf16[128,2048]{1,0:T(8,128)(2,1)S(1)}, bf16[128,2048]{1,0:T(8,128)(2,1)S(1)}, u32[]{:S(2)}, u32[]{:S(2)}) collective-permute-start(bf16[128,2048]{1,0:T(8,128)(2,1)S(1)} %copy-done.42), channel_id=1, source_target_pairs={{0,16},{16,0},{1,17},{17,1},{2,18},{18,2},{3,19},{19,3},{4,20},{20... | collective-permute-start | bytes 1572872 | tf_op jit(solution)/shard_map/ppermute | solution.py:39
  87.1 18.9 %collective-permute-start.23 = (bf16[256,768]{1,0:T(8,128)(2,1)S(1)}, bf16[256,768]{1,0:T(8,128)(2,1)S(1)}, u32[]{:S(2)}, u32[]{:S(2)}) collective-permute-start(bf16[256,768]{1,0:T(8,128)(2,1)S(1)} %constant_dynamic-slice_fusion.6), channel_id=1, source_target_pairs={{0,2},{2,0},{1,3},{3,1},{4,6},{6,4},{5,7},{7,5},{8,10},{10,8},{9,1... | collective-permute-start | bytes 1179656 | tf_op jit(solution)/shard_map/ppermute | solution.py:39
  111.9 28.1 %collective-permute-start.26 = (bf16[384,768]{1,0:T(8,128)(2,1)S(1)}, bf16[384,768]{1,0:T(8,128)(2,1)S(1)}, u32[]{:S(2)}, u32[]{:S(2)}) collective-permute-start(bf16[384,768]{1,0:T(8,128)(2,1)S(1)} %pad_maximum_fusion.7), channel_id=1, source_target_pairs={{0,4},{4,0},{1,5},{5,1},{2,6},{6,2},{3,7},{7,3},{8,12},{12,8},{9,1... | collective-permute-start | bytes 1769480 | tf_op jit(solution)/shard_map/ppermute | solution.py:39
  112.0 24.0 %collective-permute-start.27 = (bf16[128,2048]{1,0:T(8,128)(2,1)S(1)}, bf16[128,2048]{1,0:T(8,128)(2,1)S(1)}, u32[]{:S(2)}, u32[]{:S(2)}) collective-permute-start(bf16[128,2048]{1,0:T(8,128)(2,1)S(1)} %copy-done.42), channel_id=1, source_target_pairs={{0,2},{2,0},{1,3},{3,1},{4,6},{6,4},{5,7},{7,5},{8,10},{10,8},{9,1... | collective-permute-start | bytes 1572872 | tf_op jit(solution)/shard_map/ppermute | solution.py:39
  140.0 15.9 %collective-permute-start.28 = (bf16[512,2048]{1,0:T(8,128)(2,1)S(1)}, bf16[512,2048]{1,0:T(8,128)(2,1)S(1)}, u32[]{:S(2)}, u32[]{:S(2)}) collective-permute-start(bf16[512,2048]{1,0:T(8,128)(2,1)S(1)} %convolution_convert_fusion), channel_id=1, source_target_pairs={{0,8},{8,0},{1,9},{9,1},{2,10},{10,2},{3,11},{11,3},{4,12},{12,4},... | collective-permute-start | bytes 6291464 | tf_op jit(solution)/shard_map/ppermute | solution.py:39
  140.0 15.8 %collective-permute-start.31 = (bf16[128,2048]{1,0:T(8,128)(2,1)S(1)}, bf16[128,2048]{1,0:T(8,128)(2,1)S(1)}, u32[]{:S(2)}, u32[]{:S(2)}) collective-permute-start(bf16[128,2048]{1,0:T(8,128)(2,1)S(1)} %collective-permute-done.27), channel_id=1, source_target_pairs={{0,16},{16,0},{1,17},{17,1},{2,18},{18,2},{3,19},{19,3},{4,20},{20... | collective-permute-start | bytes 1572872 | tf_op jit(solution)/shard_map/ppermute | solution.py:39
  172.2 24.0 %collective-permute-start.40 = (bf16[512,2048]{1,0:T(8,128)(2,1)S(1)}, bf16[512,2048]{1,0:T(8,128)(2,1)S(1)}, u32[]{:S(2)}, u32[]{:S(2)}) collective-permute-start(bf16[512,2048]{1,0:T(8,128)(2,1)S(1)} %pad_maximum_fusion.refs_0_), channel_id=1, source_target_pairs={{0,8},{8,0},{1,9},{9,1},{2,10},{10,2},{3,11},{11,3},{4,12},{12,4},... | collective-permute-start | bytes 6291464 | tf_op jit(solution)/shard_map/ppermute | solution.py:39
  172.3 23.9 %collective-permute-start.38 = (bf16[512,768]{1,0:T(8,128)(2,1)S(1)}, bf16[512,768]{1,0:T(8,128)(2,1)S(1)}, u32[]{:S(2)}, u32[]{:S(2)}) collective-permute-start(bf16[512,768]{1,0:T(8,128)(2,1)S(1)} %assemble.5.refs_1_), channel_id=1, source_target_pairs={{0,1},{1,0},{2,3},{3,2},{4,5},{5,4},{6,7},{7,6},{8,9},{9,8},{10,11... | collective-permute-start | bytes 2359304 | tf_op jit(solution)/shard_map/ppermute | solution.py:39
  173.6 20.5 %collective-permute-start.36 = (bf16[128,2048]{1,0:T(8,128)(2,1)S(1)}, bf16[128,2048]{1,0:T(8,128)(2,1)S(1)}, u32[]{:S(2)}, u32[]{:S(2)}) collective-permute-start(bf16[128,2048]{1,0:T(8,128)(2,1)S(1)} %slice.547), channel_id=1, source_target_pairs={{0,16},{16,0},{1,17},{17,1},{2,18},{18,2},{3,19},{19,3},{4,20},{20... | collective-permute-start | bytes 1572872 | tf_op jit(solution)/shard_map/ppermute | solution.py:39
  174.1 22.1 %collective-permute-start.37 = (bf16[128,2048]{1,0:T(8,128)(2,1)S(1)}, bf16[128,2048]{1,0:T(8,128)(2,1)S(1)}, u32[]{:S(2)}, u32[]{:S(2)}) collective-permute-start(bf16[128,2048]{1,0:T(8,128)(2,1)S(1)} %add_convert_fusion.8), channel_id=1, source_target_pairs={{0,2},{2,0},{1,3},{3,1},{4,6},{6,4},{5,7},{7,5},{8,10},{10,8},{9,1... | collective-permute-start | bytes 1572872 | tf_op jit(solution)/shard_map/ppermute | solution.py:39
  174.1 19.9 %collective-permute-start.39 = (bf16[256,768]{1,0:T(8,128)(2,1)S(1)}, bf16[256,768]{1,0:T(8,128)(2,1)S(1)}, u32[]{:S(2)}, u32[]{:S(2)}) collective-permute-start(bf16[256,768]{1,0:T(8,128)(2,1)S(1)} %slice.317), channel_id=1, source_target_pairs={{0,4},{4,0},{1,5},{5,1},{2,6},{6,2},{3,7},{7,3},{8,12},{12,8},{9,1... | collective-permute-start | bytes 1179656 | tf_op jit(solution)/shard_map/ppermute | solution.py:39
  196.8 21.0 %collective-permute-start.41 = (bf16[128,2048]{1,0:T(8,128)(2,1)S(1)}, bf16[128,2048]{1,0:T(8,128)(2,1)S(1)}, u32[]{:S(2)}, u32[]{:S(2)}) collective-permute-start(bf16[128,2048]{1,0:T(8,128)(2,1)S(1)} %multiply_convert_fusion.4), channel_id=1, source_target_pairs={{0,16},{16,0},{1,17},{17,1},{2,18},{18,2},{3,19},{19,3},{4,20},{20... | collective-permute-start | bytes 1572872 | tf_op jit(solution)/shard_map/ppermute | solution.py:39
  198.4 21.1 %collective-permute-start.42 = (bf16[128,2048]{1,0:T(8,128)(2,1)S(1)}, bf16[128,2048]{1,0:T(8,128)(2,1)S(1)}, u32[]{:S(2)}, u32[]{:S(2)}) collective-permute-start(bf16[128,2048]{1,0:T(8,128)(2,1)S(1)} %multiply_convert_fusion.4), channel_id=1, source_target_pairs={{0,2},{2,0},{1,3},{3,1},{4,6},{6,4},{5,7},{7,5},{8,10},{10,8},{9,1... | collective-permute-start | bytes 1572872 | tf_op jit(solution)/shard_map/ppermute | solution.py:39
  199.7 17.5 %collective-permute-start.44 = (bf16[256,768]{1,0:T(8,128)(2,1)S(1)}, bf16[256,768]{1,0:T(8,128)(2,1)S(1)}, u32[]{:S(2)}, u32[]{:S(2)}) collective-permute-start(bf16[256,768]{1,0:T(8,128)(2,1)S(1)} %constant_dynamic-update-slice_fusion.11.refs_1_), channel_id=1, source_target_pairs={{0,1},{1,0},{2,3},{3,2},{4,5},{5,4},{6,7},{7,6},{8,9},{9,8},{10,11... | collective-permute-start | bytes 1179656 | tf_op jit(solution)/shard_map/ppermute | solution.py:39
  201.0 16.8 %collective-permute-start.45 = (bf16[768,256]{1,0:T(8,128)(2,1)S(1)}, bf16[768,256]{1,0:T(8,128)(2,1)S(1)}, u32[]{:S(2)}, u32[]{:S(2)}) collective-permute-start(bf16[768,256]{1,0:T(8,128)(2,1)S(1)} %constant_dynamic-slice_fusion.9.refs_0_), channel_id=1, source_target_pairs={{0,4},{4,0},{1,5},{5,1},{2,6},{6,2},{3,7},{7,3},{8,12},{12,8},{9,1... | collective-permute-start | bytes 1179656 | tf_op jit(solution)/shard_map/ppermute | solution.py:39
  231.5 16.0 %collective-permute-start.50 = (bf16[512,2048]{1,0:T(8,128)(2,1)S(1)}, bf16[512,2048]{1,0:T(8,128)(2,1)S(1)}, u32[]{:S(2)}, u32[]{:S(2)}) collective-permute-start(bf16[512,2048]{1,0:T(8,128)(2,1)S(1)} %get-tuple-element.550), channel_id=1, source_target_pairs={{0,8},{8,0},{1,9},{9,1},{2,10},{10,2},{3,11},{11,3},{4,12},{12,4},... | collective-permute-start | bytes 6291464 | tf_op jit(solution)/shard_map/ppermute | solution.py:39
  231.6 15.9 %collective-permute-start.52 = (bf16[768,256]{1,0:T(8,128)(2,1)S(1)}, bf16[768,256]{1,0:T(8,128)(2,1)S(1)}, u32[]{:S(2)}, u32[]{:S(2)}) collective-permute-start(bf16[768,256]{1,0:T(8,128)(2,1)S(1)} %collective-permute-done.45.refs_2_), channel_id=1, source_target_pairs={{0,1},{1,0},{2,3},{3,2},{4,5},{5,4},{6,7},{7,6},{8,9},{9,8},{10,11... | collective-permute-start | bytes 1179656 | tf_op jit(solution)/shard_map/ppermute | solution.py:39
  261.2 18.6 %collective-permute-start.55 = (bf16[768,512]{1,0:T(8,128)(2,1)}, bf16[768,512]{1,0:T(8,128)(2,1)}, u32[]{:S(2)}, u32[]{:S(2)}) collective-permute-start(bf16[768,512]{1,0:T(8,128)(2,1)} %convolution_convert_fusion.8), channel_id=1, source_target_pairs={{0,1},{1,0},{2,3},{3,2},{4,5},{5,4},{6,7},{7,6},{8,9},{9,8},{10,11... | collective-permute-start | bytes 2359304 | tf_op jit(solution)/shard_map/ppermute | solution.py:39
  295.6 19.3 %collective-permute-start.60 = (bf16[512,768]{1,0:T(8,128)(2,1)S(1)}, bf16[512,768]{1,0:T(8,128)(2,1)S(1)}, u32[]{:S(2)}, u32[]{:S(2)}) collective-permute-start(bf16[512,768]{1,0:T(8,128)(2,1)S(1)} %convolution_convert_fusion.7), channel_id=1, source_target_pairs={{0,1},{1,0},{2,3},{3,2},{4,5},{5,4},{6,7},{7,6},{8,9},{9,8},{10,11... | collective-permute-start | bytes 2359304 | tf_op jit(solution)/shard_map/ppermute | solution.py:39
  297.5 16.3 %collective-permute-start.58 = (bf16[128,2048]{1,0:T(8,128)(2,1)S(1)}, bf16[128,2048]{1,0:T(8,128)(2,1)S(1)}, u32[]{:S(2)}, u32[]{:S(2)}) collective-permute-start(bf16[128,2048]{1,0:T(8,128)(2,1)S(1)} %slice.546), channel_id=1, source_target_pairs={{0,16},{16,0},{1,17},{17,1},{2,18},{18,2},{3,19},{19,3},{4,20},{20... | collective-permute-start | bytes 1572872 | tf_op jit(solution)/shard_map/ppermute | solution.py:39
  315.2 23.6 %collective-permute-start.64 = (bf16[512,768]{1,0:T(8,128)(2,1)S(1)}, bf16[512,768]{1,0:T(8,128)(2,1)S(1)}, u32[]{:S(2)}, u32[]{:S(2)}) collective-permute-start(bf16[512,768]{1,0:T(8,128)(2,1)S(1)} %convolution_convert_fusion.5), channel_id=1, source_target_pairs={{0,1},{1,0},{2,3},{3,2},{4,5},{5,4},{6,7},{7,6},{8,9},{9,8},{10,11... | collective-permute-start | bytes 2359304 | tf_op jit(solution)/shard_map/ppermute | solution.py:39
  317.2 19.4 %collective-permute-start.61 = (bf16[128,2048]{1,0:T(8,128)(2,1)S(1)}, bf16[128,2048]{1,0:T(8,128)(2,1)S(1)}, u32[]{:S(2)}, u32[]{:S(2)}) collective-permute-start(bf16[128,2048]{1,0:T(8,128)(2,1)S(1)} %slice.545), channel_id=1, source_target_pairs={{0,16},{16,0},{1,17},{17,1},{2,18},{18,2},{3,19},{19,3},{4,20},{20... | collective-permute-start | bytes 1572872 | tf_op jit(solution)/shard_map/ppermute | solution.py:39
  318.8 20.0 %collective-permute-start.62 = (bf16[128,2048]{1,0:T(8,128)(2,1)S(1)}, bf16[128,2048]{1,0:T(8,128)(2,1)S(1)}, u32[]{:S(2)}, u32[]{:S(2)}) collective-permute-start(bf16[128,2048]{1,0:T(8,128)(2,1)S(1)} %add_convert_fusion.7), channel_id=1, source_target_pairs={{0,2},{2,0},{1,3},{3,1},{4,6},{6,4},{5,7},{7,5},{8,10},{10,8},{9,1... | collective-permute-start | bytes 1572872 | tf_op jit(solution)/shard_map/ppermute | solution.py:39
  318.8 17.8 %collective-permute-start.63 = (bf16[352,512]{1,0:T(8,128)(2,1)S(1)}, bf16[352,512]{1,0:T(8,128)(2,1)S(1)}, u32[]{:S(2)}, u32[]{:S(2)}) collective-permute-start(bf16[352,512]{1,0:T(8,128)(2,1)S(1)} %slice.338), channel_id=1, source_target_pairs={{0,4},{4,0},{1,5},{5,1},{2,6},{6,2},{3,7},{7,3},{8,12},{12,8},{9,1... | collective-permute-start | bytes 1081352 | tf_op jit(solution)/shard_map/ppermute | solution.py:39
  340.8 20.3 %collective-permute-start.65 = (bf16[128,2048]{1,0:T(8,128)(2,1)S(1)}, bf16[128,2048]{1,0:T(8,128)(2,1)S(1)}, u32[]{:S(2)}, u32[]{:S(2)}) collective-permute-start(bf16[128,2048]{1,0:T(8,128)(2,1)S(1)} %get-tuple-element.632), channel_id=1, source_target_pairs={{0,16},{16,0},{1,17},{17,1},{2,18},{18,2},{3,19},{19,3},{4,20},{20... | collective-permute-start | bytes 1572872 | tf_op jit(solution)/shard_map/ppermute | solution.py:39
  341.6 21.0 %collective-permute-start.66 = (bf16[128,2048]{1,0:T(8,128)(2,1)S(1)}, bf16[128,2048]{1,0:T(8,128)(2,1)S(1)}, u32[]{:S(2)}, u32[]{:S(2)}) collective-permute-start(bf16[128,2048]{1,0:T(8,128)(2,1)S(1)} %get-tuple-element.632), channel_id=1, source_target_pairs={{0,2},{2,0},{1,3},{3,1},{4,6},{6,4},{5,7},{7,5},{8,10},{10,8},{9,1... | collective-permute-start | bytes 1572872 | tf_op jit(solution)/shard_map/ppermute | solution.py:39
  342.7 18.3 %collective-permute-start.67 = (bf16[256,768]{1,0:T(8,128)(2,1)S(1)}, bf16[256,768]{1,0:T(8,128)(2,1)S(1)}, u32[]{:S(2)}, u32[]{:S(2)}) collective-permute-start(bf16[256,768]{1,0:T(8,128)(2,1)S(1)} %slice.341), channel_id=1, source_target_pairs={{0,4},{4,0},{1,5},{5,1},{2,6},{6,2},{3,7},{7,3},{8,12},{12,8},{9,1... | collective-permute-start | bytes 1179656 | tf_op jit(solution)/shard_map/ppermute | solution.py:39
  344.5 18.2 %collective-permute-start.68 = (bf16[512,768]{1,0:T(8,128)(2,1)S(1)}, bf16[512,768]{1,0:T(8,128)(2,1)S(1)}, u32[]{:S(2)}, u32[]{:S(2)}) collective-permute-start(bf16[512,768]{1,0:T(8,128)(2,1)S(1)} %convolution_convert_fusion.4), channel_id=1, source_target_pairs={{0,1},{1,0},{2,3},{3,2},{4,5},{5,4},{6,7},{7,6},{8,9},{9,8},{10,11... | collective-permute-start | bytes 2359304 | tf_op jit(solution)/shard_map/ppermute | solution.py:39
  385.9 16.8 %collective-permute-start.76 = (bf16[192,768]{1,0:T(8,128)(2,1)S(1)}, bf16[192,768]{1,0:T(8,128)(2,1)S(1)}, u32[]{:S(2)}, u32[]{:S(2)}) collective-permute-start(bf16[192,768]{1,0:T(8,128)(2,1)S(1)} %pad_maximum_fusion.15), channel_id=1, source_target_pairs={{0,4},{4,0},{1,5},{5,1},{2,6},{6,2},{3,7},{7,3},{8,12},{12,8},{9,1... | collective-permute-start | bytes 884744 | tf_op jit(solution)/shard_map/ppermute | solution.py:39
  385.9 16.7 %collective-permute-start.77 = (bf16[256,768]{1,0:T(8,128)(2,1)S(1)}, bf16[256,768]{1,0:T(8,128)(2,1)S(1)}, u32[]{:S(2)}, u32[]{:S(2)}) collective-permute-start(bf16[256,768]{1,0:T(8,128)(2,1)S(1)} %get-tuple-element.671), channel_id=1, source_target_pairs={{0,1},{1,0},{2,3},{3,2},{4,5},{5,4},{6,7},{7,6},{8,9},{9,8},{10,11... | collective-permute-start | bytes 1179656 | tf_op jit(solution)/shard_map/ppermute | solution.py:39
  403.6 16.9 %collective-permute-start.80 = (bf16[1024,256]{1,0:T(8,128)(2,1)S(1)}, bf16[1024,256]{1,0:T(8,128)(2,1)S(1)}, u32[]{:S(2)}, u32[]{:S(2)}) collective-permute-start(bf16[1024,256]{1,0:T(8,128)(2,1)S(1)} %get-tuple-element.682), channel_id=1, source_target_pairs={{0,1},{1,0},{2,3},{3,2},{4,5},{5,4},{6,7},{7,6},{8,9},{9,8},{10,11... | collective-permute-start | bytes 1572872 | tf_op jit(solution)/shard_map/ppermute | solution.py:39
  422.1 25.2 %collective-permute-start.84 = (bf16[1024,256]{1,0:T(8,128)(2,1)S(1)}, bf16[1024,256]{1,0:T(8,128)(2,1)S(1)}, u32[]{:S(2)}, u32[]{:S(2)}) collective-permute-start(bf16[1024,256]{1,0:T(8,128)(2,1)S(1)} %add_convert_fusion.6), channel_id=1, source_target_pairs={{0,4},{4,0},{1,5},{5,1},{2,6},{6,2},{3,7},{7,3},{8,12},{12,8},{9,1... | collective-permute-start | bytes 1572872 | tf_op jit(solution)/shard_map/ppermute | solution.py:39
  425.5 21.8 %collective-permute-start.85 = (bf16[128,2048]{1,0:T(8,128)(2,1)S(1)}, bf16[128,2048]{1,0:T(8,128)(2,1)S(1)}, u32[]{:S(2)}, u32[]{:S(2)}) collective-permute-start(bf16[128,2048]{1,0:T(8,128)(2,1)S(1)} %get-tuple-element.697), channel_id=1, source_target_pairs={{0,16},{16,0},{1,17},{17,1},{2,18},{18,2},{3,19},{19,3},{4,20},{20... | collective-permute-start | bytes 1572872 | tf_op jit(solution)/shard_map/ppermute | solution.py:39
  426.6 22.1 %collective-permute-start.86 = (bf16[128,2048]{1,0:T(8,128)(2,1)S(1)}, bf16[128,2048]{1,0:T(8,128)(2,1)S(1)}, u32[]{:S(2)}, u32[]{:S(2)}) collective-permute-start(bf16[128,2048]{1,0:T(8,128)(2,1)S(1)} %add_convert_fusion.5), channel_id=1, source_target_pairs={{0,2},{2,0},{1,3},{3,1},{4,6},{6,4},{5,7},{7,5},{8,10},{10,8},{9,1... | collective-permute-start | bytes 1572872 | tf_op jit(solution)/shard_map/ppermute | solution.py:39
  471.1 21.1 %collective-permute-start.91 = (bf16[512,2048]{1,0:T(8,128)(2,1)}, bf16[512,2048]{1,0:T(8,128)(2,1)}, u32[]{:S(2)}, u32[]{:S(2)}) collective-permute-start(bf16[512,2048]{1,0:T(8,128)(2,1)} %convolution_convert_fusion.1), channel_id=1, source_target_pairs={{0,8},{8,0},{1,9},{9,1},{2,10},{10,2},{3,11},{11,3},{4,12},{12,4},... | collective-permute-start | bytes 6291464 | tf_op jit(solution)/shard_map/ppermute | solution.py:39
  471.1 18.4 %collective-permute-start.95 = (bf16[768,256]{1,0:T(8,128)(2,1)}, bf16[768,256]{1,0:T(8,128)(2,1)}, u32[]{:S(2)}, u32[]{:S(2)}) collective-permute-start(bf16[768,256]{1,0:T(8,128)(2,1)} %select_convert_fusion.1), channel_id=1, source_target_pairs={{0,2},{2,0},{1,3},{3,1},{4,6},{6,4},{5,7},{7,5},{8,10},{10,8},{9,1... | collective-permute-start | bytes 1179656 | tf_op jit(solution)/shard_map/ppermute | solution.py:39
  511.0 19.8 %collective-permute-start.98 = (bf16[128,2048]{1,0:T(8,128)(2,1)S(1)}, bf16[128,2048]{1,0:T(8,128)(2,1)S(1)}, u32[]{:S(2)}, u32[]{:S(2)}) collective-permute-start(bf16[128,2048]{1,0:T(8,128)(2,1)S(1)} %slice.543), channel_id=1, source_target_pairs={{0,16},{16,0},{1,17},{17,1},{2,18},{18,2},{3,19},{19,3},{4,20},{20... | collective-permute-start | bytes 1572872 | tf_op jit(solution)/shard_map/ppermute | solution.py:39
  511.8 19.5 %collective-permute-start.99 = (bf16[128,2048]{1,0:T(8,128)(2,1)S(1)}, bf16[128,2048]{1,0:T(8,128)(2,1)S(1)}, u32[]{:S(2)}, u32[]{:S(2)}) collective-permute-start(bf16[128,2048]{1,0:T(8,128)(2,1)S(1)} %add_convert_fusion.3), channel_id=1, source_target_pairs={{0,2},{2,0},{1,3},{3,1},{4,6},{6,4},{5,7},{7,5},{8,10},{10,8},{9,1... | collective-permute-start | bytes 1572872 | tf_op jit(solution)/shard_map/ppermute | solution.py:39
  511.8 19.5 %collective-permute-start.100 = (bf16[512,512]{1,0:T(8,128)(2,1)S(1)}, bf16[512,512]{1,0:T(8,128)(2,1)S(1)}, u32[]{:S(2)}, u32[]{:S(2)}) collective-permute-start(bf16[512,512]{1,0:T(8,128)(2,1)S(1)} %copy-done.68), channel_id=1, source_target_pairs={{0,1},{1,0},{2,3},{3,2},{4,5},{5,4},{6,7},{7,6},{8,9},{9,8},{10,11... | collective-permute-start | bytes 1572872 | tf_op jit(solution)/shard_map/ppermute | solution.py:39
  513.2 17.7 %collective-permute-start.103 = (bf16[256,512]{1,0:T(8,128)(2,1)S(1)}, bf16[256,512]{1,0:T(8,128)(2,1)S(1)}, u32[]{:S(2)}, u32[]{:S(2)}) collective-permute-start(bf16[256,512]{1,0:T(8,128)(2,1)S(1)} %fusion.6), channel_id=1, source_target_pairs={{0,4},{4,0},{1,5},{5,1},{2,6},{6,2},{3,7},{7,3},{8,12},{12,8},{9,1... | collective-permute-start | bytes 786440 | tf_op jit(solution)/shard_map/ppermute | solution.py:39
  534.7 18.2 %collective-permute-start.110 = (bf16[256,768]{1,0:T(8,128)(2,1)S(1)}, bf16[256,768]{1,0:T(8,128)(2,1)S(1)}, u32[]{:S(2)}, u32[]{:S(2)}) collective-permute-start(bf16[256,768]{1,0:T(8,128)(2,1)S(1)} %select_convert_fusion), channel_id=1, source_target_pairs={{0,2},{2,0},{1,3},{3,1},{4,6},{6,4},{5,7},{7,5},{8,10},{10,8},{9,1... | collective-permute-start | bytes 1179656 | tf_op jit(solution)/shard_map/ppermute | solution.py:39
  (145 other events, 1557.6 us)
where the time goes:
time: 563 us; the launch traced here: 555 us
  waiting for transfers between devices  268 us (48%)
  starting transfers between devices  122 us (22%)
  matrix products  54.9 us (10%)
  Pallas kernels  43.2 us (8%)
  other arithmetic  42.1 us (7%)
  local copies, waits for them, and re-layouts  20.8 us (4%)
    ppermute x111, waiting for transfers between devices, swap(): return lax.ppermute(value, axis, SWAP)  268 us
    ppermute x111, starting transfers between devices, swap(): return lax.ppermute(value, axis, SWAP)  122 us
    dot_general x22, matrix products, contract_rows(): lax.dot_general(left, right, PAIRS_OF_ROWS, preferred_element_type=F32)  27.9 us
    dot_general x7, matrix products, matmul(): return jnp.dot(left, right, preferred_element_type=F32)  14.6 us
    dot_general x5, matrix products, contract_cols(): lax.dot_general(left, right, PAIRS_OF_COLS, preferred_element_type=F32)  12.3 us
    unnamed x180, local copies, waits for them, and re-layouts  11.3 us
  transfers between devices with their start and end apart: 111, of which 57 were waited for; matrix products, arithmetic and copies ran while one was open for 15% of the time, Pallas kernels for 7%

commit v1 on v0

--- a/solution.py
+++ b/solution.py
@@ -769,10 +769,7 @@
         ],
         0,
     )
-    token, (mlp_theirs, up_cols, down_zf1, down_xzk, down_xzf0) = meet(
-        token, (mlp_theirs, up_cols, down_zf1, down_xzk, down_xzf0)
-    )
-    (down_xzf1,) = trade(token, [(down_zf1, "x")])
+    token, (mlp_theirs, up_cols) = meet(token, (mlp_theirs, up_cols))
     mlp_rows = jnp.concatenate([mlp_mine, mlp_theirs], axis=0)
     gate_act = matmul(mlp_rows, gate_cols)
     token, (gate_act, up_cols, mlp_rows) = meet(token, (gate_act, up_cols, mlp_rows))
@@ -784,10 +781,13 @@
     up_act = matmul(mlp_rows, up_cols)
     hidden = (silu * up_act).astype(BF16)
     gate_slope = (up_act * slope).astype(BF16)
+    token, (hidden, gate_slope, up_slope, down_zf1, down_xzk, down_xzf0) = meet(
+        token, (hidden, gate_slope, up_slope, down_zf1, down_xzk, down_xzf0)
+    )
+    (down_xzf1,) = trade(token, [(down_zf1, "x")])
     down_zf = jnp.concatenate([down_zf0, down_zf1], axis=0)
-    token, (hidden, gate_slope, up_slope, grad_rows, down_xzf1, down_zf) = meet(
-        token, (hidden, gate_slope, up_slope, grad_rows, down_xzf1, down_zf)
-    )
+    down_3 = contract_rows(hidden, grad_rows[:, 3 * quarter :]).astype(BF16)
+    token, (down_3, down_xzf1, down_zf) = meet(token, (down_3, down_xzf1, down_zf))
     down_xzf = jnp.concatenate([down_xzf0, down_xzf1], axis=0)
 
     def columns_of(value, piece):
@@ -807,8 +807,7 @@
         ],
         1,
     )
-    down_3 = contract_rows(hidden, columns_of(grad_rows, 3)).astype(BF16)
-    token, (down_3, down_cols) = meet(token, (down_3, down_cols))
+    token, (down_cols,) = meet(token, (down_cols,))
     (down_3,) = trade(token, [(down_3, "x")])
     hidden_grad = contract_cols(grad_rows, down_cols)
     gate_low = (hidden_grad * gate_slope.astype(F32)).astype(BF16)

time: 563 us -> 556 us (0.988)
  waiting for transfers between devices: 268 us -> 252 us
  Pallas kernels: 43.2 us -> 55.4 us
    ppermute x111, waiting for transfers between devices: 268 us -> 252 us  [swap(): return lax.ppermute(value, axis, SWAP)]
    pallas_call x2, Pallas kernels: 11 us -> 18.1 us  [attend_back(): pl.pallas_call(functools.partial(attend_back_kernel, parts=parts, first=f...]
  transfers between devices with their start and end apart: 111 -> 111, of which waited for: 57 -> 55; matrix products, arithmetic and copies ran while one was open for 15% -> 16% of each run, Pallas kernels for 7% -> 9%
where the time goes in v1:
time: 556 us; the launch traced here: 545 us
  waiting for transfers between devices  252 us (45%)
  starting transfers between devices  117 us (21%)
  Pallas kernels  55.4 us (10%)
  matrix products  54.9 us (10%)
  other arithmetic  42.1 us (8%)
  local copies, waits for them, and re-layouts  20.9 us (4%)
    ppermute x111, waiting for transfers between devices, swap(): return lax.ppermute(value, axis, SWAP)  252 us
    ppermute x111, starting transfers between devices, swap(): return lax.ppermute(value, axis, SWAP)  117 us
    dot_general x22, matrix products, contract_rows(): lax.dot_general(left, right, PAIRS_OF_ROWS, preferred_element_type=F32)  27.9 us
    pallas_call x2, Pallas kernels, attend_back(): pl.pallas_call(functools.partial(attend_back_kernel, parts=parts, first=f...  18.1 us
    dot_general x7, matrix products, matmul(): return jnp.dot(left, right, preferred_element_type=F32)  14.7 us
    pallas_call x2, Pallas kernels, attend(): pl.pallas_call(functools.partial(attend_kernel, parts=parts, first=first,...  12.6 us
    dot_general x5, matrix products, contract_cols(): lax.dot_general(left, right, PAIRS_OF_COLS, preferred_element_type=F32)  12.3 us
    unnamed x180, local copies, waits for them, and re-layouts  11.6 us
  transfers between devices with their start and end apart: 111, of which 55 were waited for; matrix products, arithmetic and copies ran while one was open for 16% of the time, Pallas kernels for 9%

profile of v1, /device:TPU:0, one launch (start us, length us, event | category | flops | bytes accessed | tf_op | source)
XLA Modules:
  0.0 545.4 jit_solution(15562670681758962987)
XLA Ops:
  4.2 3.3 prologue.1
  7.5 4.0 collective-permute-start.1
  23.8 5.0 collective-permute-done.4
  39.6 3.3 collective-permute-done.5
  43.0 4.5 collective-permute-done.8
  47.5 5.6 %collective-permute-done.9.refs_4_ = bf16[768,256]{1,0:T(8,128)(2,1)S(1)} collective-permute-done((bf16[768,256]{1,0:T(8,128)(2,1)S(1)}, bf16[768,256]{1,0:T(8,128)(2,1)S(1)}, u32[]{:S(2)}, u32[]{:S(2)}) %collective-permute-start.9) | collective-permute-done | bytes 393248 | tf_op jit(solution)/shard_map/ppermute | solution.py:39
  59.8 3.0 collective-permute-done.12
  64.3 3.2 collective-permute-done.14
  80.5 4.4 collective-permute-done.17
  89.2 9.3 %collective-permute-done.19.refs_1_ = bf16[1024,256]{1,0:T(8,128)(2,1)S(1)} collective-permute-done((bf16[1024,256]{1,0:T(8,128)(2,1)S(1)}, bf16[1024,256]{1,0:T(8,128)(2,1)S(1)}, u32[]{:S(2)}, u32[]{:S(2)}) %collective-permute-start.19) | collective-permute-done | bytes 524320 | tf_op jit(solution)/shard_map/ppermute | solution.py:39
  100.1 5.4 attend.2.refs_2_
  106.1 4.9 collective-permute-done.20.refs_0_
  114.8 10.1 %collective-permute-done.24.refs_1_ = bf16[1024,256]{1,0:T(8,128)(2,1)S(1)} collective-permute-done((bf16[1024,256]{1,0:T(8,128)(2,1)S(1)}, bf16[1024,256]{1,0:T(8,128)(2,1)S(1)}, u32[]{:S(2)}, u32[]{:S(2)}) %collective-permute-start.24) | collective-permute-done | bytes 524320 | tf_op jit(solution)/shard_map/ppermute | solution.py:39
  125.9 7.2 %attend.3 = (bf16[1024,256]{1,0:T(8,128)(2,1)S(1)}, f32[8,2,128]{2,1,0:T(2,128)S(1)}) custom-call(s32[32]{0:T(128)S(1)} %broadcast_add_fusion.off_ref, s32[8]{0:T(128)S(1)} %get-tuple-element.834.tile_ref, s32[8]{0:T(128)S(1)} %and_select_fusion.low_ref, bf16[1024,256]{1,0:T(8,128)(2,1)S(1)} %get-tuple-element.462.q_ref, ...), custom_call_target="tpu_custom_call" | custom-call | flops 1000 | bytes 1000 | tf_op jit(solution)/shard_map/attend/pallas_call | solution.py:195
  136.0 4.0 collective-permute-done.26
  144.9 8.8 %collective-permute-done.29 = bf16[96,768]{1,0:T(8,128)(2,1)S(1)} collective-permute-done((bf16[96,768]{1,0:T(8,128)(2,1)S(1)}, bf16[96,768]{1,0:T(8,128)(2,1)S(1)}, u32[]{:S(2)}, u32[]{:S(2)}) %collective-permute-start.29) | collective-permute-done | bytes 147488 | tf_op jit(solution)/shard_map/ppermute | solution.py:39
  160.9 11.1 %collective-permute-done.35 = bf16[160,768]{1,0:T(8,128)(2,1)S(1)} collective-permute-done((bf16[160,768]{1,0:T(8,128)(2,1)S(1)}, bf16[160,768]{1,0:T(8,128)(2,1)S(1)}, u32[]{:S(2)}, u32[]{:S(2)}) %collective-permute-start.35) | collective-permute-done | bytes 245792 | tf_op jit(solution)/shard_map/ppermute | solution.py:39
  176.4 17.6 %collective-permute-done.39.refs_2_ = bf16[256,768]{1,0:T(8,128)(2,1)S(1)} collective-permute-done((bf16[256,768]{1,0:T(8,128)(2,1)S(1)}, bf16[256,768]{1,0:T(8,128)(2,1)S(1)}, u32[]{:S(2)}, u32[]{:S(2)}) %collective-permute-start.39) | collective-permute-done | bytes 393248 | tf_op jit(solution)/shard_map/ppermute | solution.py:39
  203.4 7.7 %collective-permute-done.43.refs_5_ = bf16[768,256]{1,0:T(8,128)(2,1)S(1)} collective-permute-done((bf16[768,256]{1,0:T(8,128)(2,1)S(1)}, bf16[768,256]{1,0:T(8,128)(2,1)S(1)}, u32[]{:S(2)}, u32[]{:S(2)}) %collective-permute-start.43) | collective-permute-done | bytes 393248 | tf_op jit(solution)/shard_map/ppermute | solution.py:39
  211.0 6.2 %collective-permute-done.44.refs_5_ = bf16[256,768]{1,0:T(8,128)(2,1)S(1)} collective-permute-done((bf16[256,768]{1,0:T(8,128)(2,1)S(1)}, bf16[256,768]{1,0:T(8,128)(2,1)S(1)}, u32[]{:S(2)}, u32[]{:S(2)}) %collective-permute-start.44) | collective-permute-done | bytes 393248 | tf_op jit(solution)/shard_map/ppermute | solution.py:39
  225.2 6.2 %collective-permute-done.48 = bf16[400,256]{1,0:T(8,128)(2,1)S(1)} collective-permute-done((bf16[400,256]{1,0:T(8,128)(2,1)S(1)}, bf16[400,256]{1,0:T(8,128)(2,1)S(1)}, u32[]{:S(2)}, u32[]{:S(2)}) %collective-permute-start.48) | collective-permute-done | bytes 204832 | tf_op jit(solution)/shard_map/ppermute | solution.py:39
  235.9 3.4 fusion.81
  240.6 3.9 multiply_convert_fusion.2
  244.5 4.1 collective-permute-done.53
  251.3 3.2 collective-permute-done.54
  255.9 4.9 multiply_convert_fusion
  260.8 10.8 %two_terms.1 = (f32[512,2048]{1,0:T(8,128)}, bf16[512,2048]{1,0:T(8,128)(2,1)}) custom-call(bf16[1024,768]{1,0:T(8,128)(2,1)} %get-tuple-element.652.left_ref, bf16[1024,768]{1,0:T(8,128)(2,1)} %get-tuple-element.780.right_ref, bf16[2048,768]{1,0:T(8,128)(2,1)} %copy-done.2, bf16[2048,768]{1,0:T(8,128)(2,1)} %copy-done.3), custom_call_target="tpu_custom_call" | custom-call | flops 1000 | bytes 1000 | tf_op jit(solution)/shard_map/two_terms/pallas_call | solution.py:384
  273.3 2.8 fusion.27
  281.6 6.5 %collective-permute-done.57 = bf16[144,512]{1,0:T(8,128)(2,1)S(1)} collective-permute-done((bf16[144,512]{1,0:T(8,128)(2,1)S(1)}, bf16[144,512]{1,0:T(8,128)(2,1)S(1)}, u32[]{:S(2)}, u32[]{:S(2)}) %collective-permute-start.57) | collective-permute-done | bytes 147488 | tf_op jit(solution)/shard_map/ppermute | solution.py:39
  294.9 12.4 %collective-permute-done.59 = bf16[272,512]{1,0:T(8,128)(2,1)S(1)} collective-permute-done((bf16[272,512]{1,0:T(8,128)(2,1)S(1)}, bf16[272,512]{1,0:T(8,128)(2,1)S(1)}, u32[]{:S(2)}, u32[]{:S(2)}) %collective-permute-start.59) | collective-permute-done | bytes 278560 | tf_op jit(solution)/shard_map/ppermute | solution.py:39
  315.7 14.3 %collective-permute-done.63 = bf16[352,512]{1,0:T(8,128)(2,1)S(1)} collective-permute-done((bf16[352,512]{1,0:T(8,128)(2,1)S(1)}, bf16[352,512]{1,0:T(8,128)(2,1)S(1)}, u32[]{:S(2)}, u32[]{:S(2)}) %collective-permute-start.63) | collective-permute-done | bytes 360480 | tf_op jit(solution)/shard_map/ppermute | solution.py:39
  342.0 12.5 %collective-permute-done.67 = bf16[256,768]{1,0:T(8,128)(2,1)S(1)} collective-permute-done((bf16[256,768]{1,0:T(8,128)(2,1)S(1)}, bf16[256,768]{1,0:T(8,128)(2,1)S(1)}, u32[]{:S(2)}, u32[]{:S(2)}) %collective-permute-start.67) | collective-permute-done | bytes 393248 | tf_op jit(solution)/shard_map/ppermute | solution.py:39
  364.0 4.1 collective-permute-done.71
  374.2 5.1 collective-permute-done.74
  382.4 10.0 %attend_back.2 = (f32[1024,256]{1,0:T(8,128)S(1)}, bf16[1024,256]{1,0:T(8,128)(2,1)S(1)}, bf16[1024,256]{1,0:T(8,128)(2,1)S(1)}) custom-call(s32[32]{0:T(128)S(1)} %broadcast_add_fusion.off_ref, s32[8]{0:T(128)S(1)} %get-tuple-element.834.tile_ref, s32[8]{0:T(128)S(1)} %and_select_fusion.low_ref, bf16[1024,256]{1,0:T(8,128)(2,1)S(1)} %get-tuple-element.462.q_ref, ...), custom_call_target="tpu_custom_call" | custom-call | flops 1000 | bytes 1000 | tf_op jit(solution)/shard_map/attend_back/pallas_call | solution.py:213
  392.4 3.7 collective-permute-done.78
  401.8 8.1 %attend_back.3 = (bf16[1024,256]{1,0:T(8,128)(2,1)S(1)}, bf16[1024,256]{1,0:T(8,128)(2,1)S(1)}, bf16[1024,256]{1,0:T(8,128)(2,1)S(1)}) custom-call(s32[32]{0:T(128)S(1)} %broadcast_add_fusion.1.off_ref, s32[8]{0:T(128)S(1)} %get-tuple-element.834.tile_ref, s32[8]{0:T(128)S(1)} %and_select_fusion.low_ref, bf16[1024,256]{1,0:T(8,128)(2,1)S(1)} %get-tuple-element.462.q_ref, ...), custom_call_target="tpu_custom_call" | custom-call | flops 1000 | bytes 1000 | tf_op jit(solution)/shard_map/attend_back/pallas_call | solution.py:213
  409.9 4.0 collective-permute-done.81
  418.9 8.4 %collective-permute-done.83 = bf16[1024,256]{1,0:T(8,128)(2,1)S(1)} collective-permute-done((bf16[1024,256]{1,0:T(8,128)(2,1)S(1)}, bf16[1024,256]{1,0:T(8,128)(2,1)S(1)}, u32[]{:S(2)}, u32[]{:S(2)}) %collective-permute-start.83) | collective-permute-done | bytes 524320 | tf_op jit(solution)/shard_map/ppermute | solution.py:39
  450.1 4.3 collective-permute-done.87
  455.2 3.7 collective-permute-done.89
  469.3 3.2 fusion.47
  477.1 3.1 collective-permute-done.95
  481.4 3.6 convert_add_fusion
  493.8 6.9 %collective-permute-done.97 = bf16[512,256]{1,0:T(8,128)(2,1)S(1)} collective-permute-done((bf16[512,256]{1,0:T(8,128)(2,1)S(1)}, bf16[512,256]{1,0:T(8,128)(2,1)S(1)}, u32[]{:S(2)}, u32[]{:S(2)}) %collective-permute-start.97) | collective-permute-done | bytes 262176 | tf_op jit(solution)/shard_map/ppermute | solution.py:39
  513.9 7.1 %collective-permute-done.102 = f32[1,4352]{1,0:T(1,128)S(1)} collective-permute-done((f32[1,4352]{1,0:T(1,128)S(1)}, f32[1,4352]{1,0:T(1,128)S(1)}, u32[]{:S(2)}, u32[]{:S(2)}) %collective-permute-start.102) | collective-permute-done | bytes 17440 | tf_op jit(solution)/shard_map/ppermute | solution.py:39
  527.8 3.5 reorder.3
  539.0 3.9 collective-permute-done.109
  (585 shorter events, 245.7 us)
Async XLA Ops:
  7.5 21.3 %collective-permute-start.1 = (bf16[272,512]{1,0:T(8,128)(2,1)}, bf16[272,512]{1,0:T(8,128)(2,1)S(1)}, u32[]{:S(2)}, u32[]{:S(2)}) collective-permute-start(bf16[272,512]{1,0:T(8,128)(2,1)} %get-tuple-element.419), channel_id=1, source_target_pairs={{0,4},{4,0},{1,5},{5,1},{2,6},{6,2},{3,7},{7,3},{8,12},{12,8},{9,1... | collective-permute-start | bytes 835592 | tf_op jit(solution)/shard_map/ppermute | solution.py:39
  11.5 17.3 %collective-permute-start.2 = (bf16[272,512]{1,0:T(8,128)(2,1)}, bf16[272,512]{1,0:T(8,128)(2,1)S(1)}, u32[]{:S(2)}, u32[]{:S(2)}) collective-permute-start(bf16[272,512]{1,0:T(8,128)(2,1)} %get-tuple-element.419), channel_id=1, source_target_pairs={{0,1},{1,0},{2,3},{3,2},{4,5},{5,4},{6,7},{7,6},{8,9},{9,8},{10,11... | collective-permute-start | bytes 835592 | tf_op jit(solution)/shard_map/ppermute | solution.py:39
  13.0 15.8 %collective-permute-start = (bf16[272,512]{1,0:T(8,128)(2,1)}, bf16[272,512]{1,0:T(8,128)(2,1)}, u32[]{:S(2)}, u32[]{:S(2)}) collective-permute-start(bf16[272,512]{1,0:T(8,128)(2,1)} %get-tuple-element.418), channel_id=1, source_target_pairs={{0,2},{2,0},{1,3},{3,1},{4,6},{6,4},{5,7},{7,5},{8,10},{10,8},{9,1... | collective-permute-start | bytes 835592 | tf_op jit(solution)/shard_map/ppermute | solution.py:39
  29.5 23.6 %collective-permute-start.6 = (bf16[128,2048]{1,0:T(8,128)(2,1)S(1)}, bf16[128,2048]{1,0:T(8,128)(2,1)S(1)}, u32[]{:S(2)}, u32[]{:S(2)}) collective-permute-start(bf16[128,2048]{1,0:T(8,128)(2,1)S(1)} %copy-done.34), channel_id=1, source_target_pairs={{0,2},{2,0},{1,3},{3,1},{4,6},{6,4},{5,7},{7,5},{8,10},{10,8},{9,1... | collective-permute-start | bytes 1572872 | tf_op jit(solution)/shard_map/ppermute | solution.py:39
  34.0 19.1 %collective-permute-start.9 = (bf16[768,256]{1,0:T(8,128)(2,1)S(1)}, bf16[768,256]{1,0:T(8,128)(2,1)S(1)}, u32[]{:S(2)}, u32[]{:S(2)}) collective-permute-start(bf16[768,256]{1,0:T(8,128)(2,1)S(1)} %constant_dynamic-slice_fusion.9.refs_0_), channel_id=1, source_target_pairs={{0,1},{1,0},{2,3},{3,2},{4,5},{5,4},{6,7},{7,6},{8,9},{9,8},{10,11... | collective-permute-start | bytes 1179656 | tf_op jit(solution)/shard_map/ppermute | solution.py:39
  68.5 16.4 %collective-permute-start.17 = (bf16[256,768]{1,0:T(8,128)(2,1)S(1)}, bf16[256,768]{1,0:T(8,128)(2,1)S(1)}, u32[]{:S(2)}, u32[]{:S(2)}) collective-permute-start(bf16[256,768]{1,0:T(8,128)(2,1)S(1)} %get-tuple-element.453), channel_id=1, source_target_pairs={{0,2},{2,0},{1,3},{3,1},{4,6},{6,4},{5,7},{7,5},{8,10},{10,8},{9,1... | collective-permute-start | bytes 1179656 | tf_op jit(solution)/shard_map/ppermute | solution.py:39
  86.2 24.8 %collective-permute-start.20 = (bf16[1024,256]{1,0:T(8,128)(2,1)S(1)}, bf16[1024,256]{1,0:T(8,128)(2,1)S(1)}, u32[]{:S(2)}, u32[]{:S(2)}) collective-permute-start(bf16[1024,256]{1,0:T(8,128)(2,1)S(1)} %get-tuple-element.461.refs_0_), channel_id=1, source_target_pairs={{0,4},{4,0},{1,5},{5,1},{2,6},{6,2},{3,7},{7,3},{8,12},{12,8},{9,1... | collective-permute-start | bytes 1572872 | tf_op jit(solution)/shard_map/ppermute | solution.py:39
  86.6 24.4 %collective-permute-start.21 = (bf16[128,2048]{1,0:T(8,128)(2,1)S(1)}, bf16[128,2048]{1,0:T(8,128)(2,1)S(1)}, u32[]{:S(2)}, u32[]{:S(2)}) collective-permute-start(bf16[128,2048]{1,0:T(8,128)(2,1)S(1)} %copy-done.42), channel_id=1, source_target_pairs={{0,16},{16,0},{1,17},{17,1},{2,18},{18,2},{3,19},{19,3},{4,20},{20... | collective-permute-start | bytes 1572872 | tf_op jit(solution)/shard_map/ppermute | solution.py:39
  87.1 18.9 %collective-permute-start.23 = (bf16[256,768]{1,0:T(8,128)(2,1)S(1)}, bf16[256,768]{1,0:T(8,128)(2,1)S(1)}, u32[]{:S(2)}, u32[]{:S(2)}) collective-permute-start(bf16[256,768]{1,0:T(8,128)(2,1)S(1)} %constant_dynamic-slice_fusion.6), channel_id=1, source_target_pairs={{0,2},{2,0},{1,3},{3,1},{4,6},{6,4},{5,7},{7,5},{8,10},{10,8},{9,1... | collective-permute-start | bytes 1179656 | tf_op jit(solution)/shard_map/ppermute | solution.py:39
  111.9 28.1 %collective-permute-start.26 = (bf16[384,768]{1,0:T(8,128)(2,1)S(1)}, bf16[384,768]{1,0:T(8,128)(2,1)S(1)}, u32[]{:S(2)}, u32[]{:S(2)}) collective-permute-start(bf16[384,768]{1,0:T(8,128)(2,1)S(1)} %pad_maximum_fusion.7), channel_id=1, source_target_pairs={{0,4},{4,0},{1,5},{5,1},{2,6},{6,2},{3,7},{7,3},{8,12},{12,8},{9,1... | collective-permute-start | bytes 1769480 | tf_op jit(solution)/shard_map/ppermute | solution.py:39
  112.0 24.0 %collective-permute-start.27 = (bf16[128,2048]{1,0:T(8,128)(2,1)S(1)}, bf16[128,2048]{1,0:T(8,128)(2,1)S(1)}, u32[]{:S(2)}, u32[]{:S(2)}) collective-permute-start(bf16[128,2048]{1,0:T(8,128)(2,1)S(1)} %copy-done.42), channel_id=1, source_target_pairs={{0,2},{2,0},{1,3},{3,1},{4,6},{6,4},{5,7},{7,5},{8,10},{10,8},{9,1... | collective-permute-start | bytes 1572872 | tf_op jit(solution)/shard_map/ppermute | solution.py:39
  140.0 15.9 %collective-permute-start.28 = (bf16[512,2048]{1,0:T(8,128)(2,1)S(1)}, bf16[512,2048]{1,0:T(8,128)(2,1)S(1)}, u32[]{:S(2)}, u32[]{:S(2)}) collective-permute-start(bf16[512,2048]{1,0:T(8,128)(2,1)S(1)} %convolution_convert_fusion), channel_id=1, source_target_pairs={{0,8},{8,0},{1,9},{9,1},{2,10},{10,2},{3,11},{11,3},{4,12},{12,4},... | collective-permute-start | bytes 6291464 | tf_op jit(solution)/shard_map/ppermute | solution.py:39
  140.0 15.8 %collective-permute-start.31 = (bf16[128,2048]{1,0:T(8,128)(2,1)S(1)}, bf16[128,2048]{1,0:T(8,128)(2,1)S(1)}, u32[]{:S(2)}, u32[]{:S(2)}) collective-permute-start(bf16[128,2048]{1,0:T(8,128)(2,1)S(1)} %collective-permute-done.27), channel_id=1, source_target_pairs={{0,16},{16,0},{1,17},{17,1},{2,18},{18,2},{3,19},{19,3},{4,20},{20... | collective-permute-start | bytes 1572872 | tf_op jit(solution)/shard_map/ppermute | solution.py:39
  172.2 24.0 %collective-permute-start.40 = (bf16[512,2048]{1,0:T(8,128)(2,1)S(1)}, bf16[512,2048]{1,0:T(8,128)(2,1)S(1)}, u32[]{:S(2)}, u32[]{:S(2)}) collective-permute-start(bf16[512,2048]{1,0:T(8,128)(2,1)S(1)} %pad_maximum_fusion.refs_0_), channel_id=1, source_target_pairs={{0,8},{8,0},{1,9},{9,1},{2,10},{10,2},{3,11},{11,3},{4,12},{12,4},... | collective-permute-start | bytes 6291464 | tf_op jit(solution)/shard_map/ppermute | solution.py:39
  172.3 23.9 %collective-permute-start.38 = (bf16[512,768]{1,0:T(8,128)(2,1)S(1)}, bf16[512,768]{1,0:T(8,128)(2,1)S(1)}, u32[]{:S(2)}, u32[]{:S(2)}) collective-permute-start(bf16[512,768]{1,0:T(8,128)(2,1)S(1)} %assemble.5.refs_1_), channel_id=1, source_target_pairs={{0,1},{1,0},{2,3},{3,2},{4,5},{5,4},{6,7},{7,6},{8,9},{9,8},{10,11... | collective-permute-start | bytes 2359304 | tf_op jit(solution)/shard_map/ppermute | solution.py:39
  173.6 20.5 %collective-permute-start.36 = (bf16[128,2048]{1,0:T(8,128)(2,1)S(1)}, bf16[128,2048]{1,0:T(8,128)(2,1)S(1)}, u32[]{:S(2)}, u32[]{:S(2)}) collective-permute-start(bf16[128,2048]{1,0:T(8,128)(2,1)S(1)} %slice.547), channel_id=1, source_target_pairs={{0,16},{16,0},{1,17},{17,1},{2,18},{18,2},{3,19},{19,3},{4,20},{20... | collective-permute-start | bytes 1572872 | tf_op jit(solution)/shard_map/ppermute | solution.py:39
  174.1 22.1 %collective-permute-start.37 = (bf16[128,2048]{1,0:T(8,128)(2,1)S(1)}, bf16[128,2048]{1,0:T(8,128)(2,1)S(1)}, u32[]{:S(2)}, u32[]{:S(2)}) collective-permute-start(bf16[128,2048]{1,0:T(8,128)(2,1)S(1)} %add_convert_fusion.8), channel_id=1, source_target_pairs={{0,2},{2,0},{1,3},{3,1},{4,6},{6,4},{5,7},{7,5},{8,10},{10,8},{9,1... | collective-permute-start | bytes 1572872 | tf_op jit(solution)/shard_map/ppermute | solution.py:39
  174.1 19.9 %collective-permute-start.39 = (bf16[256,768]{1,0:T(8,128)(2,1)S(1)}, bf16[256,768]{1,0:T(8,128)(2,1)S(1)}, u32[]{:S(2)}, u32[]{:S(2)}) collective-permute-start(bf16[256,768]{1,0:T(8,128)(2,1)S(1)} %slice.317), channel_id=1, source_target_pairs={{0,4},{4,0},{1,5},{5,1},{2,6},{6,2},{3,7},{7,3},{8,12},{12,8},{9,1... | collective-permute-start | bytes 1179656 | tf_op jit(solution)/shard_map/ppermute | solution.py:39
  196.8 21.0 %collective-permute-start.41 = (bf16[128,2048]{1,0:T(8,128)(2,1)S(1)}, bf16[128,2048]{1,0:T(8,128)(2,1)S(1)}, u32[]{:S(2)}, u32[]{:S(2)}) collective-permute-start(bf16[128,2048]{1,0:T(8,128)(2,1)S(1)} %multiply_convert_fusion.4), channel_id=1, source_target_pairs={{0,16},{16,0},{1,17},{17,1},{2,18},{18,2},{3,19},{19,3},{4,20},{20... | collective-permute-start | bytes 1572872 | tf_op jit(solution)/shard_map/ppermute | solution.py:39
  198.4 21.1 %collective-permute-start.42 = (bf16[128,2048]{1,0:T(8,128)(2,1)S(1)}, bf16[128,2048]{1,0:T(8,128)(2,1)S(1)}, u32[]{:S(2)}, u32[]{:S(2)}) collective-permute-start(bf16[128,2048]{1,0:T(8,128)(2,1)S(1)} %multiply_convert_fusion.4), channel_id=1, source_target_pairs={{0,2},{2,0},{1,3},{3,1},{4,6},{6,4},{5,7},{7,5},{8,10},{10,8},{9,1... | collective-permute-start | bytes 1572872 | tf_op jit(solution)/shard_map/ppermute | solution.py:39
  199.7 17.5 %collective-permute-start.44 = (bf16[256,768]{1,0:T(8,128)(2,1)S(1)}, bf16[256,768]{1,0:T(8,128)(2,1)S(1)}, u32[]{:S(2)}, u32[]{:S(2)}) collective-permute-start(bf16[256,768]{1,0:T(8,128)(2,1)S(1)} %constant_dynamic-update-slice_fusion.11.refs_1_), channel_id=1, source_target_pairs={{0,1},{1,0},{2,3},{3,2},{4,5},{5,4},{6,7},{7,6},{8,9},{9,8},{10,11... | collective-permute-start | bytes 1179656 | tf_op jit(solution)/shard_map/ppermute | solution.py:39
  201.0 16.8 %collective-permute-start.45 = (bf16[768,256]{1,0:T(8,128)(2,1)S(1)}, bf16[768,256]{1,0:T(8,128)(2,1)S(1)}, u32[]{:S(2)}, u32[]{:S(2)}) collective-permute-start(bf16[768,256]{1,0:T(8,128)(2,1)S(1)} %constant_dynamic-slice_fusion.9.refs_0_), channel_id=1, source_target_pairs={{0,4},{4,0},{1,5},{5,1},{2,6},{6,2},{3,7},{7,3},{8,12},{12,8},{9,1... | collective-permute-start | bytes 1179656 | tf_op jit(solution)/shard_map/ppermute | solution.py:39
  255.0 18.2 %collective-permute-start.55 = (bf16[768,512]{1,0:T(8,128)(2,1)}, bf16[768,512]{1,0:T(8,128)(2,1)}, u32[]{:S(2)}, u32[]{:S(2)}) collective-permute-start(bf16[768,512]{1,0:T(8,128)(2,1)} %convolution_convert_fusion.8), channel_id=1, source_target_pairs={{0,1},{1,0},{2,3},{3,2},{4,5},{5,4},{6,7},{7,6},{8,9},{9,8},{10,11... | collective-permute-start | bytes 2359304 | tf_op jit(solution)/shard_map/ppermute | solution.py:39
  289.2 19.3 %collective-permute-start.60 = (bf16[512,768]{1,0:T(8,128)(2,1)S(1)}, bf16[512,768]{1,0:T(8,128)(2,1)S(1)}, u32[]{:S(2)}, u32[]{:S(2)}) collective-permute-start(bf16[512,768]{1,0:T(8,128)(2,1)S(1)} %convolution_convert_fusion.7), channel_id=1, source_target_pairs={{0,1},{1,0},{2,3},{3,2},{4,5},{5,4},{6,7},{7,6},{8,9},{9,8},{10,11... | collective-permute-start | bytes 2359304 | tf_op jit(solution)/shard_map/ppermute | solution.py:39
  291.1 16.3 %collective-permute-start.58 = (bf16[128,2048]{1,0:T(8,128)(2,1)S(1)}, bf16[128,2048]{1,0:T(8,128)(2,1)S(1)}, u32[]{:S(2)}, u32[]{:S(2)}) collective-permute-start(bf16[128,2048]{1,0:T(8,128)(2,1)S(1)} %slice.546), channel_id=1, source_target_pairs={{0,16},{16,0},{1,17},{17,1},{2,18},{18,2},{3,19},{19,3},{4,20},{20... | collective-permute-start | bytes 1572872 | tf_op jit(solution)/shard_map/ppermute | solution.py:39
  308.6 23.5 %collective-permute-start.64 = (bf16[512,768]{1,0:T(8,128)(2,1)S(1)}, bf16[512,768]{1,0:T(8,128)(2,1)S(1)}, u32[]{:S(2)}, u32[]{:S(2)}) collective-permute-start(bf16[512,768]{1,0:T(8,128)(2,1)S(1)} %convolution_convert_fusion.5), channel_id=1, source_target_pairs={{0,1},{1,0},{2,3},{3,2},{4,5},{5,4},{6,7},{7,6},{8,9},{9,8},{10,11... | collective-permute-start | bytes 2359304 | tf_op jit(solution)/shard_map/ppermute | solution.py:39
  310.6 19.3 %collective-permute-start.61 = (bf16[128,2048]{1,0:T(8,128)(2,1)S(1)}, bf16[128,2048]{1,0:T(8,128)(2,1)S(1)}, u32[]{:S(2)}, u32[]{:S(2)}) collective-permute-start(bf16[128,2048]{1,0:T(8,128)(2,1)S(1)} %slice.545), channel_id=1, source_target_pairs={{0,16},{16,0},{1,17},{17,1},{2,18},{18,2},{3,19},{19,3},{4,20},{20... | collective-permute-start | bytes 1572872 | tf_op jit(solution)/shard_map/ppermute | solution.py:39
  312.2 19.9 %collective-permute-start.62 = (bf16[128,2048]{1,0:T(8,128)(2,1)S(1)}, bf16[128,2048]{1,0:T(8,128)(2,1)S(1)}, u32[]{:S(2)}, u32[]{:S(2)}) collective-permute-start(bf16[128,2048]{1,0:T(8,128)(2,1)S(1)} %add_convert_fusion.7), channel_id=1, source_target_pairs={{0,2},{2,0},{1,3},{3,1},{4,6},{6,4},{5,7},{7,5},{8,10},{10,8},{9,1... | collective-permute-start | bytes 1572872 | tf_op jit(solution)/shard_map/ppermute | solution.py:39
  312.2 17.7 %collective-permute-start.63 = (bf16[352,512]{1,0:T(8,128)(2,1)S(1)}, bf16[352,512]{1,0:T(8,128)(2,1)S(1)}, u32[]{:S(2)}, u32[]{:S(2)}) collective-permute-start(bf16[352,512]{1,0:T(8,128)(2,1)S(1)} %slice.338), channel_id=1, source_target_pairs={{0,4},{4,0},{1,5},{5,1},{2,6},{6,2},{3,7},{7,3},{8,12},{12,8},{9,1... | collective-permute-start | bytes 1081352 | tf_op jit(solution)/shard_map/ppermute | solution.py:39
  334.2 20.4 %collective-permute-start.65 = (bf16[128,2048]{1,0:T(8,128)(2,1)S(1)}, bf16[128,2048]{1,0:T(8,128)(2,1)S(1)}, u32[]{:S(2)}, u32[]{:S(2)}) collective-permute-start(bf16[128,2048]{1,0:T(8,128)(2,1)S(1)} %get-tuple-element.632), channel_id=1, source_target_pairs={{0,16},{16,0},{1,17},{17,1},{2,18},{18,2},{3,19},{19,3},{4,20},{20... | collective-permute-start | bytes 1572872 | tf_op jit(solution)/shard_map/ppermute | solution.py:39
  335.2 21.0 %collective-permute-start.66 = (bf16[128,2048]{1,0:T(8,128)(2,1)S(1)}, bf16[128,2048]{1,0:T(8,128)(2,1)S(1)}, u32[]{:S(2)}, u32[]{:S(2)}) collective-permute-start(bf16[128,2048]{1,0:T(8,128)(2,1)S(1)} %get-tuple-element.632), channel_id=1, source_target_pairs={{0,2},{2,0},{1,3},{3,1},{4,6},{6,4},{5,7},{7,5},{8,10},{10,8},{9,1... | collective-permute-start | bytes 1572872 | tf_op jit(solution)/shard_map/ppermute | solution.py:39
  336.2 18.3 %collective-permute-start.67 = (bf16[256,768]{1,0:T(8,128)(2,1)S(1)}, bf16[256,768]{1,0:T(8,128)(2,1)S(1)}, u32[]{:S(2)}, u32[]{:S(2)}) collective-permute-start(bf16[256,768]{1,0:T(8,128)(2,1)S(1)} %slice.341), channel_id=1, source_target_pairs={{0,4},{4,0},{1,5},{5,1},{2,6},{6,2},{3,7},{7,3},{8,12},{12,8},{9,1... | collective-permute-start | bytes 1179656 | tf_op jit(solution)/shard_map/ppermute | solution.py:39
  337.9 18.3 %collective-permute-start.68 = (bf16[512,768]{1,0:T(8,128)(2,1)S(1)}, bf16[512,768]{1,0:T(8,128)(2,1)S(1)}, u32[]{:S(2)}, u32[]{:S(2)}) collective-permute-start(bf16[512,768]{1,0:T(8,128)(2,1)S(1)} %convolution_convert_fusion.4), channel_id=1, source_target_pairs={{0,1},{1,0},{2,3},{3,2},{4,5},{5,4},{6,7},{7,6},{8,9},{9,8},{10,11... | collective-permute-start | bytes 2359304 | tf_op jit(solution)/shard_map/ppermute | solution.py:39
  379.3 16.8 %collective-permute-start.76 = (bf16[192,768]{1,0:T(8,128)(2,1)S(1)}, bf16[192,768]{1,0:T(8,128)(2,1)S(1)}, u32[]{:S(2)}, u32[]{:S(2)}) collective-permute-start(bf16[192,768]{1,0:T(8,128)(2,1)S(1)} %pad_maximum_fusion.15), channel_id=1, source_target_pairs={{0,4},{4,0},{1,5},{5,1},{2,6},{6,2},{3,7},{7,3},{8,12},{12,8},{9,1... | collective-permute-start | bytes 884744 | tf_op jit(solution)/shard_map/ppermute | solution.py:39
  379.4 16.7 %collective-permute-start.77 = (bf16[256,768]{1,0:T(8,128)(2,1)S(1)}, bf16[256,768]{1,0:T(8,128)(2,1)S(1)}, u32[]{:S(2)}, u32[]{:S(2)}) collective-permute-start(bf16[256,768]{1,0:T(8,128)(2,1)S(1)} %get-tuple-element.671), channel_id=1, source_target_pairs={{0,1},{1,0},{2,3},{3,2},{4,5},{5,4},{6,7},{7,6},{8,9},{9,8},{10,11... | collective-permute-start | bytes 1179656 | tf_op jit(solution)/shard_map/ppermute | solution.py:39
  397.1 16.9 %collective-permute-start.80 = (bf16[1024,256]{1,0:T(8,128)(2,1)S(1)}, bf16[1024,256]{1,0:T(8,128)(2,1)S(1)}, u32[]{:S(2)}, u32[]{:S(2)}) collective-permute-start(bf16[1024,256]{1,0:T(8,128)(2,1)S(1)} %get-tuple-element.682), channel_id=1, source_target_pairs={{0,1},{1,0},{2,3},{3,2},{4,5},{5,4},{6,7},{7,6},{8,9},{9,8},{10,11... | collective-permute-start | bytes 1572872 | tf_op jit(solution)/shard_map/ppermute | solution.py:39
  398.3 15.7 %collective-permute-start.82 = (bf16[128,2048]{1,0:T(8,128)(2,1)S(1)}, bf16[128,2048]{1,0:T(8,128)(2,1)S(1)}, u32[]{:S(2)}, u32[]{:S(2)}) collective-permute-start(bf16[128,2048]{1,0:T(8,128)(2,1)S(1)} %get-tuple-element.684), channel_id=1, source_target_pairs={{0,16},{16,0},{1,17},{17,1},{2,18},{18,2},{3,19},{19,3},{4,20},{20... | collective-permute-start | bytes 1572872 | tf_op jit(solution)/shard_map/ppermute | solution.py:39
  415.5 23.0 %collective-permute-start.84 = (bf16[1024,256]{1,0:T(8,128)(2,1)S(1)}, bf16[1024,256]{1,0:T(8,128)(2,1)S(1)}, u32[]{:S(2)}, u32[]{:S(2)}) collective-permute-start(bf16[1024,256]{1,0:T(8,128)(2,1)S(1)} %add_convert_fusion.6), channel_id=1, source_target_pairs={{0,4},{4,0},{1,5},{5,1},{2,6},{6,2},{3,7},{7,3},{8,12},{12,8},{9,1... | collective-permute-start | bytes 1572872 | tf_op jit(solution)/shard_map/ppermute | solution.py:39
  415.6 23.0 %collective-permute-start.85 = (bf16[128,2048]{1,0:T(8,128)(2,1)S(1)}, bf16[128,2048]{1,0:T(8,128)(2,1)S(1)}, u32[]{:S(2)}, u32[]{:S(2)}) collective-permute-start(bf16[128,2048]{1,0:T(8,128)(2,1)S(1)} %get-tuple-element.697), channel_id=1, source_target_pairs={{0,16},{16,0},{1,17},{17,1},{2,18},{18,2},{3,19},{19,3},{4,20},{20... | collective-permute-start | bytes 1572872 | tf_op jit(solution)/shard_map/ppermute | solution.py:39
  416.5 23.6 %collective-permute-start.86 = (bf16[128,2048]{1,0:T(8,128)(2,1)S(1)}, bf16[128,2048]{1,0:T(8,128)(2,1)S(1)}, u32[]{:S(2)}, u32[]{:S(2)}) collective-permute-start(bf16[128,2048]{1,0:T(8,128)(2,1)S(1)} %add_convert_fusion.5), channel_id=1, source_target_pairs={{0,2},{2,0},{1,3},{3,1},{4,6},{6,4},{5,7},{7,5},{8,10},{10,8},{9,1... | collective-permute-start | bytes 1572872 | tf_op jit(solution)/shard_map/ppermute | solution.py:39
  462.6 18.8 %collective-permute-start.91 = (bf16[512,2048]{1,0:T(8,128)(2,1)}, bf16[512,2048]{1,0:T(8,128)(2,1)}, u32[]{:S(2)}, u32[]{:S(2)}) collective-permute-start(bf16[512,2048]{1,0:T(8,128)(2,1)} %convolution_convert_fusion.1), channel_id=1, source_target_pairs={{0,8},{8,0},{1,9},{9,1},{2,10},{10,2},{3,11},{11,3},{4,12},{12,4},... | collective-permute-start | bytes 6291464 | tf_op jit(solution)/shard_map/ppermute | solution.py:39
  462.6 17.5 %collective-permute-start.95 = (bf16[768,256]{1,0:T(8,128)(2,1)}, bf16[768,256]{1,0:T(8,128)(2,1)}, u32[]{:S(2)}, u32[]{:S(2)}) collective-permute-start(bf16[768,256]{1,0:T(8,128)(2,1)} %select_convert_fusion.1), channel_id=1, source_target_pairs={{0,2},{2,0},{1,3},{3,1},{4,6},{6,4},{5,7},{7,5},{8,10},{10,8},{9,1... | collective-permute-start | bytes 1179656 | tf_op jit(solution)/shard_map/ppermute | solution.py:39
  485.2 15.6 %collective-permute-start.96 = (bf16[128,2048]{1,0:T(8,128)(2,1)S(1)}, bf16[128,2048]{1,0:T(8,128)(2,1)S(1)}, u32[]{:S(2)}, u32[]{:S(2)}) collective-permute-start(bf16[128,2048]{1,0:T(8,128)(2,1)S(1)} %slice.544), channel_id=1, source_target_pairs={{0,16},{16,0},{1,17},{17,1},{2,18},{18,2},{3,19},{19,3},{4,20},{20... | collective-permute-start | bytes 1572872 | tf_op jit(solution)/shard_map/ppermute | solution.py:39
  501.0 20.0 %collective-permute-start.98 = (bf16[128,2048]{1,0:T(8,128)(2,1)S(1)}, bf16[128,2048]{1,0:T(8,128)(2,1)S(1)}, u32[]{:S(2)}, u32[]{:S(2)}) collective-permute-start(bf16[128,2048]{1,0:T(8,128)(2,1)S(1)} %slice.543), channel_id=1, source_target_pairs={{0,16},{16,0},{1,17},{17,1},{2,18},{18,2},{3,19},{19,3},{4,20},{20... | collective-permute-start | bytes 1572872 | tf_op jit(solution)/shard_map/ppermute | solution.py:39
  501.4 19.6 %collective-permute-start.99 = (bf16[128,2048]{1,0:T(8,128)(2,1)S(1)}, bf16[128,2048]{1,0:T(8,128)(2,1)S(1)}, u32[]{:S(2)}, u32[]{:S(2)}) collective-permute-start(bf16[128,2048]{1,0:T(8,128)(2,1)S(1)} %add_convert_fusion.3), channel_id=1, source_target_pairs={{0,2},{2,0},{1,3},{3,1},{4,6},{6,4},{5,7},{7,5},{8,10},{10,8},{9,1... | collective-permute-start | bytes 1572872 | tf_op jit(solution)/shard_map/ppermute | solution.py:39
  501.4 19.6 %collective-permute-start.100 = (bf16[512,512]{1,0:T(8,128)(2,1)S(1)}, bf16[512,512]{1,0:T(8,128)(2,1)S(1)}, u32[]{:S(2)}, u32[]{:S(2)}) collective-permute-start(bf16[512,512]{1,0:T(8,128)(2,1)S(1)} %copy-done.68), channel_id=1, source_target_pairs={{0,1},{1,0},{2,3},{3,2},{4,5},{5,4},{6,7},{7,6},{8,9},{9,8},{10,11... | collective-permute-start | bytes 1572872 | tf_op jit(solution)/shard_map/ppermute | solution.py:39
  503.1 17.9 %collective-permute-start.103 = (bf16[256,512]{1,0:T(8,128)(2,1)S(1)}, bf16[256,512]{1,0:T(8,128)(2,1)S(1)}, u32[]{:S(2)}, u32[]{:S(2)}) collective-permute-start(bf16[256,512]{1,0:T(8,128)(2,1)S(1)} %fusion.6), channel_id=1, source_target_pairs={{0,4},{4,0},{1,5},{5,1},{2,6},{6,2},{3,7},{7,3},{8,12},{12,8},{9,1... | collective-permute-start | bytes 786440 | tf_op jit(solution)/shard_map/ppermute | solution.py:39
  525.2 18.6 %collective-permute-start.110 = (bf16[256,768]{1,0:T(8,128)(2,1)S(1)}, bf16[256,768]{1,0:T(8,128)(2,1)S(1)}, u32[]{:S(2)}, u32[]{:S(2)}) collective-permute-start(bf16[256,768]{1,0:T(8,128)(2,1)S(1)} %select_convert_fusion), channel_id=1, source_target_pairs={{0,2},{2,0},{1,3},{3,1},{4,6},{6,4},{5,7},{7,5},{8,10},{10,8},{9,1... | collective-permute-start | bytes 1179656 | tf_op jit(solution)/shard_map/ppermute | solution.py:39
  (145 other events, 1530.8 us)

commit v2 on v1

--- a/solution.py
+++ b/solution.py
@@ -443,7 +443,7 @@
     put = (place == at_ref[1] * small).astype(BF16)
     extra = jnp.concatenate(
         [
-            jnp.concatenate([norm_ref[...], mlp_ref[...]], axis=1),
+            jnp.concatenate([norm_ref[...].reshape(1, rows), mlp_ref[...].reshape(1, rows)], axis=1),
             jnp.concatenate(
                 [
                     matmul(q_gain_ref[...], put).astype(BF16),
@@ -465,7 +465,7 @@
 
 def prologue(order, at, tokens, out_grad, q_weight, k_weight, v_weight, gains):
     shape = jax.ShapeDtypeStruct((q_weight.shape[0] + 16, (q_weight.shape[1] + 2 * k_weight.shape[1]) // 2), BF16)
-    whole = lambda value: pl.BlockSpec(value.shape, lambda i, order_ref, at_ref: (0, 0))
+    whole = lambda value: pl.BlockSpec(value.shape, lambda i, order_ref, at_ref: (0,) * len(value.shape))
     fixed = (q_weight, k_weight, v_weight) + gains
     return pl.pallas_call(
         prologue_kernel,
@@ -624,7 +624,7 @@
         q_weight,
         k_weight,
         v_weight,
-        (norm_gain[None], mlp_gain[None], q_gain[None], k_gain[None]),
+        (norm_gain, mlp_gain, q_gain[None], k_gain[None]),
     )
     local_rows = local_low.astype(F32)
     o_give = half_of(o_weight, 1 - za_at, 0)

time: 556 us -> 558 us (level)
  starting transfers between devices: 117 us -> 132 us
  Pallas kernels: 55.4 us -> 47.6 us
    ppermute x111, starting transfers between devices: 117 us -> 132 us  [swap(): return lax.ppermute(value, axis, SWAP)]
  transfers between devices with their start and end apart: 111 -> 111, of which waited for: 55 -> 57; matrix products, arithmetic and copies ran while one was open for 16% -> 16% of each run, Pallas kernels for 9% -> 8%
where the time goes in v2:
time: 558 us; the launch traced here: 550 us
  waiting for transfers between devices  252 us (45%)
  starting transfers between devices  132 us (24%)
  matrix products  54.9 us (10%)
  Pallas kernels  47.6 us (9%)
  other arithmetic  42.1 us (8%)
  local copies, waits for them, and re-layouts  18.2 us (3%)
    ppermute x111, waiting for transfers between devices, swap(): return lax.ppermute(value, axis, SWAP)  252 us
    ppermute x111, starting transfers between devices, swap(): return lax.ppermute(value, axis, SWAP)  132 us
    dot_general x22, matrix products, contract_rows(): lax.dot_general(left, right, PAIRS_OF_ROWS, preferred_element_type=F32)  27.9 us
    dot_general x7, matrix products, matmul(): return jnp.dot(left, right, preferred_element_type=F32)  14.7 us
    pallas_call x2, Pallas kernels, attend_back(): pl.pallas_call(functools.partial(attend_back_kernel, parts=parts, first=f...  13.6 us
    dot_general x5, matrix products, contract_cols(): lax.dot_general(left, right, PAIRS_OF_COLS, preferred_element_type=F32)  12.3 us
    unnamed x180, local copies, waits for them, and re-layouts  11.3 us
  transfers between devices with their start and end apart: 111, of which 57 were waited for; matrix products, arithmetic and copies ran while one was open for 16% of the time, Pallas kernels for 8%

profile of v2, /device:TPU:0, one launch (start us, length us, event | category | flops | bytes accessed | tf_op | source)
XLA Modules:
  0.0 550.3 jit_solution(15549072132010118422)
XLA Ops:
  1.8 3.3 prologue.1
  5.1 4.0 collective-permute-start.1
  21.4 5.0 collective-permute-done.4
  37.2 3.3 collective-permute-done.5
  40.5 4.5 collective-permute-done.8
  45.1 5.6 %collective-permute-done.9.refs_4_ = bf16[768,256]{1,0:T(8,128)(2,1)S(1)} collective-permute-done((bf16[768,256]{1,0:T(8,128)(2,1)S(1)}, bf16[768,256]{1,0:T(8,128)(2,1)S(1)}, u32[]{:S(2)}, u32[]{:S(2)}) %collective-permute-start.9) | collective-permute-done | bytes 393248 | tf_op jit(solution)/shard_map/ppermute | solution.py:39
  57.4 3.0 collective-permute-done.12
  61.9 3.2 collective-permute-done.14
  78.1 4.4 collective-permute-done.17
  86.7 9.3 %collective-permute-done.19.refs_1_ = bf16[1024,256]{1,0:T(8,128)(2,1)S(1)} collective-permute-done((bf16[1024,256]{1,0:T(8,128)(2,1)S(1)}, bf16[1024,256]{1,0:T(8,128)(2,1)S(1)}, u32[]{:S(2)}, u32[]{:S(2)}) %collective-permute-start.19) | collective-permute-done | bytes 524320 | tf_op jit(solution)/shard_map/ppermute | solution.py:39
  97.6 5.9 %attend.2.refs_2_ = f32[8,256,256]{2,1,0:T(8,128)S(1)} custom-call(s32[32]{0:T(128)S(1)} %broadcast_add_fusion.1.off_ref, s32[8]{0:T(128)S(1)} %get-tuple-element.834.tile_ref, s32[8]{0:T(128)S(1)} %and_select_fusion.low_ref, bf16[1024,256]{1,0:T(8,128)(2,1)S(1)} %get-tuple-element.462.q_ref, s32[1024,128]{1,0:T(8,128)S(1)} %broadcast_in_dim.115.start_ref, ...), custom_call_target="tpu_custom_call" | custom-call | flops 1000 | bytes 1000 | tf_op jit(solution)/shard_map/attend/pallas_call | solution.py:195
  103.6 4.9 collective-permute-done.20.refs_0_
  114.1 8.4 %collective-permute-done.24.refs_1_ = bf16[1024,256]{1,0:T(8,128)(2,1)S(1)} collective-permute-done((bf16[1024,256]{1,0:T(8,128)(2,1)S(1)}, bf16[1024,256]{1,0:T(8,128)(2,1)S(1)}, u32[]{:S(2)}, u32[]{:S(2)}) %collective-permute-start.24) | collective-permute-done | bytes 524320 | tf_op jit(solution)/shard_map/ppermute | solution.py:39
  123.5 3.4 attend.3
  127.6 7.4 %collective-permute-done.27 = bf16[128,2048]{1,0:T(8,128)(2,1)S(1)} collective-permute-done((bf16[128,2048]{1,0:T(8,128)(2,1)S(1)}, bf16[128,2048]{1,0:T(8,128)(2,1)S(1)}, u32[]{:S(2)}, u32[]{:S(2)}) %collective-permute-start.27) | collective-permute-done | bytes 524320 | tf_op jit(solution)/shard_map/ppermute | solution.py:39
  135.0 3.0 collective-permute-done.26
  140.1 3.4 collective-permute-start.29
  144.3 7.4 %collective-permute-done.29 = bf16[96,768]{1,0:T(8,128)(2,1)S(1)} collective-permute-done((bf16[96,768]{1,0:T(8,128)(2,1)S(1)}, bf16[96,768]{1,0:T(8,128)(2,1)S(1)}, u32[]{:S(2)}, u32[]{:S(2)}) %collective-permute-start.29) | collective-permute-done | bytes 147488 | tf_op jit(solution)/shard_map/ppermute | solution.py:39
  158.9 11.1 %collective-permute-done.35 = bf16[160,768]{1,0:T(8,128)(2,1)S(1)} collective-permute-done((bf16[160,768]{1,0:T(8,128)(2,1)S(1)}, bf16[160,768]{1,0:T(8,128)(2,1)S(1)}, u32[]{:S(2)}, u32[]{:S(2)}) %collective-permute-start.35) | collective-permute-done | bytes 245792 | tf_op jit(solution)/shard_map/ppermute | solution.py:39
  174.9 17.2 %collective-permute-done.39.refs_2_ = bf16[256,768]{1,0:T(8,128)(2,1)S(1)} collective-permute-done((bf16[256,768]{1,0:T(8,128)(2,1)S(1)}, bf16[256,768]{1,0:T(8,128)(2,1)S(1)}, u32[]{:S(2)}, u32[]{:S(2)}) %collective-permute-start.39) | collective-permute-done | bytes 393248 | tf_op jit(solution)/shard_map/ppermute | solution.py:39
  201.9 7.7 %collective-permute-done.43.refs_5_ = bf16[768,256]{1,0:T(8,128)(2,1)S(1)} collective-permute-done((bf16[768,256]{1,0:T(8,128)(2,1)S(1)}, bf16[768,256]{1,0:T(8,128)(2,1)S(1)}, u32[]{:S(2)}, u32[]{:S(2)}) %collective-permute-start.43) | collective-permute-done | bytes 393248 | tf_op jit(solution)/shard_map/ppermute | solution.py:39
  209.5 6.2 %collective-permute-done.44.refs_5_ = bf16[256,768]{1,0:T(8,128)(2,1)S(1)} collective-permute-done((bf16[256,768]{1,0:T(8,128)(2,1)S(1)}, bf16[256,768]{1,0:T(8,128)(2,1)S(1)}, u32[]{:S(2)}, u32[]{:S(2)}) %collective-permute-start.44) | collective-permute-done | bytes 393248 | tf_op jit(solution)/shard_map/ppermute | solution.py:39
  223.2 6.2 %collective-permute-done.48 = bf16[400,256]{1,0:T(8,128)(2,1)S(1)} collective-permute-done((bf16[400,256]{1,0:T(8,128)(2,1)S(1)}, bf16[400,256]{1,0:T(8,128)(2,1)S(1)}, u32[]{:S(2)}, u32[]{:S(2)}) %collective-permute-start.48) | collective-permute-done | bytes 204832 | tf_op jit(solution)/shard_map/ppermute | solution.py:39
  233.8 3.4 fusion.81
  238.5 3.9 multiply_convert_fusion.2
  242.4 4.1 collective-permute-done.53
  254.2 4.9 multiply_convert_fusion
  259.1 10.8 %two_terms.1 = (f32[512,2048]{1,0:T(8,128)}, bf16[512,2048]{1,0:T(8,128)(2,1)}) custom-call(bf16[1024,768]{1,0:T(8,128)(2,1)} %get-tuple-element.652.left_ref, bf16[1024,768]{1,0:T(8,128)(2,1)} %get-tuple-element.780.right_ref, bf16[2048,768]{1,0:T(8,128)(2,1)} %copy-done.2, bf16[2048,768]{1,0:T(8,128)(2,1)} %copy-done.3), custom_call_target="tpu_custom_call" | custom-call | flops 1000 | bytes 1000 | tf_op jit(solution)/shard_map/two_terms/pallas_call | solution.py:384
  279.6 6.5 %collective-permute-done.57 = bf16[144,512]{1,0:T(8,128)(2,1)S(1)} collective-permute-done((bf16[144,512]{1,0:T(8,128)(2,1)S(1)}, bf16[144,512]{1,0:T(8,128)(2,1)S(1)}, u32[]{:S(2)}, u32[]{:S(2)}) %collective-permute-start.57) | collective-permute-done | bytes 147488 | tf_op jit(solution)/shard_map/ppermute | solution.py:39
  292.7 13.4 %collective-permute-done.59 = bf16[272,512]{1,0:T(8,128)(2,1)S(1)} collective-permute-done((bf16[272,512]{1,0:T(8,128)(2,1)S(1)}, bf16[272,512]{1,0:T(8,128)(2,1)S(1)}, u32[]{:S(2)}, u32[]{:S(2)}) %collective-permute-start.59) | collective-permute-done | bytes 278560 | tf_op jit(solution)/shard_map/ppermute | solution.py:39
  309.9 3.4 collective-permute-start.63
  314.6 13.5 %collective-permute-done.63 = bf16[352,512]{1,0:T(8,128)(2,1)S(1)} collective-permute-done((bf16[352,512]{1,0:T(8,128)(2,1)S(1)}, bf16[352,512]{1,0:T(8,128)(2,1)S(1)}, u32[]{:S(2)}, u32[]{:S(2)}) %collective-permute-start.63) | collective-permute-done | bytes 360480 | tf_op jit(solution)/shard_map/ppermute | solution.py:39
  340.1 12.5 %collective-permute-done.67 = bf16[256,768]{1,0:T(8,128)(2,1)S(1)} collective-permute-done((bf16[256,768]{1,0:T(8,128)(2,1)S(1)}, bf16[256,768]{1,0:T(8,128)(2,1)S(1)}, u32[]{:S(2)}, u32[]{:S(2)}) %collective-permute-start.67) | collective-permute-done | bytes 393248 | tf_op jit(solution)/shard_map/ppermute | solution.py:39
  362.3 4.2 collective-permute-done.71
  373.1 5.1 collective-permute-done.74
  381.3 4.6 attend_back.2
  385.9 9.2 %collective-permute-done.78 = bf16[256,512]{1,0:T(8,128)(2,1)S(1)} collective-permute-done((bf16[256,512]{1,0:T(8,128)(2,1)S(1)}, bf16[256,512]{1,0:T(8,128)(2,1)S(1)}, u32[]{:S(2)}, u32[]{:S(2)}) %collective-permute-start.78) | collective-permute-done | bytes 262176 | tf_op jit(solution)/shard_map/ppermute | solution.py:39
  399.7 9.0 %attend_back.3 = (bf16[1024,256]{1,0:T(8,128)(2,1)S(1)}, bf16[1024,256]{1,0:T(8,128)(2,1)S(1)}, bf16[1024,256]{1,0:T(8,128)(2,1)S(1)}) custom-call(s32[32]{0:T(128)S(1)} %broadcast_add_fusion.1.off_ref, s32[8]{0:T(128)S(1)} %get-tuple-element.834.tile_ref, s32[8]{0:T(128)S(1)} %and_select_fusion.low_ref, bf16[1024,256]{1,0:T(8,128)(2,1)S(1)} %get-tuple-element.462.q_ref, ...), custom_call_target="tpu_custom_call" | custom-call | flops 1000 | bytes 1000 | tf_op jit(solution)/shard_map/attend_back/pallas_call | solution.py:213
  408.7 3.2 collective-permute-done.81
  413.7 7.1 %collective-permute-start.84 = (bf16[1024,256]{1,0:T(8,128)(2,1)S(1)}, bf16[1024,256]{1,0:T(8,128)(2,1)S(1)}, u32[]{:S(2)}, u32[]{:S(2)}) collective-permute-start(bf16[1024,256]{1,0:T(8,128)(2,1)S(1)} %add_convert_fusion.6), channel_id=1, source_target_pairs={{0,4},{4,0},{1,5},{5,1},{2,6},{6,2},{3,7},{7,3},{8,12},{12,8},{9,1... | collective-permute-start | bytes 1572872 | tf_op jit(solution)/shard_map/ppermute | solution.py:39
  434.5 8.1 %collective-permute-done.84 = bf16[1024,256]{1,0:T(8,128)(2,1)S(1)} collective-permute-done((bf16[1024,256]{1,0:T(8,128)(2,1)S(1)}, bf16[1024,256]{1,0:T(8,128)(2,1)S(1)}, u32[]{:S(2)}, u32[]{:S(2)}) %collective-permute-start.84) | collective-permute-done | bytes 524320 | tf_op jit(solution)/shard_map/ppermute | solution.py:39
  456.3 7.8 %collective-permute-done.89 = bf16[176,768]{1,0:T(8,128)(2,1)S(1)} collective-permute-done((bf16[176,768]{1,0:T(8,128)(2,1)S(1)}, bf16[176,768]{1,0:T(8,128)(2,1)S(1)}, u32[]{:S(2)}, u32[]{:S(2)}) %collective-permute-start.89) | collective-permute-done | bytes 270368 | tf_op jit(solution)/shard_map/ppermute | solution.py:39
  466.4 3.5 collective-permute-start.95
  475.7 3.2 fusion.47
  487.8 3.6 convert_add_fusion
  499.6 6.9 %collective-permute-done.97 = bf16[512,256]{1,0:T(8,128)(2,1)S(1)} collective-permute-done((bf16[512,256]{1,0:T(8,128)(2,1)S(1)}, bf16[512,256]{1,0:T(8,128)(2,1)S(1)}, u32[]{:S(2)}, u32[]{:S(2)}) %collective-permute-start.97) | collective-permute-done | bytes 262176 | tf_op jit(solution)/shard_map/ppermute | solution.py:39
  519.4 7.0 %collective-permute-done.102 = f32[1,4352]{1,0:T(1,128)S(1)} collective-permute-done((f32[1,4352]{1,0:T(1,128)S(1)}, f32[1,4352]{1,0:T(1,128)S(1)}, u32[]{:S(2)}, u32[]{:S(2)}) %collective-permute-start.102) | collective-permute-done | bytes 17440 | tf_op jit(solution)/shard_map/ppermute | solution.py:39
  533.2 3.5 reorder.3
  (583 shorter events, 246.7 us)
Async XLA Ops:
  5.1 21.3 %collective-permute-start.1 = (bf16[272,512]{1,0:T(8,128)(2,1)}, bf16[272,512]{1,0:T(8,128)(2,1)S(1)}, u32[]{:S(2)}, u32[]{:S(2)}) collective-permute-start(bf16[272,512]{1,0:T(8,128)(2,1)} %get-tuple-element.419), channel_id=1, source_target_pairs={{0,4},{4,0},{1,5},{5,1},{2,6},{6,2},{3,7},{7,3},{8,12},{12,8},{9,1... | collective-permute-start | bytes 835592 | tf_op jit(solution)/shard_map/ppermute | solution.py:39
  9.1 17.3 %collective-permute-start.2 = (bf16[272,512]{1,0:T(8,128)(2,1)}, bf16[272,512]{1,0:T(8,128)(2,1)S(1)}, u32[]{:S(2)}, u32[]{:S(2)}) collective-permute-start(bf16[272,512]{1,0:T(8,128)(2,1)} %get-tuple-element.419), channel_id=1, source_target_pairs={{0,1},{1,0},{2,3},{3,2},{4,5},{5,4},{6,7},{7,6},{8,9},{9,8},{10,11... | collective-permute-start | bytes 835592 | tf_op jit(solution)/shard_map/ppermute | solution.py:39
  10.6 15.8 %collective-permute-start = (bf16[272,512]{1,0:T(8,128)(2,1)}, bf16[272,512]{1,0:T(8,128)(2,1)}, u32[]{:S(2)}, u32[]{:S(2)}) collective-permute-start(bf16[272,512]{1,0:T(8,128)(2,1)} %get-tuple-element.418), channel_id=1, source_target_pairs={{0,2},{2,0},{1,3},{3,1},{4,6},{6,4},{5,7},{7,5},{8,10},{10,8},{9,1... | collective-permute-start | bytes 835592 | tf_op jit(solution)/shard_map/ppermute | solution.py:39
  27.0 23.6 %collective-permute-start.6 = (bf16[128,2048]{1,0:T(8,128)(2,1)S(1)}, bf16[128,2048]{1,0:T(8,128)(2,1)S(1)}, u32[]{:S(2)}, u32[]{:S(2)}) collective-permute-start(bf16[128,2048]{1,0:T(8,128)(2,1)S(1)} %copy-done.34), channel_id=1, source_target_pairs={{0,2},{2,0},{1,3},{3,1},{4,6},{6,4},{5,7},{7,5},{8,10},{10,8},{9,1... | collective-permute-start | bytes 1572872 | tf_op jit(solution)/shard_map/ppermute | solution.py:39
  31.5 19.1 %collective-permute-start.9 = (bf16[768,256]{1,0:T(8,128)(2,1)S(1)}, bf16[768,256]{1,0:T(8,128)(2,1)S(1)}, u32[]{:S(2)}, u32[]{:S(2)}) collective-permute-start(bf16[768,256]{1,0:T(8,128)(2,1)S(1)} %constant_dynamic-slice_fusion.9.refs_0_), channel_id=1, source_target_pairs={{0,1},{1,0},{2,3},{3,2},{4,5},{5,4},{6,7},{7,6},{8,9},{9,8},{10,11... | collective-permute-start | bytes 1179656 | tf_op jit(solution)/shard_map/ppermute | solution.py:39
  66.1 16.4 %collective-permute-start.17 = (bf16[256,768]{1,0:T(8,128)(2,1)S(1)}, bf16[256,768]{1,0:T(8,128)(2,1)S(1)}, u32[]{:S(2)}, u32[]{:S(2)}) collective-permute-start(bf16[256,768]{1,0:T(8,128)(2,1)S(1)} %get-tuple-element.453), channel_id=1, source_target_pairs={{0,2},{2,0},{1,3},{3,1},{4,6},{6,4},{5,7},{7,5},{8,10},{10,8},{9,1... | collective-permute-start | bytes 1179656 | tf_op jit(solution)/shard_map/ppermute | solution.py:39
  83.8 24.8 %collective-permute-start.20 = (bf16[1024,256]{1,0:T(8,128)(2,1)S(1)}, bf16[1024,256]{1,0:T(8,128)(2,1)S(1)}, u32[]{:S(2)}, u32[]{:S(2)}) collective-permute-start(bf16[1024,256]{1,0:T(8,128)(2,1)S(1)} %get-tuple-element.461.refs_0_), channel_id=1, source_target_pairs={{0,4},{4,0},{1,5},{5,1},{2,6},{6,2},{3,7},{7,3},{8,12},{12,8},{9,1... | collective-permute-start | bytes 1572872 | tf_op jit(solution)/shard_map/ppermute | solution.py:39
  84.2 24.4 %collective-permute-start.21 = (bf16[128,2048]{1,0:T(8,128)(2,1)S(1)}, bf16[128,2048]{1,0:T(8,128)(2,1)S(1)}, u32[]{:S(2)}, u32[]{:S(2)}) collective-permute-start(bf16[128,2048]{1,0:T(8,128)(2,1)S(1)} %copy-done.42), channel_id=1, source_target_pairs={{0,16},{16,0},{1,17},{17,1},{2,18},{18,2},{3,19},{19,3},{4,20},{20... | collective-permute-start | bytes 1572872 | tf_op jit(solution)/shard_map/ppermute | solution.py:39
  84.7 18.9 %collective-permute-start.23 = (bf16[256,768]{1,0:T(8,128)(2,1)S(1)}, bf16[256,768]{1,0:T(8,128)(2,1)S(1)}, u32[]{:S(2)}, u32[]{:S(2)}) collective-permute-start(bf16[256,768]{1,0:T(8,128)(2,1)S(1)} %constant_dynamic-slice_fusion.6), channel_id=1, source_target_pairs={{0,2},{2,0},{1,3},{3,1},{4,6},{6,4},{5,7},{7,5},{8,10},{10,8},{9,1... | collective-permute-start | bytes 1179656 | tf_op jit(solution)/shard_map/ppermute | solution.py:39
  109.5 28.6 %collective-permute-start.26 = (bf16[384,768]{1,0:T(8,128)(2,1)S(1)}, bf16[384,768]{1,0:T(8,128)(2,1)S(1)}, u32[]{:S(2)}, u32[]{:S(2)}) collective-permute-start(bf16[384,768]{1,0:T(8,128)(2,1)S(1)} %pad_maximum_fusion.7), channel_id=1, source_target_pairs={{0,4},{4,0},{1,5},{5,1},{2,6},{6,2},{3,7},{7,3},{8,12},{12,8},{9,1... | collective-permute-start | bytes 1769480 | tf_op jit(solution)/shard_map/ppermute | solution.py:39
  112.2 22.8 %collective-permute-start.27 = (bf16[128,2048]{1,0:T(8,128)(2,1)S(1)}, bf16[128,2048]{1,0:T(8,128)(2,1)S(1)}, u32[]{:S(2)}, u32[]{:S(2)}) collective-permute-start(bf16[128,2048]{1,0:T(8,128)(2,1)S(1)} %copy-done.42), channel_id=1, source_target_pairs={{0,2},{2,0},{1,3},{3,1},{4,6},{6,4},{5,7},{7,5},{8,10},{10,8},{9,1... | collective-permute-start | bytes 1572872 | tf_op jit(solution)/shard_map/ppermute | solution.py:39
  138.0 15.9 %collective-permute-start.28 = (bf16[512,2048]{1,0:T(8,128)(2,1)S(1)}, bf16[512,2048]{1,0:T(8,128)(2,1)S(1)}, u32[]{:S(2)}, u32[]{:S(2)}) collective-permute-start(bf16[512,2048]{1,0:T(8,128)(2,1)S(1)} %convolution_convert_fusion), channel_id=1, source_target_pairs={{0,8},{8,0},{1,9},{9,1},{2,10},{10,2},{3,11},{11,3},{4,12},{12,4},... | collective-permute-start | bytes 6291464 | tf_op jit(solution)/shard_map/ppermute | solution.py:39
  138.0 15.9 %collective-permute-start.31 = (bf16[128,2048]{1,0:T(8,128)(2,1)S(1)}, bf16[128,2048]{1,0:T(8,128)(2,1)S(1)}, u32[]{:S(2)}, u32[]{:S(2)}) collective-permute-start(bf16[128,2048]{1,0:T(8,128)(2,1)S(1)} %collective-permute-done.27), channel_id=1, source_target_pairs={{0,16},{16,0},{1,17},{17,1},{2,18},{18,2},{3,19},{19,3},{4,20},{20... | collective-permute-start | bytes 1572872 | tf_op jit(solution)/shard_map/ppermute | solution.py:39
  170.3 24.1 %collective-permute-start.40 = (bf16[512,2048]{1,0:T(8,128)(2,1)S(1)}, bf16[512,2048]{1,0:T(8,128)(2,1)S(1)}, u32[]{:S(2)}, u32[]{:S(2)}) collective-permute-start(bf16[512,2048]{1,0:T(8,128)(2,1)S(1)} %pad_maximum_fusion.refs_0_), channel_id=1, source_target_pairs={{0,8},{8,0},{1,9},{9,1},{2,10},{10,2},{3,11},{11,3},{4,12},{12,4},... | collective-permute-start | bytes 6291464 | tf_op jit(solution)/shard_map/ppermute | solution.py:39
  170.3 24.0 %collective-permute-start.38 = (bf16[512,768]{1,0:T(8,128)(2,1)S(1)}, bf16[512,768]{1,0:T(8,128)(2,1)S(1)}, u32[]{:S(2)}, u32[]{:S(2)}) collective-permute-start(bf16[512,768]{1,0:T(8,128)(2,1)S(1)} %assemble.5.refs_1_), channel_id=1, source_target_pairs={{0,1},{1,0},{2,3},{3,2},{4,5},{5,4},{6,7},{7,6},{8,9},{9,8},{10,11... | collective-permute-start | bytes 2359304 | tf_op jit(solution)/shard_map/ppermute | solution.py:39
  171.7 20.5 %collective-permute-start.36 = (bf16[128,2048]{1,0:T(8,128)(2,1)S(1)}, bf16[128,2048]{1,0:T(8,128)(2,1)S(1)}, u32[]{:S(2)}, u32[]{:S(2)}) collective-permute-start(bf16[128,2048]{1,0:T(8,128)(2,1)S(1)} %slice.547), channel_id=1, source_target_pairs={{0,16},{16,0},{1,17},{17,1},{2,18},{18,2},{3,19},{19,3},{4,20},{20... | collective-permute-start | bytes 1572872 | tf_op jit(solution)/shard_map/ppermute | solution.py:39
  172.2 22.1 %collective-permute-start.37 = (bf16[128,2048]{1,0:T(8,128)(2,1)S(1)}, bf16[128,2048]{1,0:T(8,128)(2,1)S(1)}, u32[]{:S(2)}, u32[]{:S(2)}) collective-permute-start(bf16[128,2048]{1,0:T(8,128)(2,1)S(1)} %add_convert_fusion.8), channel_id=1, source_target_pairs={{0,2},{2,0},{1,3},{3,1},{4,6},{6,4},{5,7},{7,5},{8,10},{10,8},{9,1... | collective-permute-start | bytes 1572872 | tf_op jit(solution)/shard_map/ppermute | solution.py:39
  172.3 19.8 %collective-permute-start.39 = (bf16[256,768]{1,0:T(8,128)(2,1)S(1)}, bf16[256,768]{1,0:T(8,128)(2,1)S(1)}, u32[]{:S(2)}, u32[]{:S(2)}) collective-permute-start(bf16[256,768]{1,0:T(8,128)(2,1)S(1)} %slice.317), channel_id=1, source_target_pairs={{0,4},{4,0},{1,5},{5,1},{2,6},{6,2},{3,7},{7,3},{8,12},{12,8},{9,1... | collective-permute-start | bytes 1179656 | tf_op jit(solution)/shard_map/ppermute | solution.py:39
  194.9 21.4 %collective-permute-start.41 = (bf16[128,2048]{1,0:T(8,128)(2,1)S(1)}, bf16[128,2048]{1,0:T(8,128)(2,1)S(1)}, u32[]{:S(2)}, u32[]{:S(2)}) collective-permute-start(bf16[128,2048]{1,0:T(8,128)(2,1)S(1)} %multiply_convert_fusion.4), channel_id=1, source_target_pairs={{0,16},{16,0},{1,17},{17,1},{2,18},{18,2},{3,19},{19,3},{4,20},{20... | collective-permute-start | bytes 1572872 | tf_op jit(solution)/shard_map/ppermute | solution.py:39
  196.5 21.1 %collective-permute-start.42 = (bf16[128,2048]{1,0:T(8,128)(2,1)S(1)}, bf16[128,2048]{1,0:T(8,128)(2,1)S(1)}, u32[]{:S(2)}, u32[]{:S(2)}) collective-permute-start(bf16[128,2048]{1,0:T(8,128)(2,1)S(1)} %multiply_convert_fusion.4), channel_id=1, source_target_pairs={{0,2},{2,0},{1,3},{3,1},{4,6},{6,4},{5,7},{7,5},{8,10},{10,8},{9,1... | collective-permute-start | bytes 1572872 | tf_op jit(solution)/shard_map/ppermute | solution.py:39
  198.5 17.1 %collective-permute-start.44 = (bf16[256,768]{1,0:T(8,128)(2,1)S(1)}, bf16[256,768]{1,0:T(8,128)(2,1)S(1)}, u32[]{:S(2)}, u32[]{:S(2)}) collective-permute-start(bf16[256,768]{1,0:T(8,128)(2,1)S(1)} %constant_dynamic-update-slice_fusion.11.refs_1_), channel_id=1, source_target_pairs={{0,1},{1,0},{2,3},{3,2},{4,5},{5,4},{6,7},{7,6},{8,9},{9,8},{10,11... | collective-permute-start | bytes 1179656 | tf_op jit(solution)/shard_map/ppermute | solution.py:39
  199.5 16.8 %collective-permute-start.45 = (bf16[768,256]{1,0:T(8,128)(2,1)S(1)}, bf16[768,256]{1,0:T(8,128)(2,1)S(1)}, u32[]{:S(2)}, u32[]{:S(2)}) collective-permute-start(bf16[768,256]{1,0:T(8,128)(2,1)S(1)} %constant_dynamic-slice_fusion.9.refs_0_), channel_id=1, source_target_pairs={{0,4},{4,0},{1,5},{5,1},{2,6},{6,2},{3,7},{7,3},{8,12},{12,8},{9,1... | collective-permute-start | bytes 1179656 | tf_op jit(solution)/shard_map/ppermute | solution.py:39
  231.0 15.6 %collective-permute-start.52 = (bf16[768,256]{1,0:T(8,128)(2,1)S(1)}, bf16[768,256]{1,0:T(8,128)(2,1)S(1)}, u32[]{:S(2)}, u32[]{:S(2)}) collective-permute-start(bf16[768,256]{1,0:T(8,128)(2,1)S(1)} %collective-permute-done.45.refs_2_), channel_id=1, source_target_pairs={{0,1},{1,0},{2,3},{3,2},{4,5},{5,4},{6,7},{7,6},{8,9},{9,8},{10,11... | collective-permute-start | bytes 1179656 | tf_op jit(solution)/shard_map/ppermute | solution.py:39
  253.0 18.2 %collective-permute-start.55 = (bf16[768,512]{1,0:T(8,128)(2,1)}, bf16[768,512]{1,0:T(8,128)(2,1)}, u32[]{:S(2)}, u32[]{:S(2)}) collective-permute-start(bf16[768,512]{1,0:T(8,128)(2,1)} %convolution_convert_fusion.8), channel_id=1, source_target_pairs={{0,1},{1,0},{2,3},{3,2},{4,5},{5,4},{6,7},{7,6},{8,9},{9,8},{10,11... | collective-permute-start | bytes 2359304 | tf_op jit(solution)/shard_map/ppermute | solution.py:39
  287.1 19.2 %collective-permute-start.60 = (bf16[512,768]{1,0:T(8,128)(2,1)S(1)}, bf16[512,768]{1,0:T(8,128)(2,1)S(1)}, u32[]{:S(2)}, u32[]{:S(2)}) collective-permute-start(bf16[512,768]{1,0:T(8,128)(2,1)S(1)} %convolution_convert_fusion.7), channel_id=1, source_target_pairs={{0,1},{1,0},{2,3},{3,2},{4,5},{5,4},{6,7},{7,6},{8,9},{9,8},{10,11... | collective-permute-start | bytes 2359304 | tf_op jit(solution)/shard_map/ppermute | solution.py:39
  289.4 16.8 %collective-permute-start.58 = (bf16[128,2048]{1,0:T(8,128)(2,1)S(1)}, bf16[128,2048]{1,0:T(8,128)(2,1)S(1)}, u32[]{:S(2)}, u32[]{:S(2)}) collective-permute-start(bf16[128,2048]{1,0:T(8,128)(2,1)S(1)} %slice.546), channel_id=1, source_target_pairs={{0,16},{16,0},{1,17},{17,1},{2,18},{18,2},{3,19},{19,3},{4,20},{20... | collective-permute-start | bytes 1572872 | tf_op jit(solution)/shard_map/ppermute | solution.py:39
  306.5 23.9 %collective-permute-start.64 = (bf16[512,768]{1,0:T(8,128)(2,1)S(1)}, bf16[512,768]{1,0:T(8,128)(2,1)S(1)}, u32[]{:S(2)}, u32[]{:S(2)}) collective-permute-start(bf16[512,768]{1,0:T(8,128)(2,1)S(1)} %convolution_convert_fusion.5), channel_id=1, source_target_pairs={{0,1},{1,0},{2,3},{3,2},{4,5},{5,4},{6,7},{7,6},{8,9},{9,8},{10,11... | collective-permute-start | bytes 2359304 | tf_op jit(solution)/shard_map/ppermute | solution.py:39
  308.7 19.4 %collective-permute-start.61 = (bf16[128,2048]{1,0:T(8,128)(2,1)S(1)}, bf16[128,2048]{1,0:T(8,128)(2,1)S(1)}, u32[]{:S(2)}, u32[]{:S(2)}) collective-permute-start(bf16[128,2048]{1,0:T(8,128)(2,1)S(1)} %slice.545), channel_id=1, source_target_pairs={{0,16},{16,0},{1,17},{17,1},{2,18},{18,2},{3,19},{19,3},{4,20},{20... | collective-permute-start | bytes 1572872 | tf_op jit(solution)/shard_map/ppermute | solution.py:39
  309.9 20.4 %collective-permute-start.62 = (bf16[128,2048]{1,0:T(8,128)(2,1)S(1)}, bf16[128,2048]{1,0:T(8,128)(2,1)S(1)}, u32[]{:S(2)}, u32[]{:S(2)}) collective-permute-start(bf16[128,2048]{1,0:T(8,128)(2,1)S(1)} %add_convert_fusion.7), channel_id=1, source_target_pairs={{0,2},{2,0},{1,3},{3,1},{4,6},{6,4},{5,7},{7,5},{8,10},{10,8},{9,1... | collective-permute-start | bytes 1572872 | tf_op jit(solution)/shard_map/ppermute | solution.py:39
  309.9 18.2 %collective-permute-start.63 = (bf16[352,512]{1,0:T(8,128)(2,1)S(1)}, bf16[352,512]{1,0:T(8,128)(2,1)S(1)}, u32[]{:S(2)}, u32[]{:S(2)}) collective-permute-start(bf16[352,512]{1,0:T(8,128)(2,1)S(1)} %slice.338), channel_id=1, source_target_pairs={{0,4},{4,0},{1,5},{5,1},{2,6},{6,2},{3,7},{7,3},{8,12},{12,8},{9,1... | collective-permute-start | bytes 1081352 | tf_op jit(solution)/shard_map/ppermute | solution.py:39
  332.4 20.2 %collective-permute-start.65 = (bf16[128,2048]{1,0:T(8,128)(2,1)S(1)}, bf16[128,2048]{1,0:T(8,128)(2,1)S(1)}, u32[]{:S(2)}, u32[]{:S(2)}) collective-permute-start(bf16[128,2048]{1,0:T(8,128)(2,1)S(1)} %get-tuple-element.632), channel_id=1, source_target_pairs={{0,16},{16,0},{1,17},{17,1},{2,18},{18,2},{3,19},{19,3},{4,20},{20... | collective-permute-start | bytes 1572872 | tf_op jit(solution)/shard_map/ppermute | solution.py:39
  333.7 21.0 %collective-permute-start.66 = (bf16[128,2048]{1,0:T(8,128)(2,1)S(1)}, bf16[128,2048]{1,0:T(8,128)(2,1)S(1)}, u32[]{:S(2)}, u32[]{:S(2)}) collective-permute-start(bf16[128,2048]{1,0:T(8,128)(2,1)S(1)} %get-tuple-element.632), channel_id=1, source_target_pairs={{0,2},{2,0},{1,3},{3,1},{4,6},{6,4},{5,7},{7,5},{8,10},{10,8},{9,1... | collective-permute-start | bytes 1572872 | tf_op jit(solution)/shard_map/ppermute | solution.py:39
  334.2 18.3 %collective-permute-start.67 = (bf16[256,768]{1,0:T(8,128)(2,1)S(1)}, bf16[256,768]{1,0:T(8,128)(2,1)S(1)}, u32[]{:S(2)}, u32[]{:S(2)}) collective-permute-start(bf16[256,768]{1,0:T(8,128)(2,1)S(1)} %slice.341), channel_id=1, source_target_pairs={{0,4},{4,0},{1,5},{5,1},{2,6},{6,2},{3,7},{7,3},{8,12},{12,8},{9,1... | collective-permute-start | bytes 1179656 | tf_op jit(solution)/shard_map/ppermute | solution.py:39
  336.0 18.8 %collective-permute-start.68 = (bf16[512,768]{1,0:T(8,128)(2,1)S(1)}, bf16[512,768]{1,0:T(8,128)(2,1)S(1)}, u32[]{:S(2)}, u32[]{:S(2)}) collective-permute-start(bf16[512,768]{1,0:T(8,128)(2,1)S(1)} %convolution_convert_fusion.4), channel_id=1, source_target_pairs={{0,1},{1,0},{2,3},{3,2},{4,5},{5,4},{6,7},{7,6},{8,9},{9,8},{10,11... | collective-permute-start | bytes 2359304 | tf_op jit(solution)/shard_map/ppermute | solution.py:39
  378.2 16.8 %collective-permute-start.76 = (bf16[192,768]{1,0:T(8,128)(2,1)S(1)}, bf16[192,768]{1,0:T(8,128)(2,1)S(1)}, u32[]{:S(2)}, u32[]{:S(2)}) collective-permute-start(bf16[192,768]{1,0:T(8,128)(2,1)S(1)} %pad_maximum_fusion.15), channel_id=1, source_target_pairs={{0,4},{4,0},{1,5},{5,1},{2,6},{6,2},{3,7},{7,3},{8,12},{12,8},{9,1... | collective-permute-start | bytes 884744 | tf_op jit(solution)/shard_map/ppermute | solution.py:39
  378.3 16.7 %collective-permute-start.77 = (bf16[256,768]{1,0:T(8,128)(2,1)S(1)}, bf16[256,768]{1,0:T(8,128)(2,1)S(1)}, u32[]{:S(2)}, u32[]{:S(2)}) collective-permute-start(bf16[256,768]{1,0:T(8,128)(2,1)S(1)} %get-tuple-element.671), channel_id=1, source_target_pairs={{0,1},{1,0},{2,3},{3,2},{4,5},{5,4},{6,7},{7,6},{8,9},{9,8},{10,11... | collective-permute-start | bytes 1179656 | tf_op jit(solution)/shard_map/ppermute | solution.py:39
  378.9 16.1 %collective-permute-start.78 = (bf16[256,512]{1,0:T(8,128)(2,1)S(1)}, bf16[256,512]{1,0:T(8,128)(2,1)S(1)}, u32[]{:S(2)}, u32[]{:S(2)}) collective-permute-start(bf16[256,512]{1,0:T(8,128)(2,1)S(1)} %slice.355), channel_id=1, source_target_pairs={{0,1},{1,0},{2,3},{3,2},{4,5},{5,4},{6,7},{7,6},{8,9},{9,8},{10,11... | collective-permute-start | bytes 786440 | tf_op jit(solution)/shard_map/ppermute | solution.py:39
  396.0 15.9 %collective-permute-start.80 = (bf16[1024,256]{1,0:T(8,128)(2,1)S(1)}, bf16[1024,256]{1,0:T(8,128)(2,1)S(1)}, u32[]{:S(2)}, u32[]{:S(2)}) collective-permute-start(bf16[1024,256]{1,0:T(8,128)(2,1)S(1)} %get-tuple-element.682), channel_id=1, source_target_pairs={{0,1},{1,0},{2,3},{3,2},{4,5},{5,4},{6,7},{7,6},{8,9},{9,8},{10,11... | collective-permute-start | bytes 1572872 | tf_op jit(solution)/shard_map/ppermute | solution.py:39
  413.7 29.0 %collective-permute-start.84 = (bf16[1024,256]{1,0:T(8,128)(2,1)S(1)}, bf16[1024,256]{1,0:T(8,128)(2,1)S(1)}, u32[]{:S(2)}, u32[]{:S(2)}) collective-permute-start(bf16[1024,256]{1,0:T(8,128)(2,1)S(1)} %add_convert_fusion.6), channel_id=1, source_target_pairs={{0,4},{4,0},{1,5},{5,1},{2,6},{6,2},{3,7},{7,3},{8,12},{12,8},{9,1... | collective-permute-start | bytes 1572872 | tf_op jit(solution)/shard_map/ppermute | solution.py:39
  420.8 21.8 %collective-permute-start.85 = (bf16[128,2048]{1,0:T(8,128)(2,1)S(1)}, bf16[128,2048]{1,0:T(8,128)(2,1)S(1)}, u32[]{:S(2)}, u32[]{:S(2)}) collective-permute-start(bf16[128,2048]{1,0:T(8,128)(2,1)S(1)} %get-tuple-element.697), channel_id=1, source_target_pairs={{0,16},{16,0},{1,17},{17,1},{2,18},{18,2},{3,19},{19,3},{4,20},{20... | collective-permute-start | bytes 1572872 | tf_op jit(solution)/shard_map/ppermute | solution.py:39
  422.2 21.4 %collective-permute-start.86 = (bf16[128,2048]{1,0:T(8,128)(2,1)S(1)}, bf16[128,2048]{1,0:T(8,128)(2,1)S(1)}, u32[]{:S(2)}, u32[]{:S(2)}) collective-permute-start(bf16[128,2048]{1,0:T(8,128)(2,1)S(1)} %add_convert_fusion.5), channel_id=1, source_target_pairs={{0,2},{2,0},{1,3},{3,1},{4,6},{6,4},{5,7},{7,5},{8,10},{10,8},{9,1... | collective-permute-start | bytes 1572872 | tf_op jit(solution)/shard_map/ppermute | solution.py:39
  466.4 21.4 %collective-permute-start.91 = (bf16[512,2048]{1,0:T(8,128)(2,1)}, bf16[512,2048]{1,0:T(8,128)(2,1)}, u32[]{:S(2)}, u32[]{:S(2)}) collective-permute-start(bf16[512,2048]{1,0:T(8,128)(2,1)} %convolution_convert_fusion.1), channel_id=1, source_target_pairs={{0,8},{8,0},{1,9},{9,1},{2,10},{10,2},{3,11},{11,3},{4,12},{12,4},... | collective-permute-start | bytes 6291464 | tf_op jit(solution)/shard_map/ppermute | solution.py:39
  466.4 18.8 %collective-permute-start.95 = (bf16[768,256]{1,0:T(8,128)(2,1)}, bf16[768,256]{1,0:T(8,128)(2,1)}, u32[]{:S(2)}, u32[]{:S(2)}) collective-permute-start(bf16[768,256]{1,0:T(8,128)(2,1)} %select_convert_fusion.1), channel_id=1, source_target_pairs={{0,2},{2,0},{1,3},{3,1},{4,6},{6,4},{5,7},{7,5},{8,10},{10,8},{9,1... | collective-permute-start | bytes 1179656 | tf_op jit(solution)/shard_map/ppermute | solution.py:39
  506.7 19.8 %collective-permute-start.98 = (bf16[128,2048]{1,0:T(8,128)(2,1)S(1)}, bf16[128,2048]{1,0:T(8,128)(2,1)S(1)}, u32[]{:S(2)}, u32[]{:S(2)}) collective-permute-start(bf16[128,2048]{1,0:T(8,128)(2,1)S(1)} %slice.543), channel_id=1, source_target_pairs={{0,16},{16,0},{1,17},{17,1},{2,18},{18,2},{3,19},{19,3},{4,20},{20... | collective-permute-start | bytes 1572872 | tf_op jit(solution)/shard_map/ppermute | solution.py:39
  507.5 19.5 %collective-permute-start.99 = (bf16[128,2048]{1,0:T(8,128)(2,1)S(1)}, bf16[128,2048]{1,0:T(8,128)(2,1)S(1)}, u32[]{:S(2)}, u32[]{:S(2)}) collective-permute-start(bf16[128,2048]{1,0:T(8,128)(2,1)S(1)} %add_convert_fusion.3), channel_id=1, source_target_pairs={{0,2},{2,0},{1,3},{3,1},{4,6},{6,4},{5,7},{7,5},{8,10},{10,8},{9,1... | collective-permute-start | bytes 1572872 | tf_op jit(solution)/shard_map/ppermute | solution.py:39
  507.5 19.5 %collective-permute-start.100 = (bf16[512,512]{1,0:T(8,128)(2,1)S(1)}, bf16[512,512]{1,0:T(8,128)(2,1)S(1)}, u32[]{:S(2)}, u32[]{:S(2)}) collective-permute-start(bf16[512,512]{1,0:T(8,128)(2,1)S(1)} %copy-done.68), channel_id=1, source_target_pairs={{0,1},{1,0},{2,3},{3,2},{4,5},{5,4},{6,7},{7,6},{8,9},{9,8},{10,11... | collective-permute-start | bytes 1572872 | tf_op jit(solution)/shard_map/ppermute | solution.py:39
  508.8 17.7 %collective-permute-start.103 = (bf16[256,512]{1,0:T(8,128)(2,1)S(1)}, bf16[256,512]{1,0:T(8,128)(2,1)S(1)}, u32[]{:S(2)}, u32[]{:S(2)}) collective-permute-start(bf16[256,512]{1,0:T(8,128)(2,1)S(1)} %fusion.6), channel_id=1, source_target_pairs={{0,4},{4,0},{1,5},{5,1},{2,6},{6,2},{3,7},{7,3},{8,12},{12,8},{9,1... | collective-permute-start | bytes 786440 | tf_op jit(solution)/shard_map/ppermute | solution.py:39
  530.4 18.2 %collective-permute-start.110 = (bf16[256,768]{1,0:T(8,128)(2,1)S(1)}, bf16[256,768]{1,0:T(8,128)(2,1)S(1)}, u32[]{:S(2)}, u32[]{:S(2)}) collective-permute-start(bf16[256,768]{1,0:T(8,128)(2,1)S(1)} %select_convert_fusion), channel_id=1, source_target_pairs={{0,2},{2,0},{1,3},{3,1},{4,6},{6,4},{5,7},{7,5},{8,10},{10,8},{9,1... | collective-permute-start | bytes 1179656 | tf_op jit(solution)/shard_map/ppermute | solution.py:39
  (145 other events, 1505.9 us)

commit v3 on v2

--- a/solution.py
+++ b/solution.py
@@ -930,17 +930,23 @@
         token, (given, low, kv_low, k_gain_part, w_3, q_1, gate_give, up_1c, up_2b)
     )
     given_low = given
-    kv_late, normed, low = after(token, (kv_low, normed, low))
+    kv_late, normed, low, up_low = after(token, (kv_low, normed, low, up_low))
+    up_part = (
+        contract_rows(columns_of(mlp_rows, 0), up_low)
+        + jnp.concatenate([up_2a, up_2b], axis=0).astype(F32)
+        + jnp.concatenate([up_1a, up_1b, up_1c], axis=0).astype(F32)
+    )
+    up_mine, up_give = za_parts(up_part, 0)
     given, q_1, w_3, o_3 = trade(token, [(given, "core"), (q_1, "zb"), (w_3, "x"), (o_3, "x")])
     terms = contract_cols(low[:middle], qkv_cols)
     w_1 = contract_rows(columns_of(normed, 1), kv_late)
-    token, (given, terms, q_1, w_3, o_3, w_1, down_give, up_low, attn_low, branch_rows) = meet(
-        token, (given, terms, q_1, w_3, o_3, w_1, down_give, up_low, attn_low, branch_rows)
+    token, (given, terms, q_1, w_3, o_3, w_1, down_give, up_mine, up_give, attn_low, branch_rows) = meet(
+        token, (given, terms, q_1, w_3, o_3, w_1, down_give, up_mine, up_give, attn_low, branch_rows)
     )
     kept = terms + given.astype(F32)
     w_1 = (w_1 + w_3.astype(F32)).astype(BF16)
     token, (kept, w_1) = meet(token, (kept, w_1))
-    from_y, w_1 = trade(token, far_sums(kept) + [(w_1, "zb")])
+    from_y, w_1, up_give = trade(token, far_sums(kept) + [(w_1, "zb"), (up_give, "za")])
     o_1 = (contract_rows(attn_low, columns_of(branch_rows, 1)) + o_3.astype(F32)).astype(BF16)
     o_2 = contract_rows(attn_low, columns_of(branch_rows, 2)).astype(BF16)
     terms_low, given_low, normed_low = after(token, (terms, given_low, normed))
@@ -961,8 +967,8 @@
         axis=1,
     )
     qw_2 = contract_rows(columns_of(normed, 2), low).astype(BF16)
-    token, (from_y, kept, w_1, o_1, qw_2, o_2, gain_sum, up_low, attn_low, branch_rows, low) = meet(
-        token, (from_y, kept, w_1, o_1, qw_2, o_2, gain_sum, up_low, attn_low, branch_rows, low)
+    token, (from_y, kept, w_1, o_1, qw_2, o_2, gain_sum, up_give, attn_low, branch_rows, low) = meet(
+        token, (from_y, kept, w_1, o_1, qw_2, o_2, gain_sum, up_give, attn_low, branch_rows, low)
     )
     *nears, o_1, qw_2, gain_x = trade(
         token, near_sums(kept, from_y) + [(o_1, "zb"), (qw_2, "x"), (gain_sum, "core")]
@@ -970,22 +976,16 @@
     gain_sum = gain_sum + gain_x
     gain_sum = gain_sum + swap(gain_sum, "zb")
     gate_mine, gate_give, down_mine, down_give = after(token, (gate_mine, gate_give, down_mine, down_give))
-    up_part = (
-        contract_rows(columns_of(mlp_rows, 0), up_low)
-        + jnp.concatenate([up_2a, up_2b], axis=0).astype(F32)
-        + jnp.concatenate([up_1a, up_1b, up_1c], axis=0).astype(F32)
-    )
-    up_mine, up_give = za_parts(up_part, 0)
     qw_0 = contract_rows(columns_of(normed, 0), low)
     o_0 = contract_rows(attn_low, columns_of(branch_rows, 0))
     block_out = residual + own_sum(out_kept, out_nears)
-    token, (nears, kept, qw_2, qw_0, o_0, block_out, gain_sum, o_1, up_mine, up_give) = meet(
-        token, (nears, kept, qw_2, qw_0, o_0, block_out, gain_sum, o_1, up_mine, up_give)
+    token, (nears, kept, qw_2, qw_0, o_0, block_out, gain_sum, o_1) = meet(
+        token, (nears, kept, qw_2, qw_0, o_0, block_out, gain_sum, o_1)
     )
     qkv_mine, qkv_give = za_parts(qw_0 + qw_2.astype(F32) + jnp.concatenate([q_1, w_1], axis=1).astype(F32), 0)
     token, (qkv_mine, qkv_give) = meet(token, (qkv_mine, qkv_give))
-    gain_x, qkv_give, up_give, o_2 = trade(
-        token, [(gain_sum, "za"), (qkv_give, "za"), (up_give, "za"), (o_2, "x")]
+    gain_x, qkv_give, o_2 = trade(
+        token, [(gain_sum, "za"), (qkv_give, "za"), (o_2, "x")]
     )
     gain_sum = gain_sum + gain_x
     gain_x = swap(gain_sum, "y")

time: 558 us -> 553 us (level)
  starting transfers between devices: 132 us -> 117 us
  waiting for transfers between devices: 252 us -> 242 us
  local copies, waits for them, and re-layouts: 18.2 us -> 25.6 us
    ppermute x111, starting transfers between devices: 132 us -> 117 us  [swap(): return lax.ppermute(value, axis, SWAP)]
    ppermute x111, waiting for transfers between devices: 252 us -> 242 us  [swap(): return lax.ppermute(value, axis, SWAP)]
    unnamed x180 -> x208, local copies, waits for them, and re-layouts: 11.3 us -> 17 us
  transfers between devices with their start and end apart: 111 -> 111, of which waited for: 57 -> 50; matrix products, arithmetic and copies ran while one was open for 16% -> 17% of each run, Pallas kernels for 8% -> 9%
where the time goes in v3:
time: 553 us; the launch traced here: 543 us
  waiting for transfers between devices  242 us (44%)
  starting transfers between devices  117 us (21%)
  matrix products  54.3 us (10%)
  Pallas kernels  53.1 us (10%)
  other arithmetic  47.1 us (9%)
  local copies, waits for them, and re-layouts  25.6 us (5%)
    ppermute x111, waiting for transfers between devices, swap(): return lax.ppermute(value, axis, SWAP)  242 us
    ppermute x111, starting transfers between devices, swap(): return lax.ppermute(value, axis, SWAP)  117 us
    dot_general x22, matrix products, contract_rows(): lax.dot_general(left, right, PAIRS_OF_ROWS, preferred_element_type=F32)  29.3 us
    unnamed x208, local copies, waits for them, and re-layouts  17 us
    pallas_call x2, Pallas kernels, attend_back(): pl.pallas_call(functools.partial(attend_back_kernel, parts=parts, first=f...  17 us
    dot_general x7, matrix products, matmul(): return jnp.dot(left, right, preferred_element_type=F32)  14.6 us
    pallas_call x2, Pallas kernels, attend(): pl.pallas_call(functools.partial(attend_kernel, parts=parts, first=first,...  11.2 us
  transfers between devices with their start and end apart: 111, of which 50 were waited for; matrix products, arithmetic and copies ran while one was open for 17% of the time, Pallas kernels for 9%

profile of v3, /device:TPU:0, one launch (start us, length us, event | category | flops | bytes accessed | tf_op | source)
XLA Modules:
  0.0 542.7 jit_solution(17203887485015386692)
XLA Ops:
  1.8 3.3 prologue.1
  5.1 4.0 collective-permute-start.1
  21.4 4.9 collective-permute-done.4
  37.2 3.4 collective-permute-done.5
  40.5 4.5 collective-permute-done.8
  45.1 5.6 %collective-permute-done.9.refs_4_ = bf16[768,256]{1,0:T(8,128)(2,1)S(1)} collective-permute-done((bf16[768,256]{1,0:T(8,128)(2,1)S(1)}, bf16[768,256]{1,0:T(8,128)(2,1)S(1)}, u32[]{:S(2)}, u32[]{:S(2)}) %collective-permute-start.9) | collective-permute-done | bytes 393248 | tf_op jit(solution)/shard_map/ppermute | solution.py:39
  57.4 3.0 collective-permute-done.12
  61.9 3.2 collective-permute-done.14
  66.6 2.7 collective-permute-start.17
  78.6 4.4 collective-permute-done.17
  87.3 9.3 %collective-permute-done.19.refs_1_ = bf16[1024,256]{1,0:T(8,128)(2,1)S(1)} collective-permute-done((bf16[1024,256]{1,0:T(8,128)(2,1)S(1)}, bf16[1024,256]{1,0:T(8,128)(2,1)S(1)}, u32[]{:S(2)}, u32[]{:S(2)}) %collective-permute-start.19) | collective-permute-done | bytes 524320 | tf_op jit(solution)/shard_map/ppermute | solution.py:39
  98.2 6.7 %attend.2.refs_2_ = f32[8,256,256]{2,1,0:T(8,128)S(1)} custom-call(s32[32]{0:T(128)S(1)} %broadcast_add_fusion.1.off_ref, s32[8]{0:T(128)S(1)} %get-tuple-element.834.tile_ref, s32[8]{0:T(128)S(1)} %and_select_fusion.low_ref, bf16[1024,256]{1,0:T(8,128)(2,1)S(1)} %get-tuple-element.462.q_ref, s32[1024,128]{1,0:T(8,128)S(1)} %broadcast_in_dim.115.start_ref, ...), custom_call_target="tpu_custom_call" | custom-call | flops 1000 | bytes 1000 | tf_op jit(solution)/shard_map/attend/pallas_call | solution.py:195
  104.9 4.2 collective-permute-done.20.refs_0_
  112.9 10.1 %collective-permute-done.24.refs_1_ = bf16[1024,256]{1,0:T(8,128)(2,1)S(1)} collective-permute-done((bf16[1024,256]{1,0:T(8,128)(2,1)S(1)}, bf16[1024,256]{1,0:T(8,128)(2,1)S(1)}, u32[]{:S(2)}, u32[]{:S(2)}) %collective-permute-start.24) | collective-permute-done | bytes 524320 | tf_op jit(solution)/shard_map/ppermute | solution.py:39
  124.0 4.5 attend.3
  129.2 4.9 collective-permute-done.27
  134.1 4.0 collective-permute-done.26
  143.0 8.8 %collective-permute-done.29 = bf16[96,768]{1,0:T(8,128)(2,1)S(1)} collective-permute-done((bf16[96,768]{1,0:T(8,128)(2,1)S(1)}, bf16[96,768]{1,0:T(8,128)(2,1)S(1)}, u32[]{:S(2)}, u32[]{:S(2)}) %collective-permute-start.29) | collective-permute-done | bytes 147488 | tf_op jit(solution)/shard_map/ppermute | solution.py:39
  159.0 11.1 %collective-permute-done.35 = bf16[160,768]{1,0:T(8,128)(2,1)S(1)} collective-permute-done((bf16[160,768]{1,0:T(8,128)(2,1)S(1)}, bf16[160,768]{1,0:T(8,128)(2,1)S(1)}, u32[]{:S(2)}, u32[]{:S(2)}) %collective-permute-start.35) | collective-permute-done | bytes 245792 | tf_op jit(solution)/shard_map/ppermute | solution.py:39
  174.5 17.6 %collective-permute-done.39.refs_2_ = bf16[256,768]{1,0:T(8,128)(2,1)S(1)} collective-permute-done((bf16[256,768]{1,0:T(8,128)(2,1)S(1)}, bf16[256,768]{1,0:T(8,128)(2,1)S(1)}, u32[]{:S(2)}, u32[]{:S(2)}) %collective-permute-start.39) | collective-permute-done | bytes 393248 | tf_op jit(solution)/shard_map/ppermute | solution.py:39
  201.5 7.7 %collective-permute-done.43.refs_5_ = bf16[768,256]{1,0:T(8,128)(2,1)S(1)} collective-permute-done((bf16[768,256]{1,0:T(8,128)(2,1)S(1)}, bf16[768,256]{1,0:T(8,128)(2,1)S(1)}, u32[]{:S(2)}, u32[]{:S(2)}) %collective-permute-start.43) | collective-permute-done | bytes 393248 | tf_op jit(solution)/shard_map/ppermute | solution.py:39
  209.1 6.2 %collective-permute-done.44.refs_5_ = bf16[256,768]{1,0:T(8,128)(2,1)S(1)} collective-permute-done((bf16[256,768]{1,0:T(8,128)(2,1)S(1)}, bf16[256,768]{1,0:T(8,128)(2,1)S(1)}, u32[]{:S(2)}, u32[]{:S(2)}) %collective-permute-start.44) | collective-permute-done | bytes 393248 | tf_op jit(solution)/shard_map/ppermute | solution.py:39
  223.3 6.2 %collective-permute-done.48 = bf16[400,256]{1,0:T(8,128)(2,1)S(1)} collective-permute-done((bf16[400,256]{1,0:T(8,128)(2,1)S(1)}, bf16[400,256]{1,0:T(8,128)(2,1)S(1)}, u32[]{:S(2)}, u32[]{:S(2)}) %collective-permute-start.48) | collective-permute-done | bytes 204832 | tf_op jit(solution)/shard_map/ppermute | solution.py:39
  234.0 3.4 fusion.81
  238.7 3.8 multiply_convert_fusion.2
  242.6 4.2 collective-permute-done.53
  249.5 3.2 collective-permute-done.54
  254.0 4.9 multiply_convert_fusion
  258.9 10.8 %two_terms.1 = (f32[512,2048]{1,0:T(8,128)}, bf16[512,2048]{1,0:T(8,128)(2,1)}) custom-call(bf16[1024,768]{1,0:T(8,128)(2,1)} %get-tuple-element.652.left_ref, bf16[1024,768]{1,0:T(8,128)(2,1)} %get-tuple-element.742.right_ref, bf16[2048,768]{1,0:T(8,128)(2,1)} %copy-done.2, bf16[2048,768]{1,0:T(8,128)(2,1)} %copy-done.3), custom_call_target="tpu_custom_call" | custom-call | flops 1000 | bytes 1000 | tf_op jit(solution)/shard_map/two_terms/pallas_call | solution.py:384
  271.4 2.8 fusion.27
  279.6 6.6 %collective-permute-done.57 = bf16[144,512]{1,0:T(8,128)(2,1)S(1)} collective-permute-done((bf16[144,512]{1,0:T(8,128)(2,1)S(1)}, bf16[144,512]{1,0:T(8,128)(2,1)S(1)}, u32[]{:S(2)}, u32[]{:S(2)}) %collective-permute-start.57) | collective-permute-done | bytes 147488 | tf_op jit(solution)/shard_map/ppermute | solution.py:39
  292.9 12.5 %collective-permute-done.59 = bf16[272,512]{1,0:T(8,128)(2,1)S(1)} collective-permute-done((bf16[272,512]{1,0:T(8,128)(2,1)S(1)}, bf16[272,512]{1,0:T(8,128)(2,1)S(1)}, u32[]{:S(2)}, u32[]{:S(2)}) %collective-permute-start.59) | collective-permute-done | bytes 278560 | tf_op jit(solution)/shard_map/ppermute | solution.py:39
  313.6 14.3 %collective-permute-done.63 = bf16[352,512]{1,0:T(8,128)(2,1)S(1)} collective-permute-done((bf16[352,512]{1,0:T(8,128)(2,1)S(1)}, bf16[352,512]{1,0:T(8,128)(2,1)S(1)}, u32[]{:S(2)}, u32[]{:S(2)}) %collective-permute-start.63) | collective-permute-done | bytes 360480 | tf_op jit(solution)/shard_map/ppermute | solution.py:39
  341.3 11.3 %collective-permute-done.67 = bf16[256,768]{1,0:T(8,128)(2,1)S(1)} collective-permute-done((bf16[256,768]{1,0:T(8,128)(2,1)S(1)}, bf16[256,768]{1,0:T(8,128)(2,1)S(1)}, u32[]{:S(2)}, u32[]{:S(2)}) %collective-permute-start.67) | collective-permute-done | bytes 393248 | tf_op jit(solution)/shard_map/ppermute | solution.py:39
  363.2 3.0 collective-permute-done.71
  374.3 3.8 collective-permute-done.74
  381.1 6.1 %attend_back.2 = (f32[1024,256]{1,0:T(8,128)S(1)}, bf16[1024,256]{1,0:T(8,128)(2,1)S(1)}, bf16[1024,256]{1,0:T(8,128)(2,1)S(1)}) custom-call(s32[32]{0:T(128)S(1)} %broadcast_add_fusion.off_ref, s32[8]{0:T(128)S(1)} %get-tuple-element.834.tile_ref, s32[8]{0:T(128)S(1)} %and_select_fusion.low_ref, bf16[1024,256]{1,0:T(8,128)(2,1)S(1)} %get-tuple-element.462.q_ref, ...), custom_call_target="tpu_custom_call" | custom-call | flops 1000 | bytes 1000 | tf_op jit(solution)/shard_map/attend_back/pallas_call | solution.py:213
  387.2 7.6 %collective-permute-done.78 = bf16[256,512]{1,0:T(8,128)(2,1)S(1)} collective-permute-done((bf16[256,512]{1,0:T(8,128)(2,1)S(1)}, bf16[256,512]{1,0:T(8,128)(2,1)S(1)}, u32[]{:S(2)}, u32[]{:S(2)}) %collective-permute-start.78) | collective-permute-done | bytes 262176 | tf_op jit(solution)/shard_map/ppermute | solution.py:39
  401.3 10.9 %attend_back.3 = (bf16[1024,256]{1,0:T(8,128)(2,1)S(1)}, bf16[1024,256]{1,0:T(8,128)(2,1)S(1)}, bf16[1024,256]{1,0:T(8,128)(2,1)}) custom-call(s32[32]{0:T(128)S(1)} %broadcast_add_fusion.1.off_ref, s32[8]{0:T(128)S(1)} %get-tuple-element.834.tile_ref, s32[8]{0:T(128)S(1)} %and_select_fusion.low_ref, bf16[1024,256]{1,0:T(8,128)(2,1)S(1)} %get-tuple-element.462.q_ref, ...), custom_call_target="tpu_custom_call" | custom-call | flops 1000 | bytes 1000 | tf_op jit(solution)/shard_map/attend_back/pallas_call | solution.py:213
  420.2 7.8 %collective-permute-done.83 = bf16[1024,256]{1,0:T(8,128)(2,1)} collective-permute-done((bf16[1024,256]{1,0:T(8,128)(2,1)}, bf16[1024,256]{1,0:T(8,128)(2,1)}, u32[]{:S(2)}, u32[]{:S(2)}) %collective-permute-start.83) | collective-permute-done | bytes 524320 | tf_op jit(solution)/shard_map/ppermute | solution.py:39
  453.2 4.0 collective-permute-done.87
  458.0 6.8 %collective-permute-done.89 = bf16[176,768]{1,0:T(8,128)(2,1)S(1)} collective-permute-done((bf16[176,768]{1,0:T(8,128)(2,1)S(1)}, bf16[176,768]{1,0:T(8,128)(2,1)S(1)}, u32[]{:S(2)}, u32[]{:S(2)}) %collective-permute-start.89) | collective-permute-done | bytes 270368 | tf_op jit(solution)/shard_map/ppermute | solution.py:39
  468.1 3.4 collective-permute-start.92
  491.6 2.8 add_reduce_fusion
  497.3 4.4 collective-permute-done.97
  501.7 3.0 collective-permute-done.98
  518.1 6.2 %collective-permute-done.103 = f32[1,4352]{1,0:T(1,128)S(1)} collective-permute-done((f32[1,4352]{1,0:T(1,128)S(1)}, f32[1,4352]{1,0:T(1,128)S(1)}, u32[]{:S(2)}, u32[]{:S(2)}) %collective-permute-start.103) | collective-permute-done | bytes 17440 | tf_op jit(solution)/shard_map/ppermute | solution.py:39
  531.1 3.5 reorder.3
  (612 shorter events, 248.2 us)
Async XLA Ops:
  5.1 21.3 %collective-permute-start.1 = (bf16[272,512]{1,0:T(8,128)(2,1)}, bf16[272,512]{1,0:T(8,128)(2,1)S(1)}, u32[]{:S(2)}, u32[]{:S(2)}) collective-permute-start(bf16[272,512]{1,0:T(8,128)(2,1)} %get-tuple-element.419), channel_id=1, source_target_pairs={{0,4},{4,0},{1,5},{5,1},{2,6},{6,2},{3,7},{7,3},{8,12},{12,8},{9,1... | collective-permute-start | bytes 835592 | tf_op jit(solution)/shard_map/ppermute | solution.py:39
  9.1 17.3 %collective-permute-start.2 = (bf16[272,512]{1,0:T(8,128)(2,1)}, bf16[272,512]{1,0:T(8,128)(2,1)S(1)}, u32[]{:S(2)}, u32[]{:S(2)}) collective-permute-start(bf16[272,512]{1,0:T(8,128)(2,1)} %get-tuple-element.419), channel_id=1, source_target_pairs={{0,1},{1,0},{2,3},{3,2},{4,5},{5,4},{6,7},{7,6},{8,9},{9,8},{10,11... | collective-permute-start | bytes 835592 | tf_op jit(solution)/shard_map/ppermute | solution.py:39
  10.6 15.8 %collective-permute-start = (bf16[272,512]{1,0:T(8,128)(2,1)}, bf16[272,512]{1,0:T(8,128)(2,1)}, u32[]{:S(2)}, u32[]{:S(2)}) collective-permute-start(bf16[272,512]{1,0:T(8,128)(2,1)} %get-tuple-element.418), channel_id=1, source_target_pairs={{0,2},{2,0},{1,3},{3,1},{4,6},{6,4},{5,7},{7,5},{8,10},{10,8},{9,1... | collective-permute-start | bytes 835592 | tf_op jit(solution)/shard_map/ppermute | solution.py:39
  27.0 23.6 %collective-permute-start.6 = (bf16[128,2048]{1,0:T(8,128)(2,1)S(1)}, bf16[128,2048]{1,0:T(8,128)(2,1)S(1)}, u32[]{:S(2)}, u32[]{:S(2)}) collective-permute-start(bf16[128,2048]{1,0:T(8,128)(2,1)S(1)} %copy-done.38), channel_id=1, source_target_pairs={{0,2},{2,0},{1,3},{3,1},{4,6},{6,4},{5,7},{7,5},{8,10},{10,8},{9,1... | collective-permute-start | bytes 1572872 | tf_op jit(solution)/shard_map/ppermute | solution.py:39
  31.5 19.1 %collective-permute-start.9 = (bf16[768,256]{1,0:T(8,128)(2,1)S(1)}, bf16[768,256]{1,0:T(8,128)(2,1)S(1)}, u32[]{:S(2)}, u32[]{:S(2)}) collective-permute-start(bf16[768,256]{1,0:T(8,128)(2,1)S(1)} %constant_dynamic-slice_fusion.9.refs_0_), channel_id=1, source_target_pairs={{0,1},{1,0},{2,3},{3,2},{4,5},{5,4},{6,7},{7,6},{8,9},{9,8},{10,11... | collective-permute-start | bytes 1179656 | tf_op jit(solution)/shard_map/ppermute | solution.py:39
  66.6 16.4 %collective-permute-start.17 = (bf16[256,768]{1,0:T(8,128)(2,1)S(1)}, bf16[256,768]{1,0:T(8,128)(2,1)S(1)}, u32[]{:S(2)}, u32[]{:S(2)}) collective-permute-start(bf16[256,768]{1,0:T(8,128)(2,1)S(1)} %get-tuple-element.453), channel_id=1, source_target_pairs={{0,2},{2,0},{1,3},{3,1},{4,6},{6,4},{5,7},{7,5},{8,10},{10,8},{9,1... | collective-permute-start | bytes 1179656 | tf_op jit(solution)/shard_map/ppermute | solution.py:39
  84.4 24.8 %collective-permute-start.20 = (bf16[1024,256]{1,0:T(8,128)(2,1)S(1)}, bf16[1024,256]{1,0:T(8,128)(2,1)S(1)}, u32[]{:S(2)}, u32[]{:S(2)}) collective-permute-start(bf16[1024,256]{1,0:T(8,128)(2,1)S(1)} %get-tuple-element.461.refs_0_), channel_id=1, source_target_pairs={{0,4},{4,0},{1,5},{5,1},{2,6},{6,2},{3,7},{7,3},{8,12},{12,8},{9,1... | collective-permute-start | bytes 1572872 | tf_op jit(solution)/shard_map/ppermute | solution.py:39
  84.7 24.4 %collective-permute-start.21 = (bf16[128,2048]{1,0:T(8,128)(2,1)S(1)}, bf16[128,2048]{1,0:T(8,128)(2,1)S(1)}, u32[]{:S(2)}, u32[]{:S(2)}) collective-permute-start(bf16[128,2048]{1,0:T(8,128)(2,1)S(1)} %copy-done.51), channel_id=1, source_target_pairs={{0,16},{16,0},{1,17},{17,1},{2,18},{18,2},{3,19},{19,3},{4,20},{20... | collective-permute-start | bytes 1572872 | tf_op jit(solution)/shard_map/ppermute | solution.py:39
  85.3 19.6 %collective-permute-start.23 = (bf16[256,768]{1,0:T(8,128)(2,1)S(1)}, bf16[256,768]{1,0:T(8,128)(2,1)S(1)}, u32[]{:S(2)}, u32[]{:S(2)}) collective-permute-start(bf16[256,768]{1,0:T(8,128)(2,1)S(1)} %constant_dynamic-slice_fusion.6), channel_id=1, source_target_pairs={{0,2},{2,0},{1,3},{3,1},{4,6},{6,4},{5,7},{7,5},{8,10},{10,8},{9,1... | collective-permute-start | bytes 1179656 | tf_op jit(solution)/shard_map/ppermute | solution.py:39
  110.0 28.1 %collective-permute-start.26 = (bf16[384,768]{1,0:T(8,128)(2,1)S(1)}, bf16[384,768]{1,0:T(8,128)(2,1)S(1)}, u32[]{:S(2)}, u32[]{:S(2)}) collective-permute-start(bf16[384,768]{1,0:T(8,128)(2,1)S(1)} %pad_maximum_fusion.7), channel_id=1, source_target_pairs={{0,4},{4,0},{1,5},{5,1},{2,6},{6,2},{3,7},{7,3},{8,12},{12,8},{9,1... | collective-permute-start | bytes 1769480 | tf_op jit(solution)/shard_map/ppermute | solution.py:39
  110.1 24.0 %collective-permute-start.27 = (bf16[128,2048]{1,0:T(8,128)(2,1)S(1)}, bf16[128,2048]{1,0:T(8,128)(2,1)S(1)}, u32[]{:S(2)}, u32[]{:S(2)}) collective-permute-start(bf16[128,2048]{1,0:T(8,128)(2,1)S(1)} %copy-done.51), channel_id=1, source_target_pairs={{0,2},{2,0},{1,3},{3,1},{4,6},{6,4},{5,7},{7,5},{8,10},{10,8},{9,1... | collective-permute-start | bytes 1572872 | tf_op jit(solution)/shard_map/ppermute | solution.py:39
  138.1 15.9 %collective-permute-start.28 = (bf16[512,2048]{1,0:T(8,128)(2,1)S(1)}, bf16[512,2048]{1,0:T(8,128)(2,1)S(1)}, u32[]{:S(2)}, u32[]{:S(2)}) collective-permute-start(bf16[512,2048]{1,0:T(8,128)(2,1)S(1)} %convolution_convert_fusion), channel_id=1, source_target_pairs={{0,8},{8,0},{1,9},{9,1},{2,10},{10,2},{3,11},{11,3},{4,12},{12,4},... | collective-permute-start | bytes 6291464 | tf_op jit(solution)/shard_map/ppermute | solution.py:39
  138.1 15.8 %collective-permute-start.31 = (bf16[128,2048]{1,0:T(8,128)(2,1)S(1)}, bf16[128,2048]{1,0:T(8,128)(2,1)S(1)}, u32[]{:S(2)}, u32[]{:S(2)}) collective-permute-start(bf16[128,2048]{1,0:T(8,128)(2,1)S(1)} %collective-permute-done.27), channel_id=1, source_target_pairs={{0,16},{16,0},{1,17},{17,1},{2,18},{18,2},{3,19},{19,3},{4,20},{20... | collective-permute-start | bytes 1572872 | tf_op jit(solution)/shard_map/ppermute | solution.py:39
  170.3 24.0 %collective-permute-start.40 = (bf16[512,2048]{1,0:T(8,128)(2,1)S(1)}, bf16[512,2048]{1,0:T(8,128)(2,1)S(1)}, u32[]{:S(2)}, u32[]{:S(2)}) collective-permute-start(bf16[512,2048]{1,0:T(8,128)(2,1)S(1)} %pad_maximum_fusion.refs_0_), channel_id=1, source_target_pairs={{0,8},{8,0},{1,9},{9,1},{2,10},{10,2},{3,11},{11,3},{4,12},{12,4},... | collective-permute-start | bytes 6291464 | tf_op jit(solution)/shard_map/ppermute | solution.py:39
  170.4 23.9 %collective-permute-start.38 = (bf16[512,768]{1,0:T(8,128)(2,1)S(1)}, bf16[512,768]{1,0:T(8,128)(2,1)S(1)}, u32[]{:S(2)}, u32[]{:S(2)}) collective-permute-start(bf16[512,768]{1,0:T(8,128)(2,1)S(1)} %assemble.5.refs_1_), channel_id=1, source_target_pairs={{0,1},{1,0},{2,3},{3,2},{4,5},{5,4},{6,7},{7,6},{8,9},{9,8},{10,11... | collective-permute-start | bytes 2359304 | tf_op jit(solution)/shard_map/ppermute | solution.py:39
  171.7 20.5 %collective-permute-start.36 = (bf16[128,2048]{1,0:T(8,128)(2,1)S(1)}, bf16[128,2048]{1,0:T(8,128)(2,1)S(1)}, u32[]{:S(2)}, u32[]{:S(2)}) collective-permute-start(bf16[128,2048]{1,0:T(8,128)(2,1)S(1)} %slice.547), channel_id=1, source_target_pairs={{0,16},{16,0},{1,17},{17,1},{2,18},{18,2},{3,19},{19,3},{4,20},{20... | collective-permute-start | bytes 1572872 | tf_op jit(solution)/shard_map/ppermute | solution.py:39
  172.2 22.1 %collective-permute-start.37 = (bf16[128,2048]{1,0:T(8,128)(2,1)S(1)}, bf16[128,2048]{1,0:T(8,128)(2,1)S(1)}, u32[]{:S(2)}, u32[]{:S(2)}) collective-permute-start(bf16[128,2048]{1,0:T(8,128)(2,1)S(1)} %add_convert_fusion.8), channel_id=1, source_target_pairs={{0,2},{2,0},{1,3},{3,1},{4,6},{6,4},{5,7},{7,5},{8,10},{10,8},{9,1... | collective-permute-start | bytes 1572872 | tf_op jit(solution)/shard_map/ppermute | solution.py:39
  172.2 19.9 %collective-permute-start.39 = (bf16[256,768]{1,0:T(8,128)(2,1)S(1)}, bf16[256,768]{1,0:T(8,128)(2,1)S(1)}, u32[]{:S(2)}, u32[]{:S(2)}) collective-permute-start(bf16[256,768]{1,0:T(8,128)(2,1)S(1)} %slice.317), channel_id=1, source_target_pairs={{0,4},{4,0},{1,5},{5,1},{2,6},{6,2},{3,7},{7,3},{8,12},{12,8},{9,1... | collective-permute-start | bytes 1179656 | tf_op jit(solution)/shard_map/ppermute | solution.py:39
  194.9 21.0 %collective-permute-start.41 = (bf16[128,2048]{1,0:T(8,128)(2,1)S(1)}, bf16[128,2048]{1,0:T(8,128)(2,1)S(1)}, u32[]{:S(2)}, u32[]{:S(2)}) collective-permute-start(bf16[128,2048]{1,0:T(8,128)(2,1)S(1)} %multiply_convert_fusion.4), channel_id=1, source_target_pairs={{0,16},{16,0},{1,17},{17,1},{2,18},{18,2},{3,19},{19,3},{4,20},{20... | collective-permute-start | bytes 1572872 | tf_op jit(solution)/shard_map/ppermute | solution.py:39
  196.5 21.1 %collective-permute-start.42 = (bf16[128,2048]{1,0:T(8,128)(2,1)S(1)}, bf16[128,2048]{1,0:T(8,128)(2,1)S(1)}, u32[]{:S(2)}, u32[]{:S(2)}) collective-permute-start(bf16[128,2048]{1,0:T(8,128)(2,1)S(1)} %multiply_convert_fusion.4), channel_id=1, source_target_pairs={{0,2},{2,0},{1,3},{3,1},{4,6},{6,4},{5,7},{7,5},{8,10},{10,8},{9,1... | collective-permute-start | bytes 1572872 | tf_op jit(solution)/shard_map/ppermute | solution.py:39
  197.9 17.5 %collective-permute-start.44 = (bf16[256,768]{1,0:T(8,128)(2,1)S(1)}, bf16[256,768]{1,0:T(8,128)(2,1)S(1)}, u32[]{:S(2)}, u32[]{:S(2)}) collective-permute-start(bf16[256,768]{1,0:T(8,128)(2,1)S(1)} %constant_dynamic-update-slice_fusion.11.refs_1_), channel_id=1, source_target_pairs={{0,1},{1,0},{2,3},{3,2},{4,5},{5,4},{6,7},{7,6},{8,9},{9,8},{10,11... | collective-permute-start | bytes 1179656 | tf_op jit(solution)/shard_map/ppermute | solution.py:39
  199.1 16.8 %collective-permute-start.45 = (bf16[768,256]{1,0:T(8,128)(2,1)S(1)}, bf16[768,256]{1,0:T(8,128)(2,1)S(1)}, u32[]{:S(2)}, u32[]{:S(2)}) collective-permute-start(bf16[768,256]{1,0:T(8,128)(2,1)S(1)} %constant_dynamic-slice_fusion.9.refs_0_), channel_id=1, source_target_pairs={{0,4},{4,0},{1,5},{5,1},{2,6},{6,2},{3,7},{7,3},{8,12},{12,8},{9,1... | collective-permute-start | bytes 1179656 | tf_op jit(solution)/shard_map/ppermute | solution.py:39
  253.2 18.2 %collective-permute-start.55 = (bf16[768,512]{1,0:T(8,128)(2,1)}, bf16[768,512]{1,0:T(8,128)(2,1)}, u32[]{:S(2)}, u32[]{:S(2)}) collective-permute-start(bf16[768,512]{1,0:T(8,128)(2,1)} %convolution_convert_fusion.8), channel_id=1, source_target_pairs={{0,1},{1,0},{2,3},{3,2},{4,5},{5,4},{6,7},{7,6},{8,9},{9,8},{10,11... | collective-permute-start | bytes 2359304 | tf_op jit(solution)/shard_map/ppermute | solution.py:39
  287.2 19.3 %collective-permute-start.60 = (bf16[512,768]{1,0:T(8,128)(2,1)S(1)}, bf16[512,768]{1,0:T(8,128)(2,1)S(1)}, u32[]{:S(2)}, u32[]{:S(2)}) collective-permute-start(bf16[512,768]{1,0:T(8,128)(2,1)S(1)} %convolution_convert_fusion.7), channel_id=1, source_target_pairs={{0,1},{1,0},{2,3},{3,2},{4,5},{5,4},{6,7},{7,6},{8,9},{9,8},{10,11... | collective-permute-start | bytes 2359304 | tf_op jit(solution)/shard_map/ppermute | solution.py:39
  289.1 16.3 %collective-permute-start.58 = (bf16[128,2048]{1,0:T(8,128)(2,1)S(1)}, bf16[128,2048]{1,0:T(8,128)(2,1)S(1)}, u32[]{:S(2)}, u32[]{:S(2)}) collective-permute-start(bf16[128,2048]{1,0:T(8,128)(2,1)S(1)} %slice.546), channel_id=1, source_target_pairs={{0,16},{16,0},{1,17},{17,1},{2,18},{18,2},{3,19},{19,3},{4,20},{20... | collective-permute-start | bytes 1572872 | tf_op jit(solution)/shard_map/ppermute | solution.py:39
  306.7 23.5 %collective-permute-start.64 = (bf16[512,768]{1,0:T(8,128)(2,1)S(1)}, bf16[512,768]{1,0:T(8,128)(2,1)S(1)}, u32[]{:S(2)}, u32[]{:S(2)}) collective-permute-start(bf16[512,768]{1,0:T(8,128)(2,1)S(1)} %convolution_convert_fusion.5), channel_id=1, source_target_pairs={{0,1},{1,0},{2,3},{3,2},{4,5},{5,4},{6,7},{7,6},{8,9},{9,8},{10,11... | collective-permute-start | bytes 2359304 | tf_op jit(solution)/shard_map/ppermute | solution.py:39
  308.6 19.3 %collective-permute-start.61 = (bf16[128,2048]{1,0:T(8,128)(2,1)S(1)}, bf16[128,2048]{1,0:T(8,128)(2,1)S(1)}, u32[]{:S(2)}, u32[]{:S(2)}) collective-permute-start(bf16[128,2048]{1,0:T(8,128)(2,1)S(1)} %slice.545), channel_id=1, source_target_pairs={{0,16},{16,0},{1,17},{17,1},{2,18},{18,2},{3,19},{19,3},{4,20},{20... | collective-permute-start | bytes 1572872 | tf_op jit(solution)/shard_map/ppermute | solution.py:39
  310.2 19.9 %collective-permute-start.62 = (bf16[128,2048]{1,0:T(8,128)(2,1)S(1)}, bf16[128,2048]{1,0:T(8,128)(2,1)S(1)}, u32[]{:S(2)}, u32[]{:S(2)}) collective-permute-start(bf16[128,2048]{1,0:T(8,128)(2,1)S(1)} %add_convert_fusion.7), channel_id=1, source_target_pairs={{0,2},{2,0},{1,3},{3,1},{4,6},{6,4},{5,7},{7,5},{8,10},{10,8},{9,1... | collective-permute-start | bytes 1572872 | tf_op jit(solution)/shard_map/ppermute | solution.py:39
  310.2 17.7 %collective-permute-start.63 = (bf16[352,512]{1,0:T(8,128)(2,1)S(1)}, bf16[352,512]{1,0:T(8,128)(2,1)S(1)}, u32[]{:S(2)}, u32[]{:S(2)}) collective-permute-start(bf16[352,512]{1,0:T(8,128)(2,1)S(1)} %slice.338), channel_id=1, source_target_pairs={{0,4},{4,0},{1,5},{5,1},{2,6},{6,2},{3,7},{7,3},{8,12},{12,8},{9,1... | collective-permute-start | bytes 1081352 | tf_op jit(solution)/shard_map/ppermute | solution.py:39
  332.3 20.3 %collective-permute-start.65 = (bf16[128,2048]{1,0:T(8,128)(2,1)S(1)}, bf16[128,2048]{1,0:T(8,128)(2,1)S(1)}, u32[]{:S(2)}, u32[]{:S(2)}) collective-permute-start(bf16[128,2048]{1,0:T(8,128)(2,1)S(1)} %get-tuple-element.632), channel_id=1, source_target_pairs={{0,16},{16,0},{1,17},{17,1},{2,18},{18,2},{3,19},{19,3},{4,20},{20... | collective-permute-start | bytes 1572872 | tf_op jit(solution)/shard_map/ppermute | solution.py:39
  333.2 21.0 %collective-permute-start.66 = (bf16[128,2048]{1,0:T(8,128)(2,1)S(1)}, bf16[128,2048]{1,0:T(8,128)(2,1)S(1)}, u32[]{:S(2)}, u32[]{:S(2)}) collective-permute-start(bf16[128,2048]{1,0:T(8,128)(2,1)S(1)} %get-tuple-element.632), channel_id=1, source_target_pairs={{0,2},{2,0},{1,3},{3,1},{4,6},{6,4},{5,7},{7,5},{8,10},{10,8},{9,1... | collective-permute-start | bytes 1572872 | tf_op jit(solution)/shard_map/ppermute | solution.py:39
  334.3 18.3 %collective-permute-start.67 = (bf16[256,768]{1,0:T(8,128)(2,1)S(1)}, bf16[256,768]{1,0:T(8,128)(2,1)S(1)}, u32[]{:S(2)}, u32[]{:S(2)}) collective-permute-start(bf16[256,768]{1,0:T(8,128)(2,1)S(1)} %slice.341), channel_id=1, source_target_pairs={{0,4},{4,0},{1,5},{5,1},{2,6},{6,2},{3,7},{7,3},{8,12},{12,8},{9,1... | collective-permute-start | bytes 1179656 | tf_op jit(solution)/shard_map/ppermute | solution.py:39
  336.0 18.3 %collective-permute-start.68 = (bf16[512,768]{1,0:T(8,128)(2,1)S(1)}, bf16[512,768]{1,0:T(8,128)(2,1)S(1)}, u32[]{:S(2)}, u32[]{:S(2)}) collective-permute-start(bf16[512,768]{1,0:T(8,128)(2,1)S(1)} %convolution_convert_fusion.4), channel_id=1, source_target_pairs={{0,1},{1,0},{2,3},{3,2},{4,5},{5,4},{6,7},{7,6},{8,9},{9,8},{10,11... | collective-permute-start | bytes 2359304 | tf_op jit(solution)/shard_map/ppermute | solution.py:39
  378.0 16.8 %collective-permute-start.76 = (bf16[192,768]{1,0:T(8,128)(2,1)S(1)}, bf16[192,768]{1,0:T(8,128)(2,1)S(1)}, u32[]{:S(2)}, u32[]{:S(2)}) collective-permute-start(bf16[192,768]{1,0:T(8,128)(2,1)S(1)} %pad_maximum_fusion.15), channel_id=1, source_target_pairs={{0,4},{4,0},{1,5},{5,1},{2,6},{6,2},{3,7},{7,3},{8,12},{12,8},{9,1... | collective-permute-start | bytes 884744 | tf_op jit(solution)/shard_map/ppermute | solution.py:39
  378.1 16.7 %collective-permute-start.77 = (bf16[256,768]{1,0:T(8,128)(2,1)S(1)}, bf16[256,768]{1,0:T(8,128)(2,1)S(1)}, u32[]{:S(2)}, u32[]{:S(2)}) collective-permute-start(bf16[256,768]{1,0:T(8,128)(2,1)S(1)} %get-tuple-element.671), channel_id=1, source_target_pairs={{0,1},{1,0},{2,3},{3,2},{4,5},{5,4},{6,7},{7,6},{8,9},{9,8},{10,11... | collective-permute-start | bytes 1179656 | tf_op jit(solution)/shard_map/ppermute | solution.py:39
  396.6 16.8 %collective-permute-start.80 = (bf16[1024,256]{1,0:T(8,128)(2,1)S(1)}, bf16[1024,256]{1,0:T(8,128)(2,1)S(1)}, u32[]{:S(2)}, u32[]{:S(2)}) collective-permute-start(bf16[1024,256]{1,0:T(8,128)(2,1)S(1)} %get-tuple-element.682), channel_id=1, source_target_pairs={{0,1},{1,0},{2,3},{3,2},{4,5},{5,4},{6,7},{7,6},{8,9},{9,8},{10,11... | collective-permute-start | bytes 1572872 | tf_op jit(solution)/shard_map/ppermute | solution.py:39
  397.8 15.7 %collective-permute-start.82 = (bf16[128,2048]{1,0:T(8,128)(2,1)S(1)}, bf16[128,2048]{1,0:T(8,128)(2,1)S(1)}, u32[]{:S(2)}, u32[]{:S(2)}) collective-permute-start(bf16[128,2048]{1,0:T(8,128)(2,1)S(1)} %get-tuple-element.684), channel_id=1, source_target_pairs={{0,16},{16,0},{1,17},{17,1},{2,18},{18,2},{3,19},{19,3},{4,20},{20... | collective-permute-start | bytes 1572872 | tf_op jit(solution)/shard_map/ppermute | solution.py:39
  417.6 24.8 %collective-permute-start.84 = (bf16[1024,256]{1,0:T(8,128)(2,1)S(1)}, bf16[1024,256]{1,0:T(8,128)(2,1)S(1)}, u32[]{:S(2)}, u32[]{:S(2)}) collective-permute-start(bf16[1024,256]{1,0:T(8,128)(2,1)S(1)} %add_convert_fusion.6), channel_id=1, source_target_pairs={{0,4},{4,0},{1,5},{5,1},{2,6},{6,2},{3,7},{7,3},{8,12},{12,8},{9,1... | collective-permute-start | bytes 1572872 | tf_op jit(solution)/shard_map/ppermute | solution.py:39
  417.7 24.7 %collective-permute-start.85 = (bf16[128,2048]{1,0:T(8,128)(2,1)}, bf16[128,2048]{1,0:T(8,128)(2,1)S(1)}, u32[]{:S(2)}, u32[]{:S(2)}) collective-permute-start(bf16[128,2048]{1,0:T(8,128)(2,1)} %get-tuple-element.697), channel_id=1, source_target_pairs={{0,16},{16,0},{1,17},{17,1},{2,18},{18,2},{3,19},{19,3},{4,20},{20... | collective-permute-start | bytes 1572872 | tf_op jit(solution)/shard_map/ppermute | solution.py:39
  418.6 23.8 %collective-permute-start.86 = (bf16[128,2048]{1,0:T(8,128)(2,1)}, bf16[128,2048]{1,0:T(8,128)(2,1)S(1)}, u32[]{:S(2)}, u32[]{:S(2)}) collective-permute-start(bf16[128,2048]{1,0:T(8,128)(2,1)} %add_convert_fusion.5), channel_id=1, source_target_pairs={{0,2},{2,0},{1,3},{3,1},{4,6},{6,4},{5,7},{7,5},{8,10},{10,8},{9,1... | collective-permute-start | bytes 1572872 | tf_op jit(solution)/shard_map/ppermute | solution.py:39
  452.3 29.8 %collective-permute-start.95 = (bf16[768,256]{1,0:T(8,128)(2,1)}, bf16[768,256]{1,0:T(8,128)(2,1)}, u32[]{:S(2)}, u32[]{:S(2)}) collective-permute-start(bf16[768,256]{1,0:T(8,128)(2,1)} %select_convert_fusion.1), channel_id=1, source_target_pairs={{0,2},{2,0},{1,3},{3,1},{4,6},{6,4},{5,7},{7,5},{8,10},{10,8},{9,1... | collective-permute-start | bytes 1179656 | tf_op jit(solution)/shard_map/ppermute | solution.py:39
  464.8 20.4 %collective-permute-start.91 = (bf16[512,2048]{1,0:T(8,128)(2,1)}, bf16[512,2048]{1,0:T(8,128)(2,1)}, u32[]{:S(2)}, u32[]{:S(2)}) collective-permute-start(bf16[512,2048]{1,0:T(8,128)(2,1)} %convolution_convert_fusion.1), channel_id=1, source_target_pairs={{0,8},{8,0},{1,9},{9,1},{2,10},{10,2},{3,11},{11,3},{4,12},{12,4},... | collective-permute-start | bytes 6291464 | tf_op jit(solution)/shard_map/ppermute | solution.py:39
  468.1 15.6 %collective-permute-start.92 = (bf16[512,256]{1,0:T(8,128)(2,1)}, bf16[512,256]{1,0:T(8,128)(2,1)}, u32[]{:S(2)}, u32[]{:S(2)}) collective-permute-start(bf16[512,256]{1,0:T(8,128)(2,1)} %add_convert_fusion.10), channel_id=1, source_target_pairs={{0,4},{4,0},{1,5},{5,1},{2,6},{6,2},{3,7},{7,3},{8,12},{12,8},{9,1... | collective-permute-start | bytes 786440 | tf_op jit(solution)/shard_map/ppermute | solution.py:39
  488.9 15.8 %collective-permute-start.96 = (bf16[128,2048]{1,0:T(8,128)(2,1)S(1)}, bf16[128,2048]{1,0:T(8,128)(2,1)S(1)}, u32[]{:S(2)}, u32[]{:S(2)}) collective-permute-start(bf16[128,2048]{1,0:T(8,128)(2,1)S(1)} %slice.544), channel_id=1, source_target_pairs={{0,16},{16,0},{1,17},{17,1},{2,18},{18,2},{3,19},{19,3},{4,20},{20... | collective-permute-start | bytes 1572872 | tf_op jit(solution)/shard_map/ppermute | solution.py:39
  504.9 19.5 %collective-permute-start.99 = (bf16[128,2048]{1,0:T(8,128)(2,1)S(1)}, bf16[128,2048]{1,0:T(8,128)(2,1)S(1)}, u32[]{:S(2)}, u32[]{:S(2)}) collective-permute-start(bf16[128,2048]{1,0:T(8,128)(2,1)S(1)} %slice.543), channel_id=1, source_target_pairs={{0,16},{16,0},{1,17},{17,1},{2,18},{18,2},{3,19},{19,3},{4,20},{20... | collective-permute-start | bytes 1572872 | tf_op jit(solution)/shard_map/ppermute | solution.py:39
  506.6 17.8 %collective-permute-start.100 = (bf16[128,2048]{1,0:T(8,128)(2,1)S(1)}, bf16[128,2048]{1,0:T(8,128)(2,1)S(1)}, u32[]{:S(2)}, u32[]{:S(2)}) collective-permute-start(bf16[128,2048]{1,0:T(8,128)(2,1)S(1)} %add_convert_fusion.3), channel_id=1, source_target_pairs={{0,2},{2,0},{1,3},{3,1},{4,6},{6,4},{5,7},{7,5},{8,10},{10,8},{9,1... | collective-permute-start | bytes 1572872 | tf_op jit(solution)/shard_map/ppermute | solution.py:39
  506.9 17.5 %collective-permute-start.101 = (bf16[512,512]{1,0:T(8,128)(2,1)S(1)}, bf16[512,512]{1,0:T(8,128)(2,1)S(1)}, u32[]{:S(2)}, u32[]{:S(2)}) collective-permute-start(bf16[512,512]{1,0:T(8,128)(2,1)S(1)} %convolution_convert_fusion.9), channel_id=1, source_target_pairs={{0,1},{1,0},{2,3},{3,2},{4,5},{5,4},{6,7},{7,6},{8,9},{9,8},{10,11... | collective-permute-start | bytes 1572872 | tf_op jit(solution)/shard_map/ppermute | solution.py:39
  508.3 16.1 %collective-permute-start.104 = (bf16[256,512]{1,0:T(8,128)(2,1)S(1)}, bf16[256,512]{1,0:T(8,128)(2,1)S(1)}, u32[]{:S(2)}, u32[]{:S(2)}) collective-permute-start(bf16[256,512]{1,0:T(8,128)(2,1)S(1)} %fusion.6), channel_id=1, source_target_pairs={{0,4},{4,0},{1,5},{5,1},{2,6},{6,2},{3,7},{7,3},{8,12},{12,8},{9,1... | collective-permute-start | bytes 786440 | tf_op jit(solution)/shard_map/ppermute | solution.py:39
  (160 other events, 1565.4 us)
